TPU v7x, 256 devices: a whole 4x4x8 slice. The times are simulated.
256 devices in a mesh: particle: 16 (over y, z_hi), coeffici: 8 (over x, core), half: 2 (over z_lo).
Axes of the slice: x: 4, y: 4, z: 8 (z_hi: 4, z_lo: 2; z = z_hi * 2 + z_lo), core: 2. Of those that a mesh axis runs over, the one named last changes fastest.
Arguments:
- residuals: float32 [2, 16384, 16384], P('half', 'particle', 'coeffici'), may hold values from -6 to 6
- loadings: float32 [2, 16384, 256], P('half', 'coeffici'), may hold values from -0.046875 to 0.046875
Outputs:
- new_loadings: float32 [2, 16384, 256], P('half', ('coeffici', 'particle'))
- rayleigh: float32 [2, 256, 256], P('half')
All inputs are finite; a program needn't handle non-finite values.
Results may differ from a plain program's by a relative error of at most 0.00024.
Values sent between devices are 32-bit elements; how exact they have to be, the bound alone decides.
No kernel may reach another device: no remote copies, remote signals or barrier semaphores. Data moves between devices by JAX's collectives and lax.ppermute only.
A program may use at most 64 MiB of HBM per device.

v0:
```python
import functools

import jax
import jax.numpy as jnp
from jax import lax
from jax.experimental import pallas as pl
from jax.experimental.pallas import tpu as pltpu
from jax.sharding import PartitionSpec as P


F32 = jnp.float32
BF16 = jnp.bfloat16
VMEM = pl.BlockSpec(memory_space=pltpu.VMEM)
HBM = pl.BlockSpec(memory_space=pltpu.HBM)
LANE = 128

RING = (0, 1, 3, 2)
CORE, X, Y, Z = 1, 2, 4, 1
PLACES = ((0, 3, 1, 2), (0, 1, 3, 2))


def swap(value, axis, mask):
    return lax.ppermute(value, axis, [(s, s ^ mask) for s in range(lax.axis_size(axis))])


def split(value):
    high = value.astype(BF16)
    return high, (value - high.astype(F32)).astype(BF16)


def dot(left, right):
    return lax.dot_general(left, right, (((1,), (0,)), ((), ())), preferred_element_type=F32)


def dot3(lh, ll, rh, rl):
    return dot(lh, rh) + dot(ll, rh) + dot(lh, rl)


def at(index, size):
    return pl.ds(pl.multiple_of(index * size, size), size)


def params(mib):
    return pltpu.CompilerParams(vmem_limit_bytes=mib << 20)


def shape(*dims, dtype=F32):
    return jax.ShapeDtypeStruct(dims, dtype)


def cost(flops, mib):
    return pl.CostEstimate(flops=flops, bytes_accessed=mib << 20, transcendentals=0)


def scores_kernel(side, *refs):
    if side:
        res, load, out, rh, rl, lh, ll, later, rbuf, lbuf, acc, rsems, lsems, nsems = refs
    else:
        rbuf, lh, ll, out, rh, rl, acc = refs
    me = lax.axis_index("coeffici")
    core = me & 1
    size = out.shape[1]
    depth = lh.shape[0] // 4
    copies, others = [[] for _ in range(4)], []
    if side:
        for step in range(4):
            cols = slice(step * depth, (step + 1) * depth)
            copies[step].append(pltpu.make_async_copy(load.at[cols], lbuf.at[cols], lsems.at[step]))
            for t in range(4):
                copies[step].append(
                    pltpu.make_async_copy(
                        res.at[at(2 * t + (core ^ 1), size), cols], rbuf.at[pl.ds(t * size, size), cols], rsems.at[step, t]
                    )
                )
        for t in range(4):
            others.append(
                pltpu.make_async_copy(res.at[at(2 * t + core, size)], later.at[pl.ds(t * size, size)], nsems.at[t])
            )
        for copy in sum(copies, []) + others:
            copy.start()
    for step in range(4):
        for copy in copies[step]:
            copy.wait()
        cols = slice(step * depth, (step + 1) * depth)
        if side:
            lh[cols], ll[cols] = split(lbuf[cols])
        high, low = split(rbuf[:, cols])
        rh[:, cols], rl[:, cols] = high, low
        term = dot3(high, low, lh[cols], ll[cols])
        if step == 0:
            acc[...] = term
        else:
            acc[...] += term
    for t in range(4):
        mask = (me ^ (2 * t + (core ^ side))) >> 1
        out[mask ^ (mask >> 1)] = acc[t * size : (t + 1) * size]
    for copy in others:
        copy.wait()


def scores(side, res, *load):
    rows, coefs = res.shape
    rows = rows if side else 2 * rows
    k = load[0].shape[1]
    operand = shape(rows // 2, coefs, dtype=BF16)
    extra = (shape(coefs, k, dtype=BF16),) * 2 + (shape(rows // 2, coefs),)
    acc = pltpu.VMEM((rows // 2, k), F32)
    dma = pltpu.SemaphoreType.DMA
    return pl.pallas_call(
        functools.partial(scores_kernel, side),
        out_shape=(shape(4, rows // 8, k), operand, operand) + (extra if side else ()),
        in_specs=[HBM, HBM] if side else [VMEM] * 3,
        out_specs=(VMEM,) * (6 if side else 3),
        scratch_shapes=[pltpu.VMEM((rows // 2, coefs), F32), pltpu.VMEM((coefs, k), F32), acc, dma((4, 4)), dma((4,)), dma((4,))]
        if side
        else [acc],
        compiler_params=params(20),
        cost_estimate=cost(3 * rows * coefs * k, 6),
        name="scores_far" if side else "scores_near",
    )(res, *load)


def own_kernel(near, got, r1, r2, r3, out):
    out[...] = ((near[0] + got[0]) + (r1[...] + r2[...]) + r3[...]).T


def own_block(*terms):
    _, rows, k = terms[0].shape
    return pl.pallas_call(
        own_kernel,
        out_shape=shape(k, rows),
        in_specs=[VMEM] * 5,
        out_specs=VMEM,
        compiler_params=params(4),
        cost_estimate=cost(1 << 18, 1),
        name="own_block",
    )(*terms)


def stage_kernel(*refs):
    pieces, out = refs[:-1], refs[-1]
    me = lax.axis_index("coeffici")
    for n in range(4):
        piece = pieces[n][...] if len(pieces) == 4 else pieces[0][n]
        high, low = split(piece)
        where = at((me ^ (X * RING[n])) >> 1, LANE)
        for block in range(4):
            rows = slice(64 * block, 64 * block + 64)
            out[128 * block : 128 * block + 64, where] = high[rows]
            out[128 * block + 64 : 128 * block + 128, where] = low[rows]


def stage(*pieces):
    return pl.pallas_call(
        stage_kernel,
        out_shape=shape(4 * LANE, 4 * LANE, dtype=BF16),
        in_specs=[VMEM] * len(pieces),
        out_specs=VMEM,
        compiler_params=params(4),
        cost_estimate=cost(1 << 18, 1),
        name="stage",
    )(*pieces)


def columns(refs, ys, zs):
    return [jnp.concatenate([r[:, at(4 * y + z, LANE)] for z in zs for y in ys], axis=1) for r in refs]


def pair_kernel(places, sides, add, *refs):
    ops, before, (out_p, out_q) = refs[: 3 * sides], refs[3 * sides : 3 * sides + 2 * add], refs[-2:]
    particle = lax.axis_index("particle")
    y, z = particle >> 2, particle & 3
    starts = [(y ^ PLACES[part][place]) * LANE + 32 * part for part in range(2) for place in places]
    starts += [s + 64 for s in starts]
    wide = out_p.shape[2]

    @pl.loop(0, 2)
    def _(step):
        spots = [2 * step, 2 * step + 1]
        total = None
        for side in range(sides):
            st, rh, rl = ops[3 * side : 3 * side + 3]
            high, rest = columns((rh, rl), range(3), [z ^ s ^ (s >> 1) for s in spots])
            left = jnp.concatenate([st[pl.ds(pl.multiple_of(s, 32), 32)] for s in starts])
            both, low = dot(left, high), dot(left[:LANE], rest)
            term = both[:LANE] + both[LANE:] + low
            total = term if total is None else total + term
        for part, out in enumerate((out_p, out_q)):
            for n in range(2):
                for i, spot in enumerate(spots):
                    top = 64 * part + 32 * n
                    value = total[top : top + 32, wide * i : wide * (i + 1)]
                    if add:
                        value = value + before[part][4 * n + spot]
                    out[4 * n + spot] = value


def covariance_pair(places, operands, before):
    rows, coefs = operands[1].shape
    sides = len(operands) // 3
    out = shape(8, 32, 3 * LANE)
    return pl.pallas_call(
        functools.partial(pair_kernel, places, sides, len(before) // 2),
        out_shape=(out, out),
        in_specs=[VMEM] * (len(operands) + len(before)),
        out_specs=(VMEM, VMEM),
        compiler_params=params(16),
        cost_estimate=cost(3 * rows * coefs * LANE * sides, 4),
    )(*operands, *before)


def third_kernel(*refs):
    ops, out = refs[:6], refs[6]
    particle = lax.axis_index("particle")
    y, z = particle >> 2, particle & 3

    @pl.loop(0, 2)
    def _(step):
        spots = [2 * step, 2 * step + 1]
        both = low = None
        for st, rh, rl in (ops[:3], ops[3:]):
            high, rest = columns((rh, rl), [3], [z ^ s ^ (s >> 1) for s in spots])
            left_high = jnp.concatenate([st[LANE * b : LANE * b + 64] for b in range(4)])
            first, second = dot(st[...], high), dot(left_high, rest)
            both = first if both is None else both + first
            low = second if low is None else low + second
        for b in range(4):
            mask = y ^ b
            place = mask ^ (mask >> 1)
            top = LANE * b
            value = both[top : top + 64] + both[top + 64 : top + LANE] + low[64 * b : 64 * b + 64]
            for i, spot in enumerate(spots):
                out[4 * spot + place] = value[:, LANE * i : LANE * (i + 1)]


def covariance_third(operands):
    rows, coefs = operands[1].shape
    return pl.pallas_call(
        third_kernel,
        out_shape=shape(16, 64, LANE),
        in_specs=[VMEM] * 6,
        out_specs=VMEM,
        compiler_params=params(16),
        cost_estimate=cost(3 * rows * coefs * LANE, 4),
        name="covariance_third",
    )(*operands)


def shrink_kernel(factor, load_h, load_l, mine, other, w_out, corr_out, cbuf):
    particle = lax.axis_index("particle")
    y, z = particle >> 2, particle & 3
    core = lax.axis_index("coeffici") & 1
    corr = None
    for n in range(4):
        cols = slice(n * LANE, n * LANE + LANE)
        cov = mine[:, cols] * factor
        far = other[:, cols] * factor
        weighted = cov * jax.nn.sigmoid(cov * far)
        mask = y ^ n
        w_out[mask ^ (mask >> 1)] = weighted
        wh, wl = split(weighted)
        where = at(4 * n + z, LANE)
        term = dot3(wh, wl, load_h[where], load_l[where])
        corr = term if corr is None else corr + term
    cbuf[...] = corr * factor
    for n in range(2):
        rows = cbuf[at(core ^ n, 32)]
        corr_out[n, :32] = rows[:, :LANE]
        corr_out[n, 32:] = rows[:, LANE:]


def shrink(factor, *args):
    return pl.pallas_call(
        functools.partial(shrink_kernel, factor),
        out_shape=(shape(4, 64, LANE), shape(2, 64, LANE)),
        in_specs=[VMEM] * 4,
        out_specs=(VMEM, VMEM),
        scratch_shapes=[pltpu.VMEM((64, 2 * LANE), F32)],
        compiler_params=params(8),
        cost_estimate=cost(6 * 64 * 512 * 256, 1),
        name="shrink",
    )(*args)


def assemble_kernel(w, corr, r1, r2, r3, far0, far, w_out, corr_out, wbuf, cbuf):
    y = lax.axis_index("particle") >> 2
    core = lax.axis_index("coeffici") & 1
    got = (None, r1, r2, r3)
    for n in range(4):
        block = y ^ RING[n]
        wbuf[at(block, 64)] = w[0] if n == 0 else got[n][1]
        for c in range(2):
            if n == 0:
                piece = (corr if c == 0 else far0)[...]
            else:
                piece = got[n][0] if c == 0 else far[n - 1]
            where = at(2 * block + (core ^ c), 32)
            cbuf[where, :LANE] = piece[:32]
            cbuf[where, LANE:] = piece[32:]
    w_out[...] = wbuf[...].T
    corr_out[...] = cbuf[...].T


def assemble(*args):
    k = 2 * LANE
    return pl.pallas_call(
        assemble_kernel,
        out_shape=(shape(LANE, k), shape(k, k)),
        in_specs=[VMEM] * len(args),
        out_specs=(VMEM, VMEM),
        scratch_shapes=[pltpu.VMEM((k, LANE), F32), pltpu.VMEM((k, k), F32)],
        compiler_params=params(4),
        name="assemble",
    )(*args)


def ring_swap(values, axis, unit):
    return [swap(v, axis, unit * m) for v, m in zip(values, RING[1:])]


def ring_sum(value, axis, unit):
    a, b, c = ring_swap([value] * 3, axis, unit)
    return (value + a) + (b + c)


def step(residuals, loadings):
    res, load = (pltpu.with_memory_space_constraint(v[0], pltpu.HBM) for v in (residuals, loadings))
    factor = (res.shape[0] * lax.axis_size("particle")) ** -0.5

    far, fh, fl, lh, ll, rest = scores(1, res, load)
    got = swap(far, "coeffici", CORE)
    near, nh, nl = scores(0, rest, lh, ll)
    own = own_block(near, got, *ring_swap([near[n] + got[n] for n in (1, 2, 3)], "coeffici", X))
    pieces = [own] + ring_swap([own] * 3, "coeffici", X)
    others = swap(jnp.stack(pieces), "coeffici", CORE)
    near_ops = (stage(*pieces), nh, nl)
    far_ops = (stage(others), fh, fl)

    leave = covariance_pair((2, 3), near_ops, ())
    leave_p, leave_q = covariance_pair((2, 3), far_ops, leave)
    one_p = swap(leave_p, "particle", Y)
    one_q = swap(leave_q, "particle", 3 * Y)
    third = covariance_third(near_ops + far_ops)
    sums = ring_swap([third[4 * n : 4 * n + 4] for n in (1, 2, 3)], "particle", Z)
    keep_p, keep_q = covariance_pair((0, 1), near_ops + far_ops, ())
    two_p = swap(keep_p[4:] + one_p[4:], "particle", 3 * Y)
    two_q = swap(keep_q[4:] + one_q[4:], "particle", Y)

    def at_z(n):
        return jnp.concatenate([keep_p[n] + one_p[n] + two_p[n], keep_q[n] + one_q[n] + two_q[n]])

    def at_y(n):
        return third[n] + (sums[0][n] + sums[1][n]) + sums[2][n]

    r1, r2, r3 = ring_swap([at_z(n) for n in (1, 2, 3)], "particle", Z)
    t1, t2, t3 = ring_swap([at_y(n) for n in (1, 2, 3)], "particle", Y)
    mine = jnp.concatenate([at_z(0) + (r1 + r2) + r3, at_y(0) + (t1 + t2) + t3], axis=1)
    other = swap(mine, "half", 1)
    w, corr = shrink(factor, lh, ll, mine, other)

    corr = corr[0] + swap(corr[1], "coeffici", CORE)
    corr = ring_sum(corr, "coeffici", X)
    corr = ring_sum(corr, "particle", Z)
    far0 = swap(corr, "coeffici", CORE)
    got = ring_swap([jnp.stack([corr, w[n]]) for n in (1, 2, 3)], "particle", Y)
    far = swap(jnp.stack([g[0] for g in got]), "coeffici", CORE)
    weighted, rayleigh = assemble(w, corr, *got, far0, far)
    return weighted[None], rayleigh[None]


def solution(mesh):
    in_specs = (P("half", "particle", "coeffici"), P("half", "coeffici", None))
    out_specs = (P("half", ("coeffici", "particle"), None), P("half", None, None))
    return jax.shard_map(step, mesh=mesh, in_specs=in_specs, out_specs=out_specs, check_vma=False)
```

profile of v0, /device:TPU:1, one launch (start us, length us, event | category | flops | bytes accessed | tf_op | source)
XLA Modules:
  0.0 118.7 jit_solution(3470896574290719790)
XLA Ops:
  0.6 6.0 %scores_far.1 = (f32[4,128,256]{2,1,0:T(8,128)S(1)}, bf16[512,2048]{1,0:T(8,128)(2,1)S(1)}, bf16[512,2048]{1,0:T(8,128)(2,1)S(1)}, bf16[2048,256]{1,0:T(8,128)(2...) custom-call(f32[1024,2048]{1,0:T(8,128)} %bitcast.52, f32[2048,256]{1,0:T(8,128)} %bitcast.53), custom_call_target="tpu_custom_call" | custom-call | flops 1610612736 | bytes 6291456 | tf_op jit(solution)/shard_map/scores_far/pallas_call | solution.py:109
  6.6 3.3 %collective-permute-start = (f32[4,128,256]{2,1,0:T(8,128)S(1)}, f32[4,128,256]{2,1,0:T(8,128)S(1)}, u32[]{:S(2)}, u32[]{:S(2)}) collective-permute-start(f32[4,128,256]{2,1,0:T(8,128)S(1)} %get-tuple-element.25), channel_id=1, source_target_pairs={{0,2},{2,0},{4,6},{6,4},{8,10},{10,8},{12,14},{14,12},{1,3},{3,1},... | collective-permute-start | bytes 1572872 | tf_op jit(solution)/shard_map/ppermute | solution.py:23
  9.9 2.0 %scores_near.1 = (f32[4,128,256]{2,1,0:T(8,128)S(1)}, bf16[512,2048]{1,0:T(8,128)(2,1)S(1)}, bf16[512,2048]{1,0:T(8,128)(2,1)S(1)}) custom-call(f32[512,2048]{1,0:T(8,128)S(1)} %get-tuple-element.23.refs_0_, bf16[2048,256]{1,0:T(8,128)(2,1)S(1)} %get-tuple-element.21.refs_1_.load_h, bf16[2048,256]{1,0:T(8,128)(2,1)S(1)} %get-tuple-element.22.refs_2_.load_l), custom_call_target="tpu_custom_call" | custom-call | flops 1610612736 | bytes 6291456 | tf_op jit(solution)/shard_map/scores_near/pallas_call | solution.py:109
  14.7 3.9 %collective-permute-done.3.r3 = f32[128,256]{1,0:T(8,128)S(1)} collective-permute-done((f32[128,256]{1,0:T(8,128)S(1)}, f32[128,256]{1,0:T(8,128)S(1)}, u32[]{:S(2)}, u32[]{:S(2)}) %collective-permute-start.3) | collective-permute-done | bytes 131104 | tf_op jit(solution)/shard_map/ppermute | solution.py:23
  18.6 3.2 %collective-permute-done.2.r2 = f32[128,256]{1,0:T(8,128)S(1)} collective-permute-done((f32[128,256]{1,0:T(8,128)S(1)}, f32[128,256]{1,0:T(8,128)S(1)}, u32[]{:S(2)}, u32[]{:S(2)}) %collective-permute-start.2) | collective-permute-done | bytes 131104 | tf_op jit(solution)/shard_map/ppermute | solution.py:23
  24.7 3.4 %collective-permute-done.6.refs_3_ = f32[256,128]{1,0:T(8,128)S(1)} collective-permute-done((f32[256,128]{1,0:T(8,128)S(1)}, f32[256,128]{1,0:T(8,128)S(1)}, u32[]{:S(2)}, u32[]{:S(2)}) %collective-permute-start.6) | collective-permute-done | bytes 131104 | tf_op jit(solution)/shard_map/ppermute | solution.py:23
  28.1 3.6 %collective-permute-done.5.refs_2_ = f32[256,128]{1,0:T(8,128)S(1)} collective-permute-done((f32[256,128]{1,0:T(8,128)S(1)}, f32[256,128]{1,0:T(8,128)S(1)}, u32[]{:S(2)}, u32[]{:S(2)}) %collective-permute-start.5) | collective-permute-done | bytes 131104 | tf_op jit(solution)/shard_map/ppermute | solution.py:23
  36.8 2.7 %collective-permute-start.15 = (f32[4,64,128]{2,1,0:T(8,128)S(1)}, f32[4,64,128]{2,1,0:T(8,128)S(1)}, u32[]{:S(2)}, u32[]{:S(2)}) collective-permute-start(f32[4,64,128]{2,1,0:T(8,128)S(1)} %get-tuple-element.54), channel_id=1, source_target_pairs={{0,16},{16,0},{32,48},{48,32},{64,80},{80,64},{96,112},{112,96},{1... | collective-permute-start | bytes 393224 | tf_op jit(solution)/shard_map/ppermute | solution.py:23
  39.5 5.1 %collective-permute-start.17 = (f32[4,64,128]{2,1,0:T(8,128)S(1)}, f32[4,64,128]{2,1,0:T(8,128)S(1)}, u32[]{:S(2)}, u32[]{:S(2)}) collective-permute-start(f32[4,64,128]{2,1,0:T(8,128)S(1)} %get-tuple-element.55), channel_id=1, source_target_pairs={{0,32},{16,48},{32,0},{48,16},{64,96},{80,112},{96,64},{112,80},{1... | collective-permute-start | bytes 393224 | tf_op jit(solution)/shard_map/ppermute | solution.py:23
  46.5 2.2 %shard_map.41 = (f32[8,32,384]{2,1,0:T(8,128)S(1)}, f32[8,32,384]{2,1,0:T(8,128)S(1)}) custom-call(bf16[512,512]{1,0:T(8,128)(2,1)S(1)} %stage.2.refs_0_, bf16[512,2048]{1,0:T(8,128)(2,1)S(1)} %get-tuple-element.26.refs_1_, bf16[512,2048]{1,0:T(8,128)(2,1)S(1)} %get-tuple-element.27.refs_2_, bf16[512,512]{1,0:T(8,128)(2,1)S(1)} %stage.3.refs_3_.refs_0_, ...), custom_call_target="tpu_custom_call" | custom-call | flops 805306368 | bytes 4194304 | tf_op jit(solution)/shard_map/pallas_call | solution.py:202
  48.8 4.4 %collective-permute-done.17 = f32[4,64,128]{2,1,0:T(8,128)S(1)} collective-permute-done((f32[4,64,128]{2,1,0:T(8,128)S(1)}, f32[4,64,128]{2,1,0:T(8,128)S(1)}, u32[]{:S(2)}, u32[]{:S(2)}) %collective-permute-start.17) | collective-permute-done | bytes 131104 | tf_op jit(solution)/shard_map/ppermute | solution.py:23
  53.2 2.6 %collective-permute-done.16 = f32[4,64,128]{2,1,0:T(8,128)S(1)} collective-permute-done((f32[4,64,128]{2,1,0:T(8,128)S(1)}, f32[4,64,128]{2,1,0:T(8,128)S(1)}, u32[]{:S(2)}, u32[]{:S(2)}) %collective-permute-start.16) | collective-permute-done | bytes 131104 | tf_op jit(solution)/shard_map/ppermute | solution.py:23
  55.9 2.0 %collective-permute-start.19 = (f32[64,128]{1,0:T(8,128)S(1)}, f32[64,128]{1,0:T(8,128)S(1)}, u32[]{:S(2)}, u32[]{:S(2)}) collective-permute-start(f32[64,128]{1,0:T(8,128)S(1)} %get-tuple-element.51), channel_id=1, source_target_pairs={{0,192},{16,208},{32,224},{48,240},{64,128},{80,144},{96,160},{112... | collective-permute-start | bytes 98312 | tf_op jit(solution)/shard_map/ppermute | solution.py:23
  59.2 2.0 %collective-permute-start.9 = (f32[4,32,384]{2,1,0:T(8,128)S(1)}, f32[4,32,384]{2,1,0:T(8,128)S(1)}, u32[]{:S(2)}, u32[]{:S(2)}) collective-permute-start(f32[4,32,384]{2,1,0:T(8,128)S(1)} %slice_add_fusion.1), channel_id=1, source_target_pairs={{0,192},{16,208},{32,224},{48,240},{64,128},{80,144},{96,160},{112... | collective-permute-start | bytes 589832 | tf_op jit(solution)/shard_map/ppermute | solution.py:23
  61.7 4.0 %collective-permute-done.9 = f32[4,32,384]{2,1,0:T(8,128)S(1)} collective-permute-done((f32[4,32,384]{2,1,0:T(8,128)S(1)}, f32[4,32,384]{2,1,0:T(8,128)S(1)}, u32[]{:S(2)}, u32[]{:S(2)}) %collective-permute-start.9) | collective-permute-done | bytes 196640 | tf_op jit(solution)/shard_map/ppermute | solution.py:23
  66.2 2.8 %collective-permute-start.12 = (f32[64,384]{1,0:T(8,128)S(1)}, f32[64,384]{1,0:T(8,128)S(1)}, u32[]{:S(2)}, u32[]{:S(2)}) collective-permute-start(f32[64,384]{1,0:T(8,128)S(1)} %pad_maximum_fusion.2), channel_id=1, source_target_pairs={{0,16},{16,0},{32,48},{48,32},{64,80},{80,64},{96,112},{112,96},{1... | collective-permute-start | bytes 294920 | tf_op jit(solution)/shard_map/ppermute | solution.py:23
  69.0 3.8 %collective-permute-start.14 = (f32[64,384]{1,0:T(8,128)S(1)}, f32[64,384]{1,0:T(8,128)S(1)}, u32[]{:S(2)}, u32[]{:S(2)}) collective-permute-start(f32[64,384]{1,0:T(8,128)S(1)} %pad_maximum_fusion.4), channel_id=1, source_target_pairs={{0,32},{16,48},{32,0},{48,16},{64,96},{80,112},{96,64},{112,80},{1... | collective-permute-start | bytes 294920 | tf_op jit(solution)/shard_map/ppermute | solution.py:23
  72.9 3.7 %collective-permute-done.14 = f32[64,384]{1,0:T(8,128)S(1)} collective-permute-done((f32[64,384]{1,0:T(8,128)S(1)}, f32[64,384]{1,0:T(8,128)S(1)}, u32[]{:S(2)}, u32[]{:S(2)}) %collective-permute-start.14) | collective-permute-done | bytes 98336 | tf_op jit(solution)/shard_map/ppermute | solution.py:23
  76.6 4.9 %collective-permute-done.13 = f32[64,384]{1,0:T(8,128)S(1)} collective-permute-done((f32[64,384]{1,0:T(8,128)S(1)}, f32[64,384]{1,0:T(8,128)S(1)}, u32[]{:S(2)}, u32[]{:S(2)}) %collective-permute-start.13) | collective-permute-done | bytes 98336 | tf_op jit(solution)/shard_map/ppermute | solution.py:23
  82.7 2.7 %collective-permute-done.21.other = f32[64,512]{1,0:T(8,128)S(1)} collective-permute-done((f32[64,512]{1,0:T(8,128)S(1)}, f32[64,512]{1,0:T(8,128)S(1)}, u32[]{:S(2)}, u32[]{:S(2)}) %collective-permute-start.21) | collective-permute-done | bytes 131104 | tf_op jit(solution)/shard_map/ppermute | solution.py:23
  85.7 2.8 %collective-permute-start.22 = (f32[64,128]{1,0:T(8,128)S(1)}, f32[64,128]{1,0:T(8,128)S(1)}, u32[]{:S(2)}, u32[]{:S(2)}) collective-permute-start(f32[64,128]{1,0:T(8,128)S(1)} %slice_bitcast_fusion), channel_id=1, source_target_pairs={{0,2},{2,0},{4,6},{6,4},{8,10},{10,8},{12,14},{14,12},{1,3},{3,1},... | collective-permute-start | bytes 98312 | tf_op jit(solution)/shard_map/ppermute | solution.py:23
  96.0 3.6 %collective-permute-start.28 = (f32[64,128]{1,0:T(8,128)S(1)}, f32[64,128]{1,0:T(8,128)S(1)}, u32[]{:S(2)}, u32[]{:S(2)}) collective-permute-start(f32[64,128]{1,0:T(8,128)S(1)} %add_add_fusion.1), channel_id=1, source_target_pairs={{0,32},{16,48},{32,0},{48,16},{64,96},{80,112},{96,64},{112,80},{1... | collective-permute-start | bytes 98312 | tf_op jit(solution)/shard_map/ppermute | solution.py:23
  102.8 2.0 %collective-permute-done.27 = f32[64,128]{1,0:T(8,128)S(1)} collective-permute-done((f32[64,128]{1,0:T(8,128)S(1)}, f32[64,128]{1,0:T(8,128)S(1)}, u32[]{:S(2)}, u32[]{:S(2)}) %collective-permute-start.27) | collective-permute-done | bytes 32800 | tf_op jit(solution)/shard_map/ppermute | solution.py:23
  112.0 4.6 %collective-permute-start.33 = (f32[3,64,128]{2,1,0:T(8,128)S(1)}, f32[3,64,128]{2,1,0:T(8,128)S(1)}, u32[]{:S(2)}, u32[]{:S(2)}) collective-permute-start(f32[3,64,128]{2,1,0:T(8,128)S(1)} %pad_maximum_fusion.5), channel_id=1, source_target_pairs={{0,2},{2,0},{4,6},{6,4},{8,10},{10,8},{12,14},{14,12},{1,3},{3,1},... | collective-permute-start | bytes 294920 | tf_op jit(solution)/shard_map/ppermute | solution.py:23
  (79 shorter events, 36.4 us)
Async XLA Ops:
  6.6 5.3 %collective-permute-start = (f32[4,128,256]{2,1,0:T(8,128)S(1)}, f32[4,128,256]{2,1,0:T(8,128)S(1)}, u32[]{:S(2)}, u32[]{:S(2)}) collective-permute-start(f32[4,128,256]{2,1,0:T(8,128)S(1)} %get-tuple-element.25), channel_id=1, source_target_pairs={{0,2},{2,0},{4,6},{6,4},{8,10},{10,8},{12,14},{14,12},{1,3},{3,1},... | collective-permute-start | bytes 1572872 | tf_op jit(solution)/shard_map/ppermute | solution.py:23
  12.0 6.6 %collective-permute-start.3 = (f32[128,256]{1,0:T(8,128)S(1)}, f32[128,256]{1,0:T(8,128)S(1)}, u32[]{:S(2)}, u32[]{:S(2)}) collective-permute-start(f32[128,256]{1,0:T(8,128)S(1)} %get-tuple-element.40), channel_id=1, source_target_pairs={{0,8},{2,10},{4,12},{6,14},{8,0},{10,2},{12,4},{14,6},{1,9},{3,11}... | collective-permute-start | bytes 393224 | tf_op jit(solution)/shard_map/ppermute | solution.py:23
  13.1 8.7 %collective-permute-start.2 = (f32[128,256]{1,0:T(8,128)S(1)}, f32[128,256]{1,0:T(8,128)S(1)}, u32[]{:S(2)}, u32[]{:S(2)}) collective-permute-start(f32[128,256]{1,0:T(8,128)S(1)} %get-tuple-element.41), channel_id=1, source_target_pairs={{0,12},{2,14},{4,8},{6,10},{8,4},{10,6},{12,0},{14,2},{1,13},{3,15... | collective-permute-start | bytes 393224 | tf_op jit(solution)/shard_map/ppermute | solution.py:23
  14.0 7.9 %collective-permute-start.1 = (f32[128,256]{1,0:T(8,128)S(1)}, f32[128,256]{1,0:T(8,128)S(1)}, u32[]{:S(2)}, u32[]{:S(2)}) collective-permute-start(f32[128,256]{1,0:T(8,128)S(1)} %get-tuple-element.42), channel_id=1, source_target_pairs={{0,4},{2,6},{4,0},{6,2},{8,12},{10,14},{12,8},{14,10},{1,5},{3,7},... | collective-permute-start | bytes 393224 | tf_op jit(solution)/shard_map/ppermute | solution.py:23
  22.0 6.2 %collective-permute-start.6 = (f32[256,128]{1,0:T(8,128)S(1)}, f32[256,128]{1,0:T(8,128)S(1)}, u32[]{:S(2)}, u32[]{:S(2)}) collective-permute-start(f32[256,128]{1,0:T(8,128)S(1)} %own_block.1.refs_0_), channel_id=1, source_target_pairs={{0,8},{2,10},{4,12},{6,14},{8,0},{10,2},{12,4},{14,6},{1,9},{3,11}... | collective-permute-start | bytes 393224 | tf_op jit(solution)/shard_map/ppermute | solution.py:23
  23.1 8.7 %collective-permute-start.5 = (f32[256,128]{1,0:T(8,128)S(1)}, f32[256,128]{1,0:T(8,128)S(1)}, u32[]{:S(2)}, u32[]{:S(2)}) collective-permute-start(f32[256,128]{1,0:T(8,128)S(1)} %own_block.1.refs_0_), channel_id=1, source_target_pairs={{0,12},{2,14},{4,8},{6,10},{8,4},{10,6},{12,0},{14,2},{1,13},{3,15... | collective-permute-start | bytes 393224 | tf_op jit(solution)/shard_map/ppermute | solution.py:23
  23.9 7.8 %collective-permute-start.4 = (f32[256,128]{1,0:T(8,128)S(1)}, f32[256,128]{1,0:T(8,128)S(1)}, u32[]{:S(2)}, u32[]{:S(2)}) collective-permute-start(f32[256,128]{1,0:T(8,128)S(1)} %own_block.1.refs_0_), channel_id=1, source_target_pairs={{0,4},{2,6},{4,0},{6,2},{8,12},{10,14},{12,8},{14,10},{1,5},{3,7},... | collective-permute-start | bytes 393224 | tf_op jit(solution)/shard_map/ppermute | solution.py:23
  36.7 22.5 %collective-permute-start.8 = (f32[8,32,384]{2,1,0:T(8,128)S(1)}, f32[8,32,384]{2,1,0:T(8,128)S(1)}, u32[]{:S(2)}, u32[]{:S(2)}) collective-permute-start(f32[8,32,384]{2,1,0:T(8,128)S(1)} %get-tuple-element.33), channel_id=1, source_target_pairs={{0,64},{16,80},{32,96},{48,112},{64,0},{80,16},{96,32},{112,48},{1... | collective-permute-start | bytes 1179656 | tf_op jit(solution)/shard_map/ppermute | solution.py:23
  36.8 12.0 %collective-permute-start.15 = (f32[4,64,128]{2,1,0:T(8,128)S(1)}, f32[4,64,128]{2,1,0:T(8,128)S(1)}, u32[]{:S(2)}, u32[]{:S(2)}) collective-permute-start(f32[4,64,128]{2,1,0:T(8,128)S(1)} %get-tuple-element.54), channel_id=1, source_target_pairs={{0,16},{16,0},{32,48},{48,32},{64,80},{80,64},{96,112},{112,96},{1... | collective-permute-start | bytes 393224 | tf_op jit(solution)/shard_map/ppermute | solution.py:23
  39.5 13.7 %collective-permute-start.17 = (f32[4,64,128]{2,1,0:T(8,128)S(1)}, f32[4,64,128]{2,1,0:T(8,128)S(1)}, u32[]{:S(2)}, u32[]{:S(2)}) collective-permute-start(f32[4,64,128]{2,1,0:T(8,128)S(1)} %get-tuple-element.55), channel_id=1, source_target_pairs={{0,32},{16,48},{32,0},{48,16},{64,96},{80,112},{96,64},{112,80},{1... | collective-permute-start | bytes 393224 | tf_op jit(solution)/shard_map/ppermute | solution.py:23
  44.6 11.2 %collective-permute-start.16 = (f32[4,64,128]{2,1,0:T(8,128)S(1)}, f32[4,64,128]{2,1,0:T(8,128)S(1)}, u32[]{:S(2)}, u32[]{:S(2)}) collective-permute-start(f32[4,64,128]{2,1,0:T(8,128)S(1)} %get-tuple-element.56), channel_id=1, source_target_pairs={{0,48},{16,32},{32,16},{48,0},{64,112},{80,96},{96,80},{112,64},{1... | collective-permute-start | bytes 393224 | tf_op jit(solution)/shard_map/ppermute | solution.py:23
  44.6 16.6 %collective-permute-start.10 = (f32[8,32,384]{2,1,0:T(8,128)S(1)}, f32[8,32,384]{2,1,0:T(8,128)S(1)}, u32[]{:S(2)}, u32[]{:S(2)}) collective-permute-start(f32[8,32,384]{2,1,0:T(8,128)S(1)} %get-tuple-element.35), channel_id=1, source_target_pairs={{0,192},{16,208},{32,224},{48,240},{64,128},{80,144},{96,160},{112... | collective-permute-start | bytes 1179656 | tf_op jit(solution)/shard_map/ppermute | solution.py:23
  55.9 16.9 %collective-permute-start.19 = (f32[64,128]{1,0:T(8,128)S(1)}, f32[64,128]{1,0:T(8,128)S(1)}, u32[]{:S(2)}, u32[]{:S(2)}) collective-permute-start(f32[64,128]{1,0:T(8,128)S(1)} %get-tuple-element.51), channel_id=1, source_target_pairs={{0,192},{16,208},{32,224},{48,240},{64,128},{80,144},{96,160},{112... | collective-permute-start | bytes 98312 | tf_op jit(solution)/shard_map/ppermute | solution.py:23
  57.8 15.0 %collective-permute-start.20 = (f32[64,128]{1,0:T(8,128)S(1)}, f32[64,128]{1,0:T(8,128)S(1)}, u32[]{:S(2)}, u32[]{:S(2)}) collective-permute-start(f32[64,128]{1,0:T(8,128)S(1)} %get-tuple-element.52), channel_id=1, source_target_pairs={{0,128},{16,144},{32,160},{48,176},{64,192},{80,208},{96,224},{112... | collective-permute-start | bytes 98312 | tf_op jit(solution)/shard_map/ppermute | solution.py:23
  58.7 14.2 %collective-permute-start.18 = (f32[64,128]{1,0:T(8,128)S(1)}, f32[64,128]{1,0:T(8,128)S(1)}, u32[]{:S(2)}, u32[]{:S(2)}) collective-permute-start(f32[64,128]{1,0:T(8,128)S(1)} %get-tuple-element.53), channel_id=1, source_target_pairs={{0,64},{16,80},{32,96},{48,112},{64,0},{80,16},{96,32},{112,48},{1... | collective-permute-start | bytes 98312 | tf_op jit(solution)/shard_map/ppermute | solution.py:23
  59.2 6.5 %collective-permute-start.9 = (f32[4,32,384]{2,1,0:T(8,128)S(1)}, f32[4,32,384]{2,1,0:T(8,128)S(1)}, u32[]{:S(2)}, u32[]{:S(2)}) collective-permute-start(f32[4,32,384]{2,1,0:T(8,128)S(1)} %slice_add_fusion.1), channel_id=1, source_target_pairs={{0,192},{16,208},{32,224},{48,240},{64,128},{80,144},{96,160},{112... | collective-permute-start | bytes 589832 | tf_op jit(solution)/shard_map/ppermute | solution.py:23
  61.2 4.9 %collective-permute-start.11 = (f32[4,32,384]{2,1,0:T(8,128)S(1)}, f32[4,32,384]{2,1,0:T(8,128)S(1)}, u32[]{:S(2)}, u32[]{:S(2)}) collective-permute-start(f32[4,32,384]{2,1,0:T(8,128)S(1)} %slice_add_fusion), channel_id=1, source_target_pairs={{0,64},{16,80},{32,96},{48,112},{64,0},{80,16},{96,32},{112,48},{1... | collective-permute-start | bytes 589832 | tf_op jit(solution)/shard_map/ppermute | solution.py:23
  66.2 6.7 %collective-permute-start.12 = (f32[64,384]{1,0:T(8,128)S(1)}, f32[64,384]{1,0:T(8,128)S(1)}, u32[]{:S(2)}, u32[]{:S(2)}) collective-permute-start(f32[64,384]{1,0:T(8,128)S(1)} %pad_maximum_fusion.2), channel_id=1, source_target_pairs={{0,16},{16,0},{32,48},{48,32},{64,80},{80,64},{96,112},{112,96},{1... | collective-permute-start | bytes 294920 | tf_op jit(solution)/shard_map/ppermute | solution.py:23
  69.0 7.6 %collective-permute-start.14 = (f32[64,384]{1,0:T(8,128)S(1)}, f32[64,384]{1,0:T(8,128)S(1)}, u32[]{:S(2)}, u32[]{:S(2)}) collective-permute-start(f32[64,384]{1,0:T(8,128)S(1)} %pad_maximum_fusion.4), channel_id=1, source_target_pairs={{0,32},{16,48},{32,0},{48,16},{64,96},{80,112},{96,64},{112,80},{1... | collective-permute-start | bytes 294920 | tf_op jit(solution)/shard_map/ppermute | solution.py:23
  72.8 8.7 %collective-permute-start.13 = (f32[64,384]{1,0:T(8,128)S(1)}, f32[64,384]{1,0:T(8,128)S(1)}, u32[]{:S(2)}, u32[]{:S(2)}) collective-permute-start(f32[64,384]{1,0:T(8,128)S(1)} %pad_maximum_fusion.3), channel_id=1, source_target_pairs={{0,48},{16,32},{32,16},{48,0},{64,112},{80,96},{96,80},{112,64},{1... | collective-permute-start | bytes 294920 | tf_op jit(solution)/shard_map/ppermute | solution.py:23
  96.0 6.8 %collective-permute-start.28 = (f32[64,128]{1,0:T(8,128)S(1)}, f32[64,128]{1,0:T(8,128)S(1)}, u32[]{:S(2)}, u32[]{:S(2)}) collective-permute-start(f32[64,128]{1,0:T(8,128)S(1)} %add_add_fusion.1), channel_id=1, source_target_pairs={{0,32},{16,48},{32,0},{48,16},{64,96},{80,112},{96,64},{112,80},{1... | collective-permute-start | bytes 98312 | tf_op jit(solution)/shard_map/ppermute | solution.py:23
  99.7 5.2 %collective-permute-start.27 = (f32[64,128]{1,0:T(8,128)S(1)}, f32[64,128]{1,0:T(8,128)S(1)}, u32[]{:S(2)}, u32[]{:S(2)}) collective-permute-start(f32[64,128]{1,0:T(8,128)S(1)} %add_add_fusion.1), channel_id=1, source_target_pairs={{0,48},{16,32},{32,16},{48,0},{64,112},{80,96},{96,80},{112,64},{1... | collective-permute-start | bytes 98312 | tf_op jit(solution)/shard_map/ppermute | solution.py:23
  105.7 4.7 %collective-permute-start.31 = (f32[2,64,128]{2,1,0:T(8,128)S(1)}, f32[2,64,128]{2,1,0:T(8,128)S(1)}, u32[]{:S(2)}, u32[]{:S(2)}) collective-permute-start(f32[2,64,128]{2,1,0:T(8,128)S(1)} %get-tuple-element.60), channel_id=1, source_target_pairs={{0,128},{16,144},{32,160},{48,176},{64,192},{80,208},{96,224},{112... | collective-permute-start | bytes 196616 | tf_op jit(solution)/shard_map/ppermute | solution.py:23
  112.0 5.9 %collective-permute-start.33 = (f32[3,64,128]{2,1,0:T(8,128)S(1)}, f32[3,64,128]{2,1,0:T(8,128)S(1)}, u32[]{:S(2)}, u32[]{:S(2)}) collective-permute-start(f32[3,64,128]{2,1,0:T(8,128)S(1)} %pad_maximum_fusion.5), channel_id=1, source_target_pairs={{0,2},{2,0},{4,6},{6,4},{8,10},{10,8},{12,14},{14,12},{1,3},{3,1},... | collective-permute-start | bytes 294920 | tf_op jit(solution)/shard_map/ppermute | solution.py:23
  (10 other events, 34.1 us)
where the time goes:
time: 119 us
  starting transfers between devices  52.6 us (44%)
  waiting for transfers between devices  49.2 us (41%)
  Pallas kernels  15.6 us (13%)
    ppermute x34, starting transfers between devices, swap(): lax.ppermute(value, axis, [(s, s ^ mask) for s in range(lax.axis_size(axi...  52.6 us
    ppermute x34, waiting for transfers between devices, swap(): lax.ppermute(value, axis, [(s, s ^ mask) for s in range(lax.axis_size(axi...  49.2 us
    pallas_call x2, Pallas kernels, scores(): pl.pallas_call(functools.partial(scores_kernel, side), out_shape=(shape(4...  8 us
    pallas_call x3, Pallas kernels, covariance_pair(): pl.pallas_call(functools.partial(pair_kernel, places, sides, len(before)...  4.81 us
  transfers between devices with their start and end apart: 34, of which 22 were waited for; matrix products, arithmetic and copies ran while one was open for 0% of the time, Pallas kernels for 5%

commit v1 on v0

--- a/solution.py
+++ b/solution.py
@@ -76,11 +76,13 @@
             others.append(
                 pltpu.make_async_copy(res.at[at(2 * t + core, size)], later.at[pl.ds(t * size, size)], nsems.at[t])
             )
-        for copy in sum(copies, []) + others:
+        for copy in copies[0] + copies[1]:
             copy.start()
     for step in range(4):
         for copy in copies[step]:
             copy.wait()
+        for copy in (copies[2], copies[3] + others[:1], others[1:], ())[step] if side else ():
+            copy.start()
         cols = slice(step * depth, (step + 1) * depth)
         if side:
             lh[cols], ll[cols] = split(lbuf[cols])
@@ -282,33 +284,46 @@
     )(*args)
 
 
-def assemble_kernel(w, corr, r1, r2, r3, far0, far, w_out, corr_out, wbuf, cbuf):
+def place_kernel(w, r1, r2, r3, out, buf):
+    y = lax.axis_index("particle") >> 2
+    for mask, piece in zip(RING, (w[0], r1[1], r2[1], r3[1])):
+        buf[at(y ^ mask, 64)] = piece
+    out[...] = buf[...].T
+
+
+def assemble_kernel(near0, r1, r2, r3, far0, far, out, buf):
     y = lax.axis_index("particle") >> 2
     core = lax.axis_index("coeffici") & 1
-    got = (None, r1, r2, r3)
+    near = (near0[...], r1[0], r2[0], r3[0])
     for n in range(4):
-        block = y ^ RING[n]
-        wbuf[at(block, 64)] = w[0] if n == 0 else got[n][1]
-        for c in range(2):
-            if n == 0:
-                piece = (corr if c == 0 else far0)[...]
-            else:
-                piece = got[n][0] if c == 0 else far[n - 1]
-            where = at(2 * block + (core ^ c), 32)
-            cbuf[where, :LANE] = piece[:32]
-            cbuf[where, LANE:] = piece[32:]
-    w_out[...] = wbuf[...].T
-    corr_out[...] = cbuf[...].T
+        for c, piece in enumerate((near[n], far0[...] if n == 0 else far[n - 1])):
+            where = at(2 * (y ^ RING[n]) + (core ^ c), 32)
+            buf[where, :LANE] = piece[:32]
+            buf[where, LANE:] = piece[32:]
+    out[...] = buf[...].T
+
+
+def place(*args):
+    return pl.pallas_call(
+        place_kernel,
+        out_shape=shape(LANE, 2 * LANE),
+        in_specs=[VMEM] * len(args),
+        out_specs=VMEM,
+        scratch_shapes=[pltpu.VMEM((2 * LANE, LANE), F32)],
+        compiler_params=params(4),
+        cost_estimate=cost(1 << 18, 1),
+        name="place",
+    )(*args)
 
 
 def assemble(*args):
     k = 2 * LANE
     return pl.pallas_call(
         assemble_kernel,
-        out_shape=(shape(LANE, k), shape(k, k)),
+        out_shape=shape(k, k),
         in_specs=[VMEM] * len(args),
-        out_specs=(VMEM, VMEM),
-        scratch_shapes=[pltpu.VMEM((k, LANE), F32), pltpu.VMEM((k, k), F32)],
+        out_specs=VMEM,
+        scratch_shapes=[pltpu.VMEM((k, k), F32)],
         compiler_params=params(4),
         name="assemble",
     )(*args)
@@ -364,7 +379,8 @@
     far0 = swap(corr, "coeffici", CORE)
     got = ring_swap([jnp.stack([corr, w[n]]) for n in (1, 2, 3)], "particle", Y)
     far = swap(jnp.stack([g[0] for g in got]), "coeffici", CORE)
-    weighted, rayleigh = assemble(w, corr, *got, far0, far)
+    weighted = place(w, *got)
+    rayleigh = assemble(corr, *got, far0, far)
     return weighted[None], rayleigh[None]
 
 

time: 119 us -> 119 us (level)
  no operation moved by 1% of the time
where the time goes in v1:
time: 119 us; the launch traced here: 118 us
  starting transfers between devices  52.9 us (44%)
  waiting for transfers between devices  48.2 us (41%)
  Pallas kernels  16 us (13%)
    ppermute x34, starting transfers between devices, swap(): lax.ppermute(value, axis, [(s, s ^ mask) for s in range(lax.axis_size(axi...  52.9 us
    ppermute x34, waiting for transfers between devices, swap(): lax.ppermute(value, axis, [(s, s ^ mask) for s in range(lax.axis_size(axi...  48.2 us
    pallas_call x2, Pallas kernels, scores(): pl.pallas_call(functools.partial(scores_kernel, side), out_shape=(shape(4...  7.7 us
    pallas_call x3, Pallas kernels, covariance_pair(): pl.pallas_call(functools.partial(pair_kernel, places, sides, len(before)...  4.8 us
  transfers between devices with their start and end apart: 34, of which 22 were waited for; matrix products, arithmetic and copies ran while one was open for 0% of the time, Pallas kernels for 5%

profile of v1, /device:TPU:1, one launch (start us, length us, event | category | flops | bytes accessed | tf_op | source)
XLA Modules:
  0.0 118.4 jit_solution(74415258143062012)
XLA Ops:
  0.6 5.7 %scores_far.1 = (f32[4,128,256]{2,1,0:T(8,128)S(1)}, bf16[512,2048]{1,0:T(8,128)(2,1)S(1)}, bf16[512,2048]{1,0:T(8,128)(2,1)S(1)}, bf16[2048,256]{1,0:T(8,128)(2...) custom-call(f32[1024,2048]{1,0:T(8,128)} %bitcast.52, f32[2048,256]{1,0:T(8,128)} %bitcast.53), custom_call_target="tpu_custom_call" | custom-call | flops 1610612736 | bytes 6291456 | tf_op jit(solution)/shard_map/scores_far/pallas_call | solution.py:111
  6.3 3.3 %collective-permute-start = (f32[4,128,256]{2,1,0:T(8,128)S(1)}, f32[4,128,256]{2,1,0:T(8,128)S(1)}, u32[]{:S(2)}, u32[]{:S(2)}) collective-permute-start(f32[4,128,256]{2,1,0:T(8,128)S(1)} %get-tuple-element.23), channel_id=1, source_target_pairs={{0,2},{2,0},{4,6},{6,4},{8,10},{10,8},{12,14},{14,12},{1,3},{3,1},... | collective-permute-start | bytes 1572872 | tf_op jit(solution)/shard_map/ppermute | solution.py:23
  9.6 2.0 %scores_near.1 = (f32[4,128,256]{2,1,0:T(8,128)S(1)}, bf16[512,2048]{1,0:T(8,128)(2,1)S(1)}, bf16[512,2048]{1,0:T(8,128)(2,1)S(1)}) custom-call(f32[512,2048]{1,0:T(8,128)S(1)} %get-tuple-element.21.refs_0_, bf16[2048,256]{1,0:T(8,128)(2,1)S(1)} %get-tuple-element.19.refs_1_.load_h, bf16[2048,256]{1,0:T(8,128)(2,1)S(1)} %get-tuple-element.20.refs_2_.load_l), custom_call_target="tpu_custom_call" | custom-call | flops 1610612736 | bytes 6291456 | tf_op jit(solution)/shard_map/scores_near/pallas_call | solution.py:111
  14.4 3.9 %collective-permute-done.3.r3 = f32[128,256]{1,0:T(8,128)S(1)} collective-permute-done((f32[128,256]{1,0:T(8,128)S(1)}, f32[128,256]{1,0:T(8,128)S(1)}, u32[]{:S(2)}, u32[]{:S(2)}) %collective-permute-start.3) | collective-permute-done | bytes 131104 | tf_op jit(solution)/shard_map/ppermute | solution.py:23
  18.3 3.2 %collective-permute-done.2.r2 = f32[128,256]{1,0:T(8,128)S(1)} collective-permute-done((f32[128,256]{1,0:T(8,128)S(1)}, f32[128,256]{1,0:T(8,128)S(1)}, u32[]{:S(2)}, u32[]{:S(2)}) %collective-permute-start.2) | collective-permute-done | bytes 131104 | tf_op jit(solution)/shard_map/ppermute | solution.py:23
  24.4 3.4 %collective-permute-done.6.refs_3_ = f32[256,128]{1,0:T(8,128)S(1)} collective-permute-done((f32[256,128]{1,0:T(8,128)S(1)}, f32[256,128]{1,0:T(8,128)S(1)}, u32[]{:S(2)}, u32[]{:S(2)}) %collective-permute-start.6) | collective-permute-done | bytes 131104 | tf_op jit(solution)/shard_map/ppermute | solution.py:23
  27.8 3.6 %collective-permute-done.5.refs_2_ = f32[256,128]{1,0:T(8,128)S(1)} collective-permute-done((f32[256,128]{1,0:T(8,128)S(1)}, f32[256,128]{1,0:T(8,128)S(1)}, u32[]{:S(2)}, u32[]{:S(2)}) %collective-permute-start.5) | collective-permute-done | bytes 131104 | tf_op jit(solution)/shard_map/ppermute | solution.py:23
  36.5 2.7 %collective-permute-start.15 = (f32[4,64,128]{2,1,0:T(8,128)S(1)}, f32[4,64,128]{2,1,0:T(8,128)S(1)}, u32[]{:S(2)}, u32[]{:S(2)}) collective-permute-start(f32[4,64,128]{2,1,0:T(8,128)S(1)} %get-tuple-element.50), channel_id=1, source_target_pairs={{0,16},{16,0},{32,48},{48,32},{64,80},{80,64},{96,112},{112,96},{1... | collective-permute-start | bytes 393224 | tf_op jit(solution)/shard_map/ppermute | solution.py:23
  39.2 5.1 %collective-permute-start.17 = (f32[4,64,128]{2,1,0:T(8,128)S(1)}, f32[4,64,128]{2,1,0:T(8,128)S(1)}, u32[]{:S(2)}, u32[]{:S(2)}) collective-permute-start(f32[4,64,128]{2,1,0:T(8,128)S(1)} %get-tuple-element.51), channel_id=1, source_target_pairs={{0,32},{16,48},{32,0},{48,16},{64,96},{80,112},{96,64},{112,80},{1... | collective-permute-start | bytes 393224 | tf_op jit(solution)/shard_map/ppermute | solution.py:23
  46.2 2.2 %shard_map.41 = (f32[8,32,384]{2,1,0:T(8,128)S(1)}, f32[8,32,384]{2,1,0:T(8,128)S(1)}) custom-call(bf16[512,512]{1,0:T(8,128)(2,1)S(1)} %stage.2.refs_0_, bf16[512,2048]{1,0:T(8,128)(2,1)S(1)} %get-tuple-element.24.refs_1_, bf16[512,2048]{1,0:T(8,128)(2,1)S(1)} %get-tuple-element.25.refs_2_, bf16[512,512]{1,0:T(8,128)(2,1)S(1)} %stage.3.refs_3_.refs_0_, ...), custom_call_target="tpu_custom_call" | custom-call | flops 805306368 | bytes 4194304 | tf_op jit(solution)/shard_map/pallas_call | solution.py:204
  48.5 4.4 %collective-permute-done.17 = f32[4,64,128]{2,1,0:T(8,128)S(1)} collective-permute-done((f32[4,64,128]{2,1,0:T(8,128)S(1)}, f32[4,64,128]{2,1,0:T(8,128)S(1)}, u32[]{:S(2)}, u32[]{:S(2)}) %collective-permute-start.17) | collective-permute-done | bytes 131104 | tf_op jit(solution)/shard_map/ppermute | solution.py:23
  52.9 2.6 %collective-permute-done.16 = f32[4,64,128]{2,1,0:T(8,128)S(1)} collective-permute-done((f32[4,64,128]{2,1,0:T(8,128)S(1)}, f32[4,64,128]{2,1,0:T(8,128)S(1)}, u32[]{:S(2)}, u32[]{:S(2)}) %collective-permute-start.16) | collective-permute-done | bytes 131104 | tf_op jit(solution)/shard_map/ppermute | solution.py:23
  55.5 2.0 %collective-permute-start.19 = (f32[64,128]{1,0:T(8,128)S(1)}, f32[64,128]{1,0:T(8,128)S(1)}, u32[]{:S(2)}, u32[]{:S(2)}) collective-permute-start(f32[64,128]{1,0:T(8,128)S(1)} %get-tuple-element.47), channel_id=1, source_target_pairs={{0,192},{16,208},{32,224},{48,240},{64,128},{80,144},{96,160},{112... | collective-permute-start | bytes 98312 | tf_op jit(solution)/shard_map/ppermute | solution.py:23
  58.9 2.0 %collective-permute-start.9 = (f32[4,32,384]{2,1,0:T(8,128)S(1)}, f32[4,32,384]{2,1,0:T(8,128)S(1)}, u32[]{:S(2)}, u32[]{:S(2)}) collective-permute-start(f32[4,32,384]{2,1,0:T(8,128)S(1)} %slice_add_fusion.1), channel_id=1, source_target_pairs={{0,192},{16,208},{32,224},{48,240},{64,128},{80,144},{96,160},{112... | collective-permute-start | bytes 589832 | tf_op jit(solution)/shard_map/ppermute | solution.py:23
  61.4 4.0 %collective-permute-done.9 = f32[4,32,384]{2,1,0:T(8,128)S(1)} collective-permute-done((f32[4,32,384]{2,1,0:T(8,128)S(1)}, f32[4,32,384]{2,1,0:T(8,128)S(1)}, u32[]{:S(2)}, u32[]{:S(2)}) %collective-permute-start.9) | collective-permute-done | bytes 196640 | tf_op jit(solution)/shard_map/ppermute | solution.py:23
  65.9 2.8 %collective-permute-start.12 = (f32[64,384]{1,0:T(8,128)S(1)}, f32[64,384]{1,0:T(8,128)S(1)}, u32[]{:S(2)}, u32[]{:S(2)}) collective-permute-start(f32[64,384]{1,0:T(8,128)S(1)} %pad_maximum_fusion.2), channel_id=1, source_target_pairs={{0,16},{16,0},{32,48},{48,32},{64,80},{80,64},{96,112},{112,96},{1... | collective-permute-start | bytes 294920 | tf_op jit(solution)/shard_map/ppermute | solution.py:23
  68.7 3.8 %collective-permute-start.14 = (f32[64,384]{1,0:T(8,128)S(1)}, f32[64,384]{1,0:T(8,128)S(1)}, u32[]{:S(2)}, u32[]{:S(2)}) collective-permute-start(f32[64,384]{1,0:T(8,128)S(1)} %pad_maximum_fusion.4), channel_id=1, source_target_pairs={{0,32},{16,48},{32,0},{48,16},{64,96},{80,112},{96,64},{112,80},{1... | collective-permute-start | bytes 294920 | tf_op jit(solution)/shard_map/ppermute | solution.py:23
  72.6 3.6 %collective-permute-done.14 = f32[64,384]{1,0:T(8,128)S(1)} collective-permute-done((f32[64,384]{1,0:T(8,128)S(1)}, f32[64,384]{1,0:T(8,128)S(1)}, u32[]{:S(2)}, u32[]{:S(2)}) %collective-permute-start.14) | collective-permute-done | bytes 98336 | tf_op jit(solution)/shard_map/ppermute | solution.py:23
  76.3 4.7 %collective-permute-done.13 = f32[64,384]{1,0:T(8,128)S(1)} collective-permute-done((f32[64,384]{1,0:T(8,128)S(1)}, f32[64,384]{1,0:T(8,128)S(1)}, u32[]{:S(2)}, u32[]{:S(2)}) %collective-permute-start.13) | collective-permute-done | bytes 98336 | tf_op jit(solution)/shard_map/ppermute | solution.py:23
  82.4 2.6 %collective-permute-done.21.other = f32[64,512]{1,0:T(8,128)S(1)} collective-permute-done((f32[64,512]{1,0:T(8,128)S(1)}, f32[64,512]{1,0:T(8,128)S(1)}, u32[]{:S(2)}, u32[]{:S(2)}) %collective-permute-start.21) | collective-permute-done | bytes 131104 | tf_op jit(solution)/shard_map/ppermute | solution.py:23
  85.3 3.0 %collective-permute-start.22 = (f32[64,128]{1,0:T(8,128)S(1)}, f32[64,128]{1,0:T(8,128)S(1)}, u32[]{:S(2)}, u32[]{:S(2)}) collective-permute-start(f32[64,128]{1,0:T(8,128)S(1)} %slice_bitcast_fusion), channel_id=1, source_target_pairs={{0,2},{2,0},{4,6},{6,4},{8,10},{10,8},{12,14},{14,12},{1,3},{3,1},... | collective-permute-start | bytes 98312 | tf_op jit(solution)/shard_map/ppermute | solution.py:23
  95.7 3.8 %collective-permute-start.28 = (f32[64,128]{1,0:T(8,128)S(1)}, f32[64,128]{1,0:T(8,128)S(1)}, u32[]{:S(2)}, u32[]{:S(2)}) collective-permute-start(f32[64,128]{1,0:T(8,128)S(1)} %add_add_fusion.1), channel_id=1, source_target_pairs={{0,32},{16,48},{32,0},{48,16},{64,96},{80,112},{96,64},{112,80},{1... | collective-permute-start | bytes 98312 | tf_op jit(solution)/shard_map/ppermute | solution.py:23
  102.5 2.2 %collective-permute-done.27 = f32[64,128]{1,0:T(8,128)S(1)} collective-permute-done((f32[64,128]{1,0:T(8,128)S(1)}, f32[64,128]{1,0:T(8,128)S(1)}, u32[]{:S(2)}, u32[]{:S(2)}) %collective-permute-start.27) | collective-permute-done | bytes 32800 | tf_op jit(solution)/shard_map/ppermute | solution.py:23
  111.7 4.6 %collective-permute-start.33 = (f32[3,64,128]{2,1,0:T(8,128)S(1)}, f32[3,64,128]{2,1,0:T(8,128)S(1)}, u32[]{:S(2)}, u32[]{:S(2)}) collective-permute-start(f32[3,64,128]{2,1,0:T(8,128)S(1)} %pad_maximum_fusion.5), channel_id=1, source_target_pairs={{0,2},{2,0},{4,6},{6,4},{8,10},{10,8},{12,14},{14,12},{1,3},{3,1},... | collective-permute-start | bytes 294920 | tf_op jit(solution)/shard_map/ppermute | solution.py:23
  (80 shorter events, 36.1 us)
Async XLA Ops:
  6.3 5.3 %collective-permute-start = (f32[4,128,256]{2,1,0:T(8,128)S(1)}, f32[4,128,256]{2,1,0:T(8,128)S(1)}, u32[]{:S(2)}, u32[]{:S(2)}) collective-permute-start(f32[4,128,256]{2,1,0:T(8,128)S(1)} %get-tuple-element.23), channel_id=1, source_target_pairs={{0,2},{2,0},{4,6},{6,4},{8,10},{10,8},{12,14},{14,12},{1,3},{3,1},... | collective-permute-start | bytes 1572872 | tf_op jit(solution)/shard_map/ppermute | solution.py:23
  11.7 6.6 %collective-permute-start.3 = (f32[128,256]{1,0:T(8,128)S(1)}, f32[128,256]{1,0:T(8,128)S(1)}, u32[]{:S(2)}, u32[]{:S(2)}) collective-permute-start(f32[128,256]{1,0:T(8,128)S(1)} %get-tuple-element.36), channel_id=1, source_target_pairs={{0,8},{2,10},{4,12},{6,14},{8,0},{10,2},{12,4},{14,6},{1,9},{3,11}... | collective-permute-start | bytes 393224 | tf_op jit(solution)/shard_map/ppermute | solution.py:23
  12.8 8.7 %collective-permute-start.2 = (f32[128,256]{1,0:T(8,128)S(1)}, f32[128,256]{1,0:T(8,128)S(1)}, u32[]{:S(2)}, u32[]{:S(2)}) collective-permute-start(f32[128,256]{1,0:T(8,128)S(1)} %get-tuple-element.37), channel_id=1, source_target_pairs={{0,12},{2,14},{4,8},{6,10},{8,4},{10,6},{12,0},{14,2},{1,13},{3,15... | collective-permute-start | bytes 393224 | tf_op jit(solution)/shard_map/ppermute | solution.py:23
  13.7 7.9 %collective-permute-start.1 = (f32[128,256]{1,0:T(8,128)S(1)}, f32[128,256]{1,0:T(8,128)S(1)}, u32[]{:S(2)}, u32[]{:S(2)}) collective-permute-start(f32[128,256]{1,0:T(8,128)S(1)} %get-tuple-element.38), channel_id=1, source_target_pairs={{0,4},{2,6},{4,0},{6,2},{8,12},{10,14},{12,8},{14,10},{1,5},{3,7},... | collective-permute-start | bytes 393224 | tf_op jit(solution)/shard_map/ppermute | solution.py:23
  21.7 6.2 %collective-permute-start.6 = (f32[256,128]{1,0:T(8,128)S(1)}, f32[256,128]{1,0:T(8,128)S(1)}, u32[]{:S(2)}, u32[]{:S(2)}) collective-permute-start(f32[256,128]{1,0:T(8,128)S(1)} %own_block.1.refs_0_), channel_id=1, source_target_pairs={{0,8},{2,10},{4,12},{6,14},{8,0},{10,2},{12,4},{14,6},{1,9},{3,11}... | collective-permute-start | bytes 393224 | tf_op jit(solution)/shard_map/ppermute | solution.py:23
  22.8 8.7 %collective-permute-start.5 = (f32[256,128]{1,0:T(8,128)S(1)}, f32[256,128]{1,0:T(8,128)S(1)}, u32[]{:S(2)}, u32[]{:S(2)}) collective-permute-start(f32[256,128]{1,0:T(8,128)S(1)} %own_block.1.refs_0_), channel_id=1, source_target_pairs={{0,12},{2,14},{4,8},{6,10},{8,4},{10,6},{12,0},{14,2},{1,13},{3,15... | collective-permute-start | bytes 393224 | tf_op jit(solution)/shard_map/ppermute | solution.py:23
  23.6 7.8 %collective-permute-start.4 = (f32[256,128]{1,0:T(8,128)S(1)}, f32[256,128]{1,0:T(8,128)S(1)}, u32[]{:S(2)}, u32[]{:S(2)}) collective-permute-start(f32[256,128]{1,0:T(8,128)S(1)} %own_block.1.refs_0_), channel_id=1, source_target_pairs={{0,4},{2,6},{4,0},{6,2},{8,12},{10,14},{12,8},{14,10},{1,5},{3,7},... | collective-permute-start | bytes 393224 | tf_op jit(solution)/shard_map/ppermute | solution.py:23
  36.4 22.5 %collective-permute-start.8 = (f32[8,32,384]{2,1,0:T(8,128)S(1)}, f32[8,32,384]{2,1,0:T(8,128)S(1)}, u32[]{:S(2)}, u32[]{:S(2)}) collective-permute-start(f32[8,32,384]{2,1,0:T(8,128)S(1)} %get-tuple-element.31), channel_id=1, source_target_pairs={{0,64},{16,80},{32,96},{48,112},{64,0},{80,16},{96,32},{112,48},{1... | collective-permute-start | bytes 1179656 | tf_op jit(solution)/shard_map/ppermute | solution.py:23
  36.5 12.0 %collective-permute-start.15 = (f32[4,64,128]{2,1,0:T(8,128)S(1)}, f32[4,64,128]{2,1,0:T(8,128)S(1)}, u32[]{:S(2)}, u32[]{:S(2)}) collective-permute-start(f32[4,64,128]{2,1,0:T(8,128)S(1)} %get-tuple-element.50), channel_id=1, source_target_pairs={{0,16},{16,0},{32,48},{48,32},{64,80},{80,64},{96,112},{112,96},{1... | collective-permute-start | bytes 393224 | tf_op jit(solution)/shard_map/ppermute | solution.py:23
  39.2 13.7 %collective-permute-start.17 = (f32[4,64,128]{2,1,0:T(8,128)S(1)}, f32[4,64,128]{2,1,0:T(8,128)S(1)}, u32[]{:S(2)}, u32[]{:S(2)}) collective-permute-start(f32[4,64,128]{2,1,0:T(8,128)S(1)} %get-tuple-element.51), channel_id=1, source_target_pairs={{0,32},{16,48},{32,0},{48,16},{64,96},{80,112},{96,64},{112,80},{1... | collective-permute-start | bytes 393224 | tf_op jit(solution)/shard_map/ppermute | solution.py:23
  44.3 11.2 %collective-permute-start.16 = (f32[4,64,128]{2,1,0:T(8,128)S(1)}, f32[4,64,128]{2,1,0:T(8,128)S(1)}, u32[]{:S(2)}, u32[]{:S(2)}) collective-permute-start(f32[4,64,128]{2,1,0:T(8,128)S(1)} %get-tuple-element.52), channel_id=1, source_target_pairs={{0,48},{16,32},{32,16},{48,0},{64,112},{80,96},{96,80},{112,64},{1... | collective-permute-start | bytes 393224 | tf_op jit(solution)/shard_map/ppermute | solution.py:23
  44.3 16.6 %collective-permute-start.10 = (f32[8,32,384]{2,1,0:T(8,128)S(1)}, f32[8,32,384]{2,1,0:T(8,128)S(1)}, u32[]{:S(2)}, u32[]{:S(2)}) collective-permute-start(f32[8,32,384]{2,1,0:T(8,128)S(1)} %get-tuple-element.33), channel_id=1, source_target_pairs={{0,192},{16,208},{32,224},{48,240},{64,128},{80,144},{96,160},{112... | collective-permute-start | bytes 1179656 | tf_op jit(solution)/shard_map/ppermute | solution.py:23
  55.5 16.9 %collective-permute-start.19 = (f32[64,128]{1,0:T(8,128)S(1)}, f32[64,128]{1,0:T(8,128)S(1)}, u32[]{:S(2)}, u32[]{:S(2)}) collective-permute-start(f32[64,128]{1,0:T(8,128)S(1)} %get-tuple-element.47), channel_id=1, source_target_pairs={{0,192},{16,208},{32,224},{48,240},{64,128},{80,144},{96,160},{112... | collective-permute-start | bytes 98312 | tf_op jit(solution)/shard_map/ppermute | solution.py:23
  57.5 15.0 %collective-permute-start.20 = (f32[64,128]{1,0:T(8,128)S(1)}, f32[64,128]{1,0:T(8,128)S(1)}, u32[]{:S(2)}, u32[]{:S(2)}) collective-permute-start(f32[64,128]{1,0:T(8,128)S(1)} %get-tuple-element.48), channel_id=1, source_target_pairs={{0,128},{16,144},{32,160},{48,176},{64,192},{80,208},{96,224},{112... | collective-permute-start | bytes 98312 | tf_op jit(solution)/shard_map/ppermute | solution.py:23
  58.4 14.2 %collective-permute-start.18 = (f32[64,128]{1,0:T(8,128)S(1)}, f32[64,128]{1,0:T(8,128)S(1)}, u32[]{:S(2)}, u32[]{:S(2)}) collective-permute-start(f32[64,128]{1,0:T(8,128)S(1)} %get-tuple-element.49), channel_id=1, source_target_pairs={{0,64},{16,80},{32,96},{48,112},{64,0},{80,16},{96,32},{112,48},{1... | collective-permute-start | bytes 98312 | tf_op jit(solution)/shard_map/ppermute | solution.py:23
  58.9 6.5 %collective-permute-start.9 = (f32[4,32,384]{2,1,0:T(8,128)S(1)}, f32[4,32,384]{2,1,0:T(8,128)S(1)}, u32[]{:S(2)}, u32[]{:S(2)}) collective-permute-start(f32[4,32,384]{2,1,0:T(8,128)S(1)} %slice_add_fusion.1), channel_id=1, source_target_pairs={{0,192},{16,208},{32,224},{48,240},{64,128},{80,144},{96,160},{112... | collective-permute-start | bytes 589832 | tf_op jit(solution)/shard_map/ppermute | solution.py:23
  60.9 4.9 %collective-permute-start.11 = (f32[4,32,384]{2,1,0:T(8,128)S(1)}, f32[4,32,384]{2,1,0:T(8,128)S(1)}, u32[]{:S(2)}, u32[]{:S(2)}) collective-permute-start(f32[4,32,384]{2,1,0:T(8,128)S(1)} %slice_add_fusion), channel_id=1, source_target_pairs={{0,64},{16,80},{32,96},{48,112},{64,0},{80,16},{96,32},{112,48},{1... | collective-permute-start | bytes 589832 | tf_op jit(solution)/shard_map/ppermute | solution.py:23
  65.9 6.7 %collective-permute-start.12 = (f32[64,384]{1,0:T(8,128)S(1)}, f32[64,384]{1,0:T(8,128)S(1)}, u32[]{:S(2)}, u32[]{:S(2)}) collective-permute-start(f32[64,384]{1,0:T(8,128)S(1)} %pad_maximum_fusion.2), channel_id=1, source_target_pairs={{0,16},{16,0},{32,48},{48,32},{64,80},{80,64},{96,112},{112,96},{1... | collective-permute-start | bytes 294920 | tf_op jit(solution)/shard_map/ppermute | solution.py:23
  68.7 7.6 %collective-permute-start.14 = (f32[64,384]{1,0:T(8,128)S(1)}, f32[64,384]{1,0:T(8,128)S(1)}, u32[]{:S(2)}, u32[]{:S(2)}) collective-permute-start(f32[64,384]{1,0:T(8,128)S(1)} %pad_maximum_fusion.4), channel_id=1, source_target_pairs={{0,32},{16,48},{32,0},{48,16},{64,96},{80,112},{96,64},{112,80},{1... | collective-permute-start | bytes 294920 | tf_op jit(solution)/shard_map/ppermute | solution.py:23
  72.5 8.5 %collective-permute-start.13 = (f32[64,384]{1,0:T(8,128)S(1)}, f32[64,384]{1,0:T(8,128)S(1)}, u32[]{:S(2)}, u32[]{:S(2)}) collective-permute-start(f32[64,384]{1,0:T(8,128)S(1)} %pad_maximum_fusion.3), channel_id=1, source_target_pairs={{0,48},{16,32},{32,16},{48,0},{64,112},{80,96},{96,80},{112,64},{1... | collective-permute-start | bytes 294920 | tf_op jit(solution)/shard_map/ppermute | solution.py:23
  95.7 6.8 %collective-permute-start.28 = (f32[64,128]{1,0:T(8,128)S(1)}, f32[64,128]{1,0:T(8,128)S(1)}, u32[]{:S(2)}, u32[]{:S(2)}) collective-permute-start(f32[64,128]{1,0:T(8,128)S(1)} %add_add_fusion.1), channel_id=1, source_target_pairs={{0,32},{16,48},{32,0},{48,16},{64,96},{80,112},{96,64},{112,80},{1... | collective-permute-start | bytes 98312 | tf_op jit(solution)/shard_map/ppermute | solution.py:23
  99.6 5.2 %collective-permute-start.27 = (f32[64,128]{1,0:T(8,128)S(1)}, f32[64,128]{1,0:T(8,128)S(1)}, u32[]{:S(2)}, u32[]{:S(2)}) collective-permute-start(f32[64,128]{1,0:T(8,128)S(1)} %add_add_fusion.1), channel_id=1, source_target_pairs={{0,48},{16,32},{32,16},{48,0},{64,112},{80,96},{96,80},{112,64},{1... | collective-permute-start | bytes 98312 | tf_op jit(solution)/shard_map/ppermute | solution.py:23
  105.4 4.7 %collective-permute-start.31 = (f32[2,64,128]{2,1,0:T(8,128)S(1)}, f32[2,64,128]{2,1,0:T(8,128)S(1)}, u32[]{:S(2)}, u32[]{:S(2)}) collective-permute-start(f32[2,64,128]{2,1,0:T(8,128)S(1)} %get-tuple-element.56), channel_id=1, source_target_pairs={{0,128},{16,144},{32,160},{48,176},{64,192},{80,208},{96,224},{112... | collective-permute-start | bytes 196616 | tf_op jit(solution)/shard_map/ppermute | solution.py:23
  111.7 5.8 %collective-permute-start.33 = (f32[3,64,128]{2,1,0:T(8,128)S(1)}, f32[3,64,128]{2,1,0:T(8,128)S(1)}, u32[]{:S(2)}, u32[]{:S(2)}) collective-permute-start(f32[3,64,128]{2,1,0:T(8,128)S(1)} %pad_maximum_fusion.5), channel_id=1, source_target_pairs={{0,2},{2,0},{4,6},{6,4},{8,10},{10,8},{12,14},{14,12},{1,3},{3,1},... | collective-permute-start | bytes 294920 | tf_op jit(solution)/shard_map/ppermute | solution.py:23
  (10 other events, 34.3 us)

commit v2 on v1

--- a/solution.py
+++ b/solution.py
@@ -76,12 +76,12 @@
             others.append(
                 pltpu.make_async_copy(res.at[at(2 * t + core, size)], later.at[pl.ds(t * size, size)], nsems.at[t])
             )
-        for copy in copies[0] + copies[1]:
+        for copy in copies[0] + copies[1] + copies[2]:
             copy.start()
     for step in range(4):
         for copy in copies[step]:
             copy.wait()
-        for copy in (copies[2], copies[3] + others[:1], others[1:], ())[step] if side else ():
+        for copy in (copies[3] + others[:1], others[1:], (), ())[step] if side else ():
             copy.start()
         cols = slice(step * depth, (step + 1) * depth)
         if side:
@@ -330,7 +330,10 @@
 
 
 def ring_swap(values, axis, unit):
-    return [swap(v, axis, unit * m) for v, m in zip(values, RING[1:])]
+    swapped = []
+    for v, m in zip(values, RING[1:]):
+        swapped.append(swap(v, axis, unit * m))
+    return swapped
 
 
 def ring_sum(value, axis, unit):

time: 119 us -> 119 us (level)
  no operation moved by 1% of the time
where the time goes in v2:
time: 119 us; the launch traced here: 118 us
  starting transfers between devices  52.9 us (44%)
  waiting for transfers between devices  48.2 us (41%)
  Pallas kernels  16.1 us (14%)
    ppermute x34, starting transfers between devices, swap(): lax.ppermute(value, axis, [(s, s ^ mask) for s in range(lax.axis_size(axi...  52.9 us
    ppermute x34, waiting for transfers between devices, swap(): lax.ppermute(value, axis, [(s, s ^ mask) for s in range(lax.axis_size(axi...  48.2 us
    pallas_call x2, Pallas kernels, scores(): pl.pallas_call(functools.partial(scores_kernel, side), out_shape=(shape(4...  7.76 us
    pallas_call x3, Pallas kernels, covariance_pair(): pl.pallas_call(functools.partial(pair_kernel, places, sides, len(before)...  4.8 us
  transfers between devices with their start and end apart: 34, of which 22 were waited for; matrix products, arithmetic and copies ran while one was open for 0% of the time, Pallas kernels for 5%

profile of v2, /device:TPU:1, one launch (start us, length us, event | category | flops | bytes accessed | tf_op | source)
XLA Modules:
  0.0 118.5 jit_solution(17360602052700710562)
XLA Ops:
  0.6 5.8 %scores_far.1 = (f32[4,128,256]{2,1,0:T(8,128)S(1)}, bf16[512,2048]{1,0:T(8,128)(2,1)S(1)}, bf16[512,2048]{1,0:T(8,128)(2,1)S(1)}, bf16[2048,256]{1,0:T(8,128)(2...) custom-call(f32[1024,2048]{1,0:T(8,128)} %bitcast.52, f32[2048,256]{1,0:T(8,128)} %bitcast.53), custom_call_target="tpu_custom_call" | custom-call | flops 1610612736 | bytes 6291456 | tf_op jit(solution)/shard_map/scores_far/pallas_call | solution.py:111
  6.4 3.3 %collective-permute-start = (f32[4,128,256]{2,1,0:T(8,128)S(1)}, f32[4,128,256]{2,1,0:T(8,128)S(1)}, u32[]{:S(2)}, u32[]{:S(2)}) collective-permute-start(f32[4,128,256]{2,1,0:T(8,128)S(1)} %get-tuple-element.23), channel_id=1, source_target_pairs={{0,2},{2,0},{4,6},{6,4},{8,10},{10,8},{12,14},{14,12},{1,3},{3,1},... | collective-permute-start | bytes 1572872 | tf_op jit(solution)/shard_map/ppermute | solution.py:23
  9.7 2.0 %scores_near.1 = (f32[4,128,256]{2,1,0:T(8,128)S(1)}, bf16[512,2048]{1,0:T(8,128)(2,1)S(1)}, bf16[512,2048]{1,0:T(8,128)(2,1)S(1)}) custom-call(f32[512,2048]{1,0:T(8,128)S(1)} %get-tuple-element.21.refs_0_, bf16[2048,256]{1,0:T(8,128)(2,1)S(1)} %get-tuple-element.19.refs_1_.load_h, bf16[2048,256]{1,0:T(8,128)(2,1)S(1)} %get-tuple-element.20.refs_2_.load_l), custom_call_target="tpu_custom_call" | custom-call | flops 1610612736 | bytes 6291456 | tf_op jit(solution)/shard_map/scores_near/pallas_call | solution.py:111
  14.5 3.9 %collective-permute-done.3.r3 = f32[128,256]{1,0:T(8,128)S(1)} collective-permute-done((f32[128,256]{1,0:T(8,128)S(1)}, f32[128,256]{1,0:T(8,128)S(1)}, u32[]{:S(2)}, u32[]{:S(2)}) %collective-permute-start.3) | collective-permute-done | bytes 131104 | tf_op jit(solution)/shard_map/ppermute | solution.py:23
  18.4 3.2 %collective-permute-done.2.r2 = f32[128,256]{1,0:T(8,128)S(1)} collective-permute-done((f32[128,256]{1,0:T(8,128)S(1)}, f32[128,256]{1,0:T(8,128)S(1)}, u32[]{:S(2)}, u32[]{:S(2)}) %collective-permute-start.2) | collective-permute-done | bytes 131104 | tf_op jit(solution)/shard_map/ppermute | solution.py:23
  24.5 3.4 %collective-permute-done.6.refs_3_ = f32[256,128]{1,0:T(8,128)S(1)} collective-permute-done((f32[256,128]{1,0:T(8,128)S(1)}, f32[256,128]{1,0:T(8,128)S(1)}, u32[]{:S(2)}, u32[]{:S(2)}) %collective-permute-start.6) | collective-permute-done | bytes 131104 | tf_op jit(solution)/shard_map/ppermute | solution.py:23
  27.9 3.6 %collective-permute-done.5.refs_2_ = f32[256,128]{1,0:T(8,128)S(1)} collective-permute-done((f32[256,128]{1,0:T(8,128)S(1)}, f32[256,128]{1,0:T(8,128)S(1)}, u32[]{:S(2)}, u32[]{:S(2)}) %collective-permute-start.5) | collective-permute-done | bytes 131104 | tf_op jit(solution)/shard_map/ppermute | solution.py:23
  36.6 2.7 %collective-permute-start.15 = (f32[4,64,128]{2,1,0:T(8,128)S(1)}, f32[4,64,128]{2,1,0:T(8,128)S(1)}, u32[]{:S(2)}, u32[]{:S(2)}) collective-permute-start(f32[4,64,128]{2,1,0:T(8,128)S(1)} %get-tuple-element.50), channel_id=1, source_target_pairs={{0,16},{16,0},{32,48},{48,32},{64,80},{80,64},{96,112},{112,96},{1... | collective-permute-start | bytes 393224 | tf_op jit(solution)/shard_map/ppermute | solution.py:23
  39.3 5.1 %collective-permute-start.17 = (f32[4,64,128]{2,1,0:T(8,128)S(1)}, f32[4,64,128]{2,1,0:T(8,128)S(1)}, u32[]{:S(2)}, u32[]{:S(2)}) collective-permute-start(f32[4,64,128]{2,1,0:T(8,128)S(1)} %get-tuple-element.51), channel_id=1, source_target_pairs={{0,32},{16,48},{32,0},{48,16},{64,96},{80,112},{96,64},{112,80},{1... | collective-permute-start | bytes 393224 | tf_op jit(solution)/shard_map/ppermute | solution.py:23
  46.3 2.2 %shard_map.41 = (f32[8,32,384]{2,1,0:T(8,128)S(1)}, f32[8,32,384]{2,1,0:T(8,128)S(1)}) custom-call(bf16[512,512]{1,0:T(8,128)(2,1)S(1)} %stage.2.refs_0_, bf16[512,2048]{1,0:T(8,128)(2,1)S(1)} %get-tuple-element.24.refs_1_, bf16[512,2048]{1,0:T(8,128)(2,1)S(1)} %get-tuple-element.25.refs_2_, bf16[512,512]{1,0:T(8,128)(2,1)S(1)} %stage.3.refs_3_.refs_0_, ...), custom_call_target="tpu_custom_call" | custom-call | flops 805306368 | bytes 4194304 | tf_op jit(solution)/shard_map/pallas_call | solution.py:204
  48.5 4.4 %collective-permute-done.17 = f32[4,64,128]{2,1,0:T(8,128)S(1)} collective-permute-done((f32[4,64,128]{2,1,0:T(8,128)S(1)}, f32[4,64,128]{2,1,0:T(8,128)S(1)}, u32[]{:S(2)}, u32[]{:S(2)}) %collective-permute-start.17) | collective-permute-done | bytes 131104 | tf_op jit(solution)/shard_map/ppermute | solution.py:23
  53.0 2.6 %collective-permute-done.16 = f32[4,64,128]{2,1,0:T(8,128)S(1)} collective-permute-done((f32[4,64,128]{2,1,0:T(8,128)S(1)}, f32[4,64,128]{2,1,0:T(8,128)S(1)}, u32[]{:S(2)}, u32[]{:S(2)}) %collective-permute-start.16) | collective-permute-done | bytes 131104 | tf_op jit(solution)/shard_map/ppermute | solution.py:23
  55.6 2.0 %collective-permute-start.19 = (f32[64,128]{1,0:T(8,128)S(1)}, f32[64,128]{1,0:T(8,128)S(1)}, u32[]{:S(2)}, u32[]{:S(2)}) collective-permute-start(f32[64,128]{1,0:T(8,128)S(1)} %get-tuple-element.47), channel_id=1, source_target_pairs={{0,192},{16,208},{32,224},{48,240},{64,128},{80,144},{96,160},{112... | collective-permute-start | bytes 98312 | tf_op jit(solution)/shard_map/ppermute | solution.py:23
  59.0 2.0 %collective-permute-start.9 = (f32[4,32,384]{2,1,0:T(8,128)S(1)}, f32[4,32,384]{2,1,0:T(8,128)S(1)}, u32[]{:S(2)}, u32[]{:S(2)}) collective-permute-start(f32[4,32,384]{2,1,0:T(8,128)S(1)} %slice_add_fusion.1), channel_id=1, source_target_pairs={{0,192},{16,208},{32,224},{48,240},{64,128},{80,144},{96,160},{112... | collective-permute-start | bytes 589832 | tf_op jit(solution)/shard_map/ppermute | solution.py:23
  61.5 4.0 %collective-permute-done.9 = f32[4,32,384]{2,1,0:T(8,128)S(1)} collective-permute-done((f32[4,32,384]{2,1,0:T(8,128)S(1)}, f32[4,32,384]{2,1,0:T(8,128)S(1)}, u32[]{:S(2)}, u32[]{:S(2)}) %collective-permute-start.9) | collective-permute-done | bytes 196640 | tf_op jit(solution)/shard_map/ppermute | solution.py:23
  66.0 2.8 %collective-permute-start.12 = (f32[64,384]{1,0:T(8,128)S(1)}, f32[64,384]{1,0:T(8,128)S(1)}, u32[]{:S(2)}, u32[]{:S(2)}) collective-permute-start(f32[64,384]{1,0:T(8,128)S(1)} %pad_maximum_fusion.2), channel_id=1, source_target_pairs={{0,16},{16,0},{32,48},{48,32},{64,80},{80,64},{96,112},{112,96},{1... | collective-permute-start | bytes 294920 | tf_op jit(solution)/shard_map/ppermute | solution.py:23
  68.7 3.8 %collective-permute-start.14 = (f32[64,384]{1,0:T(8,128)S(1)}, f32[64,384]{1,0:T(8,128)S(1)}, u32[]{:S(2)}, u32[]{:S(2)}) collective-permute-start(f32[64,384]{1,0:T(8,128)S(1)} %pad_maximum_fusion.4), channel_id=1, source_target_pairs={{0,32},{16,48},{32,0},{48,16},{64,96},{80,112},{96,64},{112,80},{1... | collective-permute-start | bytes 294920 | tf_op jit(solution)/shard_map/ppermute | solution.py:23
  72.7 3.6 %collective-permute-done.14 = f32[64,384]{1,0:T(8,128)S(1)} collective-permute-done((f32[64,384]{1,0:T(8,128)S(1)}, f32[64,384]{1,0:T(8,128)S(1)}, u32[]{:S(2)}, u32[]{:S(2)}) %collective-permute-start.14) | collective-permute-done | bytes 98336 | tf_op jit(solution)/shard_map/ppermute | solution.py:23
  76.3 4.7 %collective-permute-done.13 = f32[64,384]{1,0:T(8,128)S(1)} collective-permute-done((f32[64,384]{1,0:T(8,128)S(1)}, f32[64,384]{1,0:T(8,128)S(1)}, u32[]{:S(2)}, u32[]{:S(2)}) %collective-permute-start.13) | collective-permute-done | bytes 98336 | tf_op jit(solution)/shard_map/ppermute | solution.py:23
  82.4 2.6 %collective-permute-done.21.other = f32[64,512]{1,0:T(8,128)S(1)} collective-permute-done((f32[64,512]{1,0:T(8,128)S(1)}, f32[64,512]{1,0:T(8,128)S(1)}, u32[]{:S(2)}, u32[]{:S(2)}) %collective-permute-start.21) | collective-permute-done | bytes 131104 | tf_op jit(solution)/shard_map/ppermute | solution.py:23
  85.3 3.0 %collective-permute-start.22 = (f32[64,128]{1,0:T(8,128)S(1)}, f32[64,128]{1,0:T(8,128)S(1)}, u32[]{:S(2)}, u32[]{:S(2)}) collective-permute-start(f32[64,128]{1,0:T(8,128)S(1)} %slice_bitcast_fusion), channel_id=1, source_target_pairs={{0,2},{2,0},{4,6},{6,4},{8,10},{10,8},{12,14},{14,12},{1,3},{3,1},... | collective-permute-start | bytes 98312 | tf_op jit(solution)/shard_map/ppermute | solution.py:23
  95.8 3.8 %collective-permute-start.28 = (f32[64,128]{1,0:T(8,128)S(1)}, f32[64,128]{1,0:T(8,128)S(1)}, u32[]{:S(2)}, u32[]{:S(2)}) collective-permute-start(f32[64,128]{1,0:T(8,128)S(1)} %add_add_fusion.1), channel_id=1, source_target_pairs={{0,32},{16,48},{32,0},{48,16},{64,96},{80,112},{96,64},{112,80},{1... | collective-permute-start | bytes 98312 | tf_op jit(solution)/shard_map/ppermute | solution.py:23
  102.6 2.5 %collective-permute-done.27 = f32[64,128]{1,0:T(8,128)S(1)} collective-permute-done((f32[64,128]{1,0:T(8,128)S(1)}, f32[64,128]{1,0:T(8,128)S(1)}, u32[]{:S(2)}, u32[]{:S(2)}) %collective-permute-start.27) | collective-permute-done | bytes 32800 | tf_op jit(solution)/shard_map/ppermute | solution.py:23
  111.8 4.6 %collective-permute-start.33 = (f32[3,64,128]{2,1,0:T(8,128)S(1)}, f32[3,64,128]{2,1,0:T(8,128)S(1)}, u32[]{:S(2)}, u32[]{:S(2)}) collective-permute-start(f32[3,64,128]{2,1,0:T(8,128)S(1)} %pad_maximum_fusion.5), channel_id=1, source_target_pairs={{0,2},{2,0},{4,6},{6,4},{8,10},{10,8},{12,14},{14,12},{1,3},{3,1},... | collective-permute-start | bytes 294920 | tf_op jit(solution)/shard_map/ppermute | solution.py:23
  (80 shorter events, 35.8 us)
Async XLA Ops:
  6.4 5.3 %collective-permute-start = (f32[4,128,256]{2,1,0:T(8,128)S(1)}, f32[4,128,256]{2,1,0:T(8,128)S(1)}, u32[]{:S(2)}, u32[]{:S(2)}) collective-permute-start(f32[4,128,256]{2,1,0:T(8,128)S(1)} %get-tuple-element.23), channel_id=1, source_target_pairs={{0,2},{2,0},{4,6},{6,4},{8,10},{10,8},{12,14},{14,12},{1,3},{3,1},... | collective-permute-start | bytes 1572872 | tf_op jit(solution)/shard_map/ppermute | solution.py:23
  11.8 6.6 %collective-permute-start.3 = (f32[128,256]{1,0:T(8,128)S(1)}, f32[128,256]{1,0:T(8,128)S(1)}, u32[]{:S(2)}, u32[]{:S(2)}) collective-permute-start(f32[128,256]{1,0:T(8,128)S(1)} %get-tuple-element.36), channel_id=1, source_target_pairs={{0,8},{2,10},{4,12},{6,14},{8,0},{10,2},{12,4},{14,6},{1,9},{3,11}... | collective-permute-start | bytes 393224 | tf_op jit(solution)/shard_map/ppermute | solution.py:23
  12.9 8.7 %collective-permute-start.2 = (f32[128,256]{1,0:T(8,128)S(1)}, f32[128,256]{1,0:T(8,128)S(1)}, u32[]{:S(2)}, u32[]{:S(2)}) collective-permute-start(f32[128,256]{1,0:T(8,128)S(1)} %get-tuple-element.37), channel_id=1, source_target_pairs={{0,12},{2,14},{4,8},{6,10},{8,4},{10,6},{12,0},{14,2},{1,13},{3,15... | collective-permute-start | bytes 393224 | tf_op jit(solution)/shard_map/ppermute | solution.py:23
  13.7 7.9 %collective-permute-start.1 = (f32[128,256]{1,0:T(8,128)S(1)}, f32[128,256]{1,0:T(8,128)S(1)}, u32[]{:S(2)}, u32[]{:S(2)}) collective-permute-start(f32[128,256]{1,0:T(8,128)S(1)} %get-tuple-element.38), channel_id=1, source_target_pairs={{0,4},{2,6},{4,0},{6,2},{8,12},{10,14},{12,8},{14,10},{1,5},{3,7},... | collective-permute-start | bytes 393224 | tf_op jit(solution)/shard_map/ppermute | solution.py:23
  21.7 6.2 %collective-permute-start.6 = (f32[256,128]{1,0:T(8,128)S(1)}, f32[256,128]{1,0:T(8,128)S(1)}, u32[]{:S(2)}, u32[]{:S(2)}) collective-permute-start(f32[256,128]{1,0:T(8,128)S(1)} %own_block.1.refs_0_), channel_id=1, source_target_pairs={{0,8},{2,10},{4,12},{6,14},{8,0},{10,2},{12,4},{14,6},{1,9},{3,11}... | collective-permute-start | bytes 393224 | tf_op jit(solution)/shard_map/ppermute | solution.py:23
  22.8 8.7 %collective-permute-start.5 = (f32[256,128]{1,0:T(8,128)S(1)}, f32[256,128]{1,0:T(8,128)S(1)}, u32[]{:S(2)}, u32[]{:S(2)}) collective-permute-start(f32[256,128]{1,0:T(8,128)S(1)} %own_block.1.refs_0_), channel_id=1, source_target_pairs={{0,12},{2,14},{4,8},{6,10},{8,4},{10,6},{12,0},{14,2},{1,13},{3,15... | collective-permute-start | bytes 393224 | tf_op jit(solution)/shard_map/ppermute | solution.py:23
  23.7 7.8 %collective-permute-start.4 = (f32[256,128]{1,0:T(8,128)S(1)}, f32[256,128]{1,0:T(8,128)S(1)}, u32[]{:S(2)}, u32[]{:S(2)}) collective-permute-start(f32[256,128]{1,0:T(8,128)S(1)} %own_block.1.refs_0_), channel_id=1, source_target_pairs={{0,4},{2,6},{4,0},{6,2},{8,12},{10,14},{12,8},{14,10},{1,5},{3,7},... | collective-permute-start | bytes 393224 | tf_op jit(solution)/shard_map/ppermute | solution.py:23
  36.4 22.5 %collective-permute-start.8 = (f32[8,32,384]{2,1,0:T(8,128)S(1)}, f32[8,32,384]{2,1,0:T(8,128)S(1)}, u32[]{:S(2)}, u32[]{:S(2)}) collective-permute-start(f32[8,32,384]{2,1,0:T(8,128)S(1)} %get-tuple-element.31), channel_id=1, source_target_pairs={{0,64},{16,80},{32,96},{48,112},{64,0},{80,16},{96,32},{112,48},{1... | collective-permute-start | bytes 1179656 | tf_op jit(solution)/shard_map/ppermute | solution.py:23
  36.6 12.0 %collective-permute-start.15 = (f32[4,64,128]{2,1,0:T(8,128)S(1)}, f32[4,64,128]{2,1,0:T(8,128)S(1)}, u32[]{:S(2)}, u32[]{:S(2)}) collective-permute-start(f32[4,64,128]{2,1,0:T(8,128)S(1)} %get-tuple-element.50), channel_id=1, source_target_pairs={{0,16},{16,0},{32,48},{48,32},{64,80},{80,64},{96,112},{112,96},{1... | collective-permute-start | bytes 393224 | tf_op jit(solution)/shard_map/ppermute | solution.py:23
  39.3 13.7 %collective-permute-start.17 = (f32[4,64,128]{2,1,0:T(8,128)S(1)}, f32[4,64,128]{2,1,0:T(8,128)S(1)}, u32[]{:S(2)}, u32[]{:S(2)}) collective-permute-start(f32[4,64,128]{2,1,0:T(8,128)S(1)} %get-tuple-element.51), channel_id=1, source_target_pairs={{0,32},{16,48},{32,0},{48,16},{64,96},{80,112},{96,64},{112,80},{1... | collective-permute-start | bytes 393224 | tf_op jit(solution)/shard_map/ppermute | solution.py:23
  44.4 11.2 %collective-permute-start.16 = (f32[4,64,128]{2,1,0:T(8,128)S(1)}, f32[4,64,128]{2,1,0:T(8,128)S(1)}, u32[]{:S(2)}, u32[]{:S(2)}) collective-permute-start(f32[4,64,128]{2,1,0:T(8,128)S(1)} %get-tuple-element.52), channel_id=1, source_target_pairs={{0,48},{16,32},{32,16},{48,0},{64,112},{80,96},{96,80},{112,64},{1... | collective-permute-start | bytes 393224 | tf_op jit(solution)/shard_map/ppermute | solution.py:23
  44.4 16.6 %collective-permute-start.10 = (f32[8,32,384]{2,1,0:T(8,128)S(1)}, f32[8,32,384]{2,1,0:T(8,128)S(1)}, u32[]{:S(2)}, u32[]{:S(2)}) collective-permute-start(f32[8,32,384]{2,1,0:T(8,128)S(1)} %get-tuple-element.33), channel_id=1, source_target_pairs={{0,192},{16,208},{32,224},{48,240},{64,128},{80,144},{96,160},{112... | collective-permute-start | bytes 1179656 | tf_op jit(solution)/shard_map/ppermute | solution.py:23
  55.6 16.9 %collective-permute-start.19 = (f32[64,128]{1,0:T(8,128)S(1)}, f32[64,128]{1,0:T(8,128)S(1)}, u32[]{:S(2)}, u32[]{:S(2)}) collective-permute-start(f32[64,128]{1,0:T(8,128)S(1)} %get-tuple-element.47), channel_id=1, source_target_pairs={{0,192},{16,208},{32,224},{48,240},{64,128},{80,144},{96,160},{112... | collective-permute-start | bytes 98312 | tf_op jit(solution)/shard_map/ppermute | solution.py:23
  57.6 15.0 %collective-permute-start.20 = (f32[64,128]{1,0:T(8,128)S(1)}, f32[64,128]{1,0:T(8,128)S(1)}, u32[]{:S(2)}, u32[]{:S(2)}) collective-permute-start(f32[64,128]{1,0:T(8,128)S(1)} %get-tuple-element.48), channel_id=1, source_target_pairs={{0,128},{16,144},{32,160},{48,176},{64,192},{80,208},{96,224},{112... | collective-permute-start | bytes 98312 | tf_op jit(solution)/shard_map/ppermute | solution.py:23
  58.4 14.2 %collective-permute-start.18 = (f32[64,128]{1,0:T(8,128)S(1)}, f32[64,128]{1,0:T(8,128)S(1)}, u32[]{:S(2)}, u32[]{:S(2)}) collective-permute-start(f32[64,128]{1,0:T(8,128)S(1)} %get-tuple-element.49), channel_id=1, source_target_pairs={{0,64},{16,80},{32,96},{48,112},{64,0},{80,16},{96,32},{112,48},{1... | collective-permute-start | bytes 98312 | tf_op jit(solution)/shard_map/ppermute | solution.py:23
  59.0 6.5 %collective-permute-start.9 = (f32[4,32,384]{2,1,0:T(8,128)S(1)}, f32[4,32,384]{2,1,0:T(8,128)S(1)}, u32[]{:S(2)}, u32[]{:S(2)}) collective-permute-start(f32[4,32,384]{2,1,0:T(8,128)S(1)} %slice_add_fusion.1), channel_id=1, source_target_pairs={{0,192},{16,208},{32,224},{48,240},{64,128},{80,144},{96,160},{112... | collective-permute-start | bytes 589832 | tf_op jit(solution)/shard_map/ppermute | solution.py:23
  61.0 4.9 %collective-permute-start.11 = (f32[4,32,384]{2,1,0:T(8,128)S(1)}, f32[4,32,384]{2,1,0:T(8,128)S(1)}, u32[]{:S(2)}, u32[]{:S(2)}) collective-permute-start(f32[4,32,384]{2,1,0:T(8,128)S(1)} %slice_add_fusion), channel_id=1, source_target_pairs={{0,64},{16,80},{32,96},{48,112},{64,0},{80,16},{96,32},{112,48},{1... | collective-permute-start | bytes 589832 | tf_op jit(solution)/shard_map/ppermute | solution.py:23
  66.0 6.7 %collective-permute-start.12 = (f32[64,384]{1,0:T(8,128)S(1)}, f32[64,384]{1,0:T(8,128)S(1)}, u32[]{:S(2)}, u32[]{:S(2)}) collective-permute-start(f32[64,384]{1,0:T(8,128)S(1)} %pad_maximum_fusion.2), channel_id=1, source_target_pairs={{0,16},{16,0},{32,48},{48,32},{64,80},{80,64},{96,112},{112,96},{1... | collective-permute-start | bytes 294920 | tf_op jit(solution)/shard_map/ppermute | solution.py:23
  68.7 7.6 %collective-permute-start.14 = (f32[64,384]{1,0:T(8,128)S(1)}, f32[64,384]{1,0:T(8,128)S(1)}, u32[]{:S(2)}, u32[]{:S(2)}) collective-permute-start(f32[64,384]{1,0:T(8,128)S(1)} %pad_maximum_fusion.4), channel_id=1, source_target_pairs={{0,32},{16,48},{32,0},{48,16},{64,96},{80,112},{96,64},{112,80},{1... | collective-permute-start | bytes 294920 | tf_op jit(solution)/shard_map/ppermute | solution.py:23
  72.5 8.5 %collective-permute-start.13 = (f32[64,384]{1,0:T(8,128)S(1)}, f32[64,384]{1,0:T(8,128)S(1)}, u32[]{:S(2)}, u32[]{:S(2)}) collective-permute-start(f32[64,384]{1,0:T(8,128)S(1)} %pad_maximum_fusion.3), channel_id=1, source_target_pairs={{0,48},{16,32},{32,16},{48,0},{64,112},{80,96},{96,80},{112,64},{1... | collective-permute-start | bytes 294920 | tf_op jit(solution)/shard_map/ppermute | solution.py:23
  95.8 6.8 %collective-permute-start.28 = (f32[64,128]{1,0:T(8,128)S(1)}, f32[64,128]{1,0:T(8,128)S(1)}, u32[]{:S(2)}, u32[]{:S(2)}) collective-permute-start(f32[64,128]{1,0:T(8,128)S(1)} %add_add_fusion.1), channel_id=1, source_target_pairs={{0,32},{16,48},{32,0},{48,16},{64,96},{80,112},{96,64},{112,80},{1... | collective-permute-start | bytes 98312 | tf_op jit(solution)/shard_map/ppermute | solution.py:23
  99.6 5.4 %collective-permute-start.27 = (f32[64,128]{1,0:T(8,128)S(1)}, f32[64,128]{1,0:T(8,128)S(1)}, u32[]{:S(2)}, u32[]{:S(2)}) collective-permute-start(f32[64,128]{1,0:T(8,128)S(1)} %add_add_fusion.1), channel_id=1, source_target_pairs={{0,48},{16,32},{32,16},{48,0},{64,112},{80,96},{96,80},{112,64},{1... | collective-permute-start | bytes 98312 | tf_op jit(solution)/shard_map/ppermute | solution.py:23
  105.5 4.7 %collective-permute-start.31 = (f32[2,64,128]{2,1,0:T(8,128)S(1)}, f32[2,64,128]{2,1,0:T(8,128)S(1)}, u32[]{:S(2)}, u32[]{:S(2)}) collective-permute-start(f32[2,64,128]{2,1,0:T(8,128)S(1)} %get-tuple-element.56), channel_id=1, source_target_pairs={{0,128},{16,144},{32,160},{48,176},{64,192},{80,208},{96,224},{112... | collective-permute-start | bytes 196616 | tf_op jit(solution)/shard_map/ppermute | solution.py:23
  111.8 5.8 %collective-permute-start.33 = (f32[3,64,128]{2,1,0:T(8,128)S(1)}, f32[3,64,128]{2,1,0:T(8,128)S(1)}, u32[]{:S(2)}, u32[]{:S(2)}) collective-permute-start(f32[3,64,128]{2,1,0:T(8,128)S(1)} %pad_maximum_fusion.5), channel_id=1, source_target_pairs={{0,2},{2,0},{4,6},{6,4},{8,10},{10,8},{12,14},{14,12},{1,3},{3,1},... | collective-permute-start | bytes 294920 | tf_op jit(solution)/shard_map/ppermute | solution.py:23
  (10 other events, 34.3 us)

commit v3 on v1

--- a/solution.py
+++ b/solution.py
@@ -52,39 +52,53 @@
     return pl.CostEstimate(flops=flops, bytes_accessed=mib << 20, transcendentals=0)
 
 
-def scores_kernel(side, *refs):
-    if side:
-        res, load, out, rh, rl, lh, ll, later, rbuf, lbuf, acc, rsems, lsems, nsems = refs
+TURNS = ((1, (1, 2)), (0, (1, 2)), (1, (3, 0)), (0, (3, 0)))
+
+
+def scores_kernel(turn, *refs):
+    last = turn == len(TURNS) - 1
+    if turn == 0:
+        res, load, out, rh, rl, lh, ll, later, rbuf, lbuf, acc, nsems, rsems, lsems = refs
+    elif last:
+        rbuf, lh, ll, out, rh, rl, acc = refs
     else:
-        rbuf, lh, ll, out, rh, rl, acc = refs
+        rbuf, lh, ll, res, out, rh, rl, later, acc, nsems = refs
     me = lax.axis_index("coeffici")
-    core = me & 1
     size = out.shape[1]
     depth = lh.shape[0] // 4
+
+    def rows_of(turn, n):
+        side, places = TURNS[turn]
+        return at(me ^ side ^ (X * RING[places[n]]), size)
+
     copies, others = [[] for _ in range(4)], []
-    if side:
+    if not last:
+        for n in range(2):
+            others.append(
+                pltpu.make_async_copy(res.at[rows_of(turn + 1, n)], later.at[pl.ds(n * size, size)], nsems.at[n])
+            )
+    if turn == 0:
         for step in range(4):
             cols = slice(step * depth, (step + 1) * depth)
             copies[step].append(pltpu.make_async_copy(load.at[cols], lbuf.at[cols], lsems.at[step]))
-            for t in range(4):
+            for n in range(2):
                 copies[step].append(
                     pltpu.make_async_copy(
-                        res.at[at(2 * t + (core ^ 1), size), cols], rbuf.at[pl.ds(t * size, size), cols], rsems.at[step, t]
+                        res.at[rows_of(0, n), cols], rbuf.at[pl.ds(n * size, size), cols], rsems.at[step, n]
                     )
                 )
-        for t in range(4):
-            others.append(
-                pltpu.make_async_copy(res.at[at(2 * t + core, size)], later.at[pl.ds(t * size, size)], nsems.at[t])
-            )
         for copy in copies[0] + copies[1]:
+            copy.start()
+    else:
+        for copy in others:
             copy.start()
     for step in range(4):
         for copy in copies[step]:
             copy.wait()
-        for copy in (copies[2], copies[3] + others[:1], others[1:], ())[step] if side else ():
+        for copy in (copies[2], copies[3], others, ())[step] if turn == 0 else ():
             copy.start()
         cols = slice(step * depth, (step + 1) * depth)
-        if side:
+        if turn == 0:
             lh[cols], ll[cols] = split(lbuf[cols])
         high, low = split(rbuf[:, cols])
         rh[:, cols], rl[:, cols] = high, low
@@ -93,37 +107,34 @@
             acc[...] = term
         else:
             acc[...] += term
-    for t in range(4):
-        mask = (me ^ (2 * t + (core ^ side))) >> 1
-        out[mask ^ (mask >> 1)] = acc[t * size : (t + 1) * size]
+    for n in range(2):
+        out[n] = acc[n * size : (n + 1) * size]
     for copy in others:
         copy.wait()
 
 
-def scores(side, res, *load):
-    rows, coefs = res.shape
-    rows = rows if side else 2 * rows
-    k = load[0].shape[1]
-    operand = shape(rows // 2, coefs, dtype=BF16)
-    extra = (shape(coefs, k, dtype=BF16),) * 2 + (shape(rows // 2, coefs),)
-    acc = pltpu.VMEM((rows // 2, k), F32)
+def scores(turn, coefs, k, size, *args):
+    last = turn == len(TURNS) - 1
+    operand = shape(2 * size, coefs, dtype=BF16)
+    loads = (shape(coefs, k, dtype=BF16),) * 2 if turn == 0 else ()
     dma = pltpu.SemaphoreType.DMA
-    return pl.pallas_call(
-        functools.partial(scores_kernel, side),
-        out_shape=(shape(4, rows // 8, k), operand, operand) + (extra if side else ()),
-        in_specs=[HBM, HBM] if side else [VMEM] * 3,
-        out_specs=(VMEM,) * (6 if side else 3),
-        scratch_shapes=[pltpu.VMEM((rows // 2, coefs), F32), pltpu.VMEM((coefs, k), F32), acc, dma((4, 4)), dma((4,)), dma((4,))]
-        if side
-        else [acc],
-        compiler_params=params(20),
-        cost_estimate=cost(3 * rows * coefs * k, 6),
-        name="scores_far" if side else "scores_near",
-    )(res, *load)
+    scratch = [pltpu.VMEM((2 * size, k), F32)] + ([] if last else [dma((2,))])
+    if turn == 0:
+        scratch = [pltpu.VMEM((2 * size, coefs), F32), pltpu.VMEM((coefs, k), F32)] + scratch + [dma((4, 2)), dma((4,))]
+    outs = (shape(2, size, k), operand, operand) + loads + (() if last else (shape(2 * size, coefs),))
+    return pl.pallas_call(
+        functools.partial(scores_kernel, turn),
+        out_shape=outs,
+        in_specs=[HBM, HBM] if turn == 0 else [VMEM] * 3 + ([] if last else [HBM]),
+        out_specs=(VMEM,) * len(outs),
+        scratch_shapes=scratch,
+        compiler_params=params(16),
+        cost_estimate=cost(12 * size * coefs * k, 4),
+    )(*args)
 
 
 def own_kernel(near, got, r1, r2, r3, out):
-    out[...] = ((near[0] + got[0]) + (r1[...] + r2[...]) + r3[...]).T
+    out[...] = ((near[1] + got[1]) + (r1[...] + r2[...]) + r3[...]).T
 
 
 def own_block(*terms):
@@ -140,24 +151,24 @@
 
 
 def stage_kernel(*refs):
-    pieces, out = refs[:-1], refs[-1]
-    me = lax.axis_index("coeffici")
-    for n in range(4):
-        piece = pieces[n][...] if len(pieces) == 4 else pieces[0][n]
-        high, low = split(piece)
-        where = at((me ^ (X * RING[n])) >> 1, LANE)
-        for block in range(4):
-            rows = slice(64 * block, 64 * block + 64)
-            out[128 * block : 128 * block + 64, where] = high[rows]
-            out[128 * block + 64 : 128 * block + 128, where] = low[rows]
+    pieces, outs = refs[:-2], refs[-2:]
+    for out, places in zip(outs, ((1, 2), (3, 0))):
+        for n, spot in enumerate(places):
+            high, low = split(pieces[spot][...] if len(pieces) == 4 else pieces[0][spot])
+            where = slice(n * LANE, (n + 1) * LANE)
+            for block in range(4):
+                rows = slice(64 * block, 64 * block + 64)
+                out[128 * block : 128 * block + 64, where] = high[rows]
+                out[128 * block + 64 : 128 * block + 128, where] = low[rows]
 
 
 def stage(*pieces):
+    out = shape(4 * LANE, 2 * LANE, dtype=BF16)
     return pl.pallas_call(
         stage_kernel,
-        out_shape=shape(4 * LANE, 4 * LANE, dtype=BF16),
+        out_shape=(out, out),
         in_specs=[VMEM] * len(pieces),
-        out_specs=VMEM,
+        out_specs=(VMEM, VMEM),
         compiler_params=params(4),
         cost_estimate=cost(1 << 18, 1),
         name="stage",
@@ -212,7 +223,7 @@
 
 
 def third_kernel(*refs):
-    ops, out = refs[:6], refs[6]
+    ops, out = refs[:-1], refs[-1]
     particle = lax.axis_index("particle")
     y, z = particle >> 2, particle & 3
 
@@ -220,7 +231,8 @@
     def _(step):
         spots = [2 * step, 2 * step + 1]
         both = low = None
-        for st, rh, rl in (ops[:3], ops[3:]):
+        for side in range(len(ops) // 3):
+            st, rh, rl = ops[3 * side : 3 * side + 3]
             high, rest = columns((rh, rl), [3], [z ^ s ^ (s >> 1) for s in spots])
             left_high = jnp.concatenate([st[LANE * b : LANE * b + 64] for b in range(4)])
             first, second = dot(st[...], high), dot(left_high, rest)
@@ -240,10 +252,10 @@
     return pl.pallas_call(
         third_kernel,
         out_shape=shape(16, 64, LANE),
-        in_specs=[VMEM] * 6,
+        in_specs=[VMEM] * len(operands),
         out_specs=VMEM,
         compiler_params=params(16),
-        cost_estimate=cost(3 * rows * coefs * LANE, 4),
+        cost_estimate=cost(6 * rows * coefs * LANE, 4),
         name="covariance_third",
     )(*operands)
 
@@ -342,14 +354,23 @@
     res, load = (pltpu.with_memory_space_constraint(v[0], pltpu.HBM) for v in (residuals, loadings))
     factor = (res.shape[0] * lax.axis_size("particle")) ** -0.5
 
-    far, fh, fl, lh, ll, rest = scores(1, res, load)
-    got = swap(far, "coeffici", CORE)
-    near, nh, nl = scores(0, rest, lh, ll)
-    own = own_block(near, got, *ring_swap([near[n] + got[n] for n in (1, 2, 3)], "coeffici", X))
+    sizes = (res.shape[1], load.shape[1], res.shape[0] // 8)
+    far_a, fh_a, fl_a, lh, ll, rest = scores(0, *sizes, res, load)
+    got_a = swap(far_a, "coeffici", CORE)
+    near_a, nh_a, nl_a, rest = scores(1, *sizes, rest, lh, ll, res)
+    r1 = swap(near_a[0] + got_a[0], "coeffici", X * RING[1])
+    r2 = swap(near_a[1] + got_a[1], "coeffici", X * RING[2])
+    far_b, fh_b, fl_b, rest = scores(2, *sizes, rest, lh, ll, res)
+    got_b = swap(far_b, "coeffici", CORE)
+    near_b, nh_b, nl_b = scores(3, *sizes, rest, lh, ll)
+    r3 = swap(near_b[0] + got_b[0], "coeffici", X * RING[3])
+    own = own_block(near_b, got_b, r1, r2, r3)
     pieces = [own] + ring_swap([own] * 3, "coeffici", X)
     others = swap(jnp.stack(pieces), "coeffici", CORE)
-    near_ops = (stage(*pieces), nh, nl)
-    far_ops = (stage(others), fh, fl)
+    st_a, st_b = stage(*pieces)
+    near_ops = (st_a, nh_a, nl_a, st_b, nh_b, nl_b)
+    st_a, st_b = stage(others)
+    far_ops = (st_a, fh_a, fl_a, st_b, fh_b, fl_b)
 
     leave = covariance_pair((2, 3), near_ops, ())
     leave_p, leave_q = covariance_pair((2, 3), far_ops, leave)

time: 119 us -> 121 us (1.017)
  Pallas kernels: 16 us -> 18.5 us
  waiting for transfers between devices: 48.2 us -> 45.7 us
  starting transfers between devices: 52.9 us -> 54.8 us
    pallas_call x4 -> x6, Pallas kernels: 7.9 us -> 10.5 us  [the longest x4 10.3 us: scores(): pl.pallas_call(functools.partial(scores_kernel, turn), out_shape=outs, in...]
    ppermute x34 -> x35, waiting for transfers between devices: 48.2 us -> 45.7 us  [swap(): lax.ppermute(value, axis, [(s, s ^ mask) for s in range(lax.axis_size(axi...]
    ppermute x34 -> x35, starting transfers between devices: 52.9 us -> 54.8 us  [swap(): lax.ppermute(value, axis, [(s, s ^ mask) for s in range(lax.axis_size(axi...]
  transfers between devices with their start and end apart: 34 -> 35, of which waited for: 22 -> 21; matrix products, arithmetic and copies ran while one was open for 0% -> 0% of each run, Pallas kernels for 5% -> 9%
where the time goes in v3:
time: 121 us; the launch traced here: 120 us
  starting transfers between devices  54.8 us (45%)
  waiting for transfers between devices  45.7 us (38%)
  Pallas kernels  18.5 us (15%)
    ppermute x35, starting transfers between devices, swap(): lax.ppermute(value, axis, [(s, s ^ mask) for s in range(lax.axis_size(axi...  54.8 us
    ppermute x35, waiting for transfers between devices, swap(): lax.ppermute(value, axis, [(s, s ^ mask) for s in range(lax.axis_size(axi...  45.7 us
    pallas_call x4, Pallas kernels, scores(): pl.pallas_call(functools.partial(scores_kernel, turn), out_shape=outs, in...  10.3 us
    pallas_call x3, Pallas kernels, covariance_pair(): pl.pallas_call(functools.partial(pair_kernel, places, sides, len(before)...  4.68 us
  transfers between devices with their start and end apart: 35, of which 21 were waited for; matrix products, arithmetic and copies ran while one was open for 0% of the time, Pallas kernels for 9%

profile of v3, /device:TPU:1, one launch (start us, length us, event | category | flops | bytes accessed | tf_op | source)
XLA Modules:
  0.0 120.3 jit_solution(14000848183697483532)
XLA Ops:
  0.6 4.3 %shard_map.41 = (f32[2,128,256]{2,1,0:T(8,128)S(1)}, bf16[256,2048]{1,0:T(8,128)(2,1)S(1)}, bf16[256,2048]{1,0:T(8,128)(2,1)S(1)}, bf16[2048,256]{1,0:T(8,128)(2...) custom-call(f32[1024,2048]{1,0:T(8,128)} %bitcast.52, f32[2048,256]{1,0:T(8,128)} %bitcast.55), custom_call_target="tpu_custom_call" | custom-call | flops 805306368 | bytes 4194304 | tf_op jit(solution)/shard_map/pallas_call | solution.py:125
  5.0 3.3 %collective-permute-start.1 = (f32[2,128,256]{2,1,0:T(8,128)S(1)}, f32[2,128,256]{2,1,0:T(8,128)S(1)}, u32[]{:S(2)}, u32[]{:S(2)}) collective-permute-start(f32[2,128,256]{2,1,0:T(8,128)S(1)} %get-tuple-element.39), channel_id=1, source_target_pairs={{0,2},{2,0},{4,6},{6,4},{8,10},{10,8},{12,14},{14,12},{1,3},{3,1},... | collective-permute-start | bytes 786440 | tf_op jit(solution)/shard_map/ppermute | solution.py:23
  8.2 2.4 %shard_map.42 = (f32[2,128,256]{2,1,0:T(8,128)S(1)}, bf16[256,2048]{1,0:T(8,128)(2,1)S(1)}, bf16[256,2048]{1,0:T(8,128)(2,1)S(1)}, f32[256,2048]{1,0:T(8,128)S(1)}) custom-call(f32[256,2048]{1,0:T(8,128)S(1)} %get-tuple-element.33.refs_0_, bf16[2048,256]{1,0:T(8,128)(2,1)S(1)} %get-tuple-element.31.refs_1_.load_h, ...), custom_call_target="tpu_custom_call" | custom-call | flops 805306368 | bytes 4194304 | tf_op jit(solution)/shard_map/pallas_call | solution.py:125
  10.7 2.4 %shard_map.43 = (f32[2,128,256]{2,1,0:T(8,128)S(1)}, bf16[256,2048]{1,0:T(8,128)(2,1)S(1)}, bf16[256,2048]{1,0:T(8,128)(2,1)S(1)}, f32[256,2048]{1,0:T(8,128)S(1)}) custom-call(f32[256,2048]{1,0:T(8,128)S(1)} %get-tuple-element.34.refs_0_, bf16[2048,256]{1,0:T(8,128)(2,1)S(1)} %get-tuple-element.31.refs_1_.load_h, ...), custom_call_target="tpu_custom_call" | custom-call | flops 805306368 | bytes 4194304 | tf_op jit(solution)/shard_map/pallas_call | solution.py:125
  15.3 3.2 %collective-permute-start.4 = (f32[128,256]{1,0:T(8,128)S(1)}, f32[128,256]{1,0:T(8,128)S(1)}, u32[]{:S(2)}, u32[]{:S(2)}) collective-permute-start(f32[128,256]{1,0:T(8,128)S(1)} %fusion), channel_id=1, source_target_pairs={{0,8},{2,10},{4,12},{6,14},{8,0},{10,2},{12,4},{14,6},{1,9},{3,11}... | collective-permute-start | bytes 393224 | tf_op jit(solution)/shard_map/ppermute | solution.py:23
  20.2 3.7 %collective-permute-done.4.r3 = f32[128,256]{1,0:T(8,128)S(1)} collective-permute-done((f32[128,256]{1,0:T(8,128)S(1)}, f32[128,256]{1,0:T(8,128)S(1)}, u32[]{:S(2)}, u32[]{:S(2)}) %collective-permute-start.4) | collective-permute-done | bytes 131104 | tf_op jit(solution)/shard_map/ppermute | solution.py:23
  24.2 2.2 %collective-permute-start.6 = (f32[256,128]{1,0:T(8,128)S(1)}, f32[256,128]{1,0:T(8,128)S(1)}, u32[]{:S(2)}, u32[]{:S(2)}) collective-permute-start(f32[256,128]{1,0:T(8,128)S(1)} %own_block.1.refs_0_), channel_id=1, source_target_pairs={{0,12},{2,14},{4,8},{6,10},{8,4},{10,6},{12,0},{14,2},{1,13},{3,15... | collective-permute-start | bytes 393224 | tf_op jit(solution)/shard_map/ppermute | solution.py:23
  26.8 2.8 %collective-permute-done.7.refs_3_ = f32[256,128]{1,0:T(8,128)S(1)} collective-permute-done((f32[256,128]{1,0:T(8,128)S(1)}, f32[256,128]{1,0:T(8,128)S(1)}, u32[]{:S(2)}, u32[]{:S(2)}) %collective-permute-start.7) | collective-permute-done | bytes 131104 | tf_op jit(solution)/shard_map/ppermute | solution.py:23
  29.6 3.1 %collective-permute-done.6.refs_2_ = f32[256,128]{1,0:T(8,128)S(1)} collective-permute-done((f32[256,128]{1,0:T(8,128)S(1)}, f32[256,128]{1,0:T(8,128)S(1)}, u32[]{:S(2)}, u32[]{:S(2)}) %collective-permute-start.6) | collective-permute-done | bytes 131104 | tf_op jit(solution)/shard_map/ppermute | solution.py:23
  38.7 3.1 %collective-permute-start.16 = (f32[4,64,128]{2,1,0:T(8,128)S(1)}, f32[4,64,128]{2,1,0:T(8,128)S(1)}, u32[]{:S(2)}, u32[]{:S(2)}) collective-permute-start(f32[4,64,128]{2,1,0:T(8,128)S(1)} %get-tuple-element.71), channel_id=1, source_target_pairs={{0,16},{16,0},{32,48},{48,32},{64,80},{80,64},{96,112},{112,96},{1... | collective-permute-start | bytes 393224 | tf_op jit(solution)/shard_map/ppermute | solution.py:23
  41.8 5.1 %collective-permute-start.18 = (f32[4,64,128]{2,1,0:T(8,128)S(1)}, f32[4,64,128]{2,1,0:T(8,128)S(1)}, u32[]{:S(2)}, u32[]{:S(2)}) collective-permute-start(f32[4,64,128]{2,1,0:T(8,128)S(1)} %get-tuple-element.72), channel_id=1, source_target_pairs={{0,32},{16,48},{32,0},{48,16},{64,96},{80,112},{96,64},{112,80},{1... | collective-permute-start | bytes 393224 | tf_op jit(solution)/shard_map/ppermute | solution.py:23
  48.8 2.2 %shard_map.45 = (f32[8,32,384]{2,1,0:T(8,128)S(1)}, f32[8,32,384]{2,1,0:T(8,128)S(1)}) custom-call(bf16[512,256]{1,0:T(8,128)(2,1)S(1)} %get-tuple-element.40.refs_0_, bf16[256,2048]{1,0:T(8,128)(2,1)S(1)} %get-tuple-element.41.refs_1_, bf16[256,2048]{1,0:T(8,128)(2,1)S(1)} %get-tuple-element.42.refs_2_, bf16[512,256]{1,0:T(8,128)(2,1)S(1)} %get-tuple-element.43.refs_3_, ...), custom_call_target="tpu_custom_call" | custom-call | flops 805306368 | bytes 4194304 | tf_op jit(solution)/shard_map/pallas_call | solution.py:215
  51.1 4.6 %collective-permute-done.18 = f32[4,64,128]{2,1,0:T(8,128)S(1)} collective-permute-done((f32[4,64,128]{2,1,0:T(8,128)S(1)}, f32[4,64,128]{2,1,0:T(8,128)S(1)}, u32[]{:S(2)}, u32[]{:S(2)}) %collective-permute-start.18) | collective-permute-done | bytes 131104 | tf_op jit(solution)/shard_map/ppermute | solution.py:23
  55.7 2.4 %collective-permute-done.17 = f32[4,64,128]{2,1,0:T(8,128)S(1)} collective-permute-done((f32[4,64,128]{2,1,0:T(8,128)S(1)}, f32[4,64,128]{2,1,0:T(8,128)S(1)}, u32[]{:S(2)}, u32[]{:S(2)}) %collective-permute-start.17) | collective-permute-done | bytes 131104 | tf_op jit(solution)/shard_map/ppermute | solution.py:23
  64.0 4.0 %collective-permute-done.10 = f32[4,32,384]{2,1,0:T(8,128)S(1)} collective-permute-done((f32[4,32,384]{2,1,0:T(8,128)S(1)}, f32[4,32,384]{2,1,0:T(8,128)S(1)}, u32[]{:S(2)}, u32[]{:S(2)}) %collective-permute-start.10) | collective-permute-done | bytes 196640 | tf_op jit(solution)/shard_map/ppermute | solution.py:23
  68.5 2.8 %collective-permute-start.13 = (f32[64,384]{1,0:T(8,128)S(1)}, f32[64,384]{1,0:T(8,128)S(1)}, u32[]{:S(2)}, u32[]{:S(2)}) collective-permute-start(f32[64,384]{1,0:T(8,128)S(1)} %pad_maximum_fusion.2), channel_id=1, source_target_pairs={{0,16},{16,0},{32,48},{48,32},{64,80},{80,64},{96,112},{112,96},{1... | collective-permute-start | bytes 294920 | tf_op jit(solution)/shard_map/ppermute | solution.py:23
  71.3 3.8 %collective-permute-start.15 = (f32[64,384]{1,0:T(8,128)S(1)}, f32[64,384]{1,0:T(8,128)S(1)}, u32[]{:S(2)}, u32[]{:S(2)}) collective-permute-start(f32[64,384]{1,0:T(8,128)S(1)} %pad_maximum_fusion.4), channel_id=1, source_target_pairs={{0,32},{16,48},{32,0},{48,16},{64,96},{80,112},{96,64},{112,80},{1... | collective-permute-start | bytes 294920 | tf_op jit(solution)/shard_map/ppermute | solution.py:23
  75.2 3.7 %collective-permute-done.15 = f32[64,384]{1,0:T(8,128)S(1)} collective-permute-done((f32[64,384]{1,0:T(8,128)S(1)}, f32[64,384]{1,0:T(8,128)S(1)}, u32[]{:S(2)}, u32[]{:S(2)}) %collective-permute-start.15) | collective-permute-done | bytes 98336 | tf_op jit(solution)/shard_map/ppermute | solution.py:23
  78.9 4.9 %collective-permute-done.14 = f32[64,384]{1,0:T(8,128)S(1)} collective-permute-done((f32[64,384]{1,0:T(8,128)S(1)}, f32[64,384]{1,0:T(8,128)S(1)}, u32[]{:S(2)}, u32[]{:S(2)}) %collective-permute-start.14) | collective-permute-done | bytes 98336 | tf_op jit(solution)/shard_map/ppermute | solution.py:23
  84.9 2.9 %collective-permute-done.22.other = f32[64,512]{1,0:T(8,128)S(1)} collective-permute-done((f32[64,512]{1,0:T(8,128)S(1)}, f32[64,512]{1,0:T(8,128)S(1)}, u32[]{:S(2)}, u32[]{:S(2)}) %collective-permute-start.22) | collective-permute-done | bytes 131104 | tf_op jit(solution)/shard_map/ppermute | solution.py:23
  88.0 2.9 %collective-permute-start.23 = (f32[64,128]{1,0:T(8,128)S(1)}, f32[64,128]{1,0:T(8,128)S(1)}, u32[]{:S(2)}, u32[]{:S(2)}) collective-permute-start(f32[64,128]{1,0:T(8,128)S(1)} %slice_bitcast_fusion), channel_id=1, source_target_pairs={{0,2},{2,0},{4,6},{6,4},{8,10},{10,8},{12,14},{14,12},{1,3},{3,1},... | collective-permute-start | bytes 98312 | tf_op jit(solution)/shard_map/ppermute | solution.py:23
  97.4 3.6 %collective-permute-start.29 = (f32[64,128]{1,0:T(8,128)S(1)}, f32[64,128]{1,0:T(8,128)S(1)}, u32[]{:S(2)}, u32[]{:S(2)}) collective-permute-start(f32[64,128]{1,0:T(8,128)S(1)} %add_add_fusion.1), channel_id=1, source_target_pairs={{0,32},{16,48},{32,0},{48,16},{64,96},{80,112},{96,64},{112,80},{1... | collective-permute-start | bytes 98312 | tf_op jit(solution)/shard_map/ppermute | solution.py:23
  107.1 2.1 %collective-permute-start.32 = (f32[2,64,128]{2,1,0:T(8,128)S(1)}, f32[2,64,128]{2,1,0:T(8,128)S(1)}, u32[]{:S(2)}, u32[]{:S(2)}) collective-permute-start(f32[2,64,128]{2,1,0:T(8,128)S(1)} %get-tuple-element.79), channel_id=1, source_target_pairs={{0,128},{16,144},{32,160},{48,176},{64,192},{80,208},{96,224},{112... | collective-permute-start | bytes 196616 | tf_op jit(solution)/shard_map/ppermute | solution.py:23
  113.5 4.7 %collective-permute-start.34 = (f32[3,64,128]{2,1,0:T(8,128)S(1)}, f32[3,64,128]{2,1,0:T(8,128)S(1)}, u32[]{:S(2)}, u32[]{:S(2)}) collective-permute-start(f32[3,64,128]{2,1,0:T(8,128)S(1)} %pad_maximum_fusion.5), channel_id=1, source_target_pairs={{0,2},{2,0},{4,6},{6,4},{8,10},{10,8},{12,14},{14,12},{1,3},{3,1},... | collective-permute-start | bytes 294920 | tf_op jit(solution)/shard_map/ppermute | solution.py:23
  (85 shorter events, 39.2 us)
Async XLA Ops:
  5.0 9.4 %collective-permute-start.1 = (f32[2,128,256]{2,1,0:T(8,128)S(1)}, f32[2,128,256]{2,1,0:T(8,128)S(1)}, u32[]{:S(2)}, u32[]{:S(2)}) collective-permute-start(f32[2,128,256]{2,1,0:T(8,128)S(1)} %get-tuple-element.39), channel_id=1, source_target_pairs={{0,2},{2,0},{4,6},{6,4},{8,10},{10,8},{12,14},{14,12},{1,3},{3,1},... | collective-permute-start | bytes 786440 | tf_op jit(solution)/shard_map/ppermute | solution.py:23
  14.4 5.9 %collective-permute-start.3 = (f32[128,256]{1,0:T(8,128)S(1)}, f32[128,256]{1,0:T(8,128)S(1)}, u32[]{:S(2)}, u32[]{:S(2)}) collective-permute-start(f32[128,256]{1,0:T(8,128)S(1)} %get-tuple-element.74), channel_id=1, source_target_pairs={{0,12},{2,14},{4,8},{6,10},{8,4},{10,6},{12,0},{14,2},{1,13},{3,15... | collective-permute-start | bytes 393224 | tf_op jit(solution)/shard_map/ppermute | solution.py:23
  15.2 5.0 %collective-permute-start.2 = (f32[128,256]{1,0:T(8,128)S(1)}, f32[128,256]{1,0:T(8,128)S(1)}, u32[]{:S(2)}, u32[]{:S(2)}) collective-permute-start(f32[128,256]{1,0:T(8,128)S(1)} %get-tuple-element.75), channel_id=1, source_target_pairs={{0,4},{2,6},{4,0},{6,2},{8,12},{10,14},{12,8},{14,10},{1,5},{3,7},... | collective-permute-start | bytes 393224 | tf_op jit(solution)/shard_map/ppermute | solution.py:23
  15.3 8.7 %collective-permute-start.4 = (f32[128,256]{1,0:T(8,128)S(1)}, f32[128,256]{1,0:T(8,128)S(1)}, u32[]{:S(2)}, u32[]{:S(2)}) collective-permute-start(f32[128,256]{1,0:T(8,128)S(1)} %fusion), channel_id=1, source_target_pairs={{0,8},{2,10},{4,12},{6,14},{8,0},{10,2},{12,4},{14,6},{1,9},{3,11}... | collective-permute-start | bytes 393224 | tf_op jit(solution)/shard_map/ppermute | solution.py:23
  24.1 5.5 %collective-permute-start.7 = (f32[256,128]{1,0:T(8,128)S(1)}, f32[256,128]{1,0:T(8,128)S(1)}, u32[]{:S(2)}, u32[]{:S(2)}) collective-permute-start(f32[256,128]{1,0:T(8,128)S(1)} %own_block.1.refs_0_), channel_id=1, source_target_pairs={{0,8},{2,10},{4,12},{6,14},{8,0},{10,2},{12,4},{14,6},{1,9},{3,11}... | collective-permute-start | bytes 393224 | tf_op jit(solution)/shard_map/ppermute | solution.py:23
  24.2 8.6 %collective-permute-start.6 = (f32[256,128]{1,0:T(8,128)S(1)}, f32[256,128]{1,0:T(8,128)S(1)}, u32[]{:S(2)}, u32[]{:S(2)}) collective-permute-start(f32[256,128]{1,0:T(8,128)S(1)} %own_block.1.refs_0_), channel_id=1, source_target_pairs={{0,12},{2,14},{4,8},{6,10},{8,4},{10,6},{12,0},{14,2},{1,13},{3,15... | collective-permute-start | bytes 393224 | tf_op jit(solution)/shard_map/ppermute | solution.py:23
  26.4 6.3 %collective-permute-start.5 = (f32[256,128]{1,0:T(8,128)S(1)}, f32[256,128]{1,0:T(8,128)S(1)}, u32[]{:S(2)}, u32[]{:S(2)}) collective-permute-start(f32[256,128]{1,0:T(8,128)S(1)} %own_block.1.refs_0_), channel_id=1, source_target_pairs={{0,4},{2,6},{4,0},{6,2},{8,12},{10,14},{12,8},{14,10},{1,5},{3,7},... | collective-permute-start | bytes 393224 | tf_op jit(solution)/shard_map/ppermute | solution.py:23
  38.5 23.0 %collective-permute-start.9 = (f32[8,32,384]{2,1,0:T(8,128)S(1)}, f32[8,32,384]{2,1,0:T(8,128)S(1)}, u32[]{:S(2)}, u32[]{:S(2)}) collective-permute-start(f32[8,32,384]{2,1,0:T(8,128)S(1)} %get-tuple-element.55), channel_id=1, source_target_pairs={{0,64},{16,80},{32,96},{48,112},{64,0},{80,16},{96,32},{112,48},{1... | collective-permute-start | bytes 1179656 | tf_op jit(solution)/shard_map/ppermute | solution.py:23
  38.7 12.4 %collective-permute-start.16 = (f32[4,64,128]{2,1,0:T(8,128)S(1)}, f32[4,64,128]{2,1,0:T(8,128)S(1)}, u32[]{:S(2)}, u32[]{:S(2)}) collective-permute-start(f32[4,64,128]{2,1,0:T(8,128)S(1)} %get-tuple-element.71), channel_id=1, source_target_pairs={{0,16},{16,0},{32,48},{48,32},{64,80},{80,64},{96,112},{112,96},{1... | collective-permute-start | bytes 393224 | tf_op jit(solution)/shard_map/ppermute | solution.py:23
  41.8 13.9 %collective-permute-start.18 = (f32[4,64,128]{2,1,0:T(8,128)S(1)}, f32[4,64,128]{2,1,0:T(8,128)S(1)}, u32[]{:S(2)}, u32[]{:S(2)}) collective-permute-start(f32[4,64,128]{2,1,0:T(8,128)S(1)} %get-tuple-element.72), channel_id=1, source_target_pairs={{0,32},{16,48},{32,0},{48,16},{64,96},{80,112},{96,64},{112,80},{1... | collective-permute-start | bytes 393224 | tf_op jit(solution)/shard_map/ppermute | solution.py:23
  46.9 11.2 %collective-permute-start.17 = (f32[4,64,128]{2,1,0:T(8,128)S(1)}, f32[4,64,128]{2,1,0:T(8,128)S(1)}, u32[]{:S(2)}, u32[]{:S(2)}) collective-permute-start(f32[4,64,128]{2,1,0:T(8,128)S(1)} %get-tuple-element.73), channel_id=1, source_target_pairs={{0,48},{16,32},{32,16},{48,0},{64,112},{80,96},{96,80},{112,64},{1... | collective-permute-start | bytes 393224 | tf_op jit(solution)/shard_map/ppermute | solution.py:23
  46.9 16.6 %collective-permute-start.11 = (f32[8,32,384]{2,1,0:T(8,128)S(1)}, f32[8,32,384]{2,1,0:T(8,128)S(1)}, u32[]{:S(2)}, u32[]{:S(2)}) collective-permute-start(f32[8,32,384]{2,1,0:T(8,128)S(1)} %get-tuple-element.57), channel_id=1, source_target_pairs={{0,192},{16,208},{32,224},{48,240},{64,128},{80,144},{96,160},{112... | collective-permute-start | bytes 1179656 | tf_op jit(solution)/shard_map/ppermute | solution.py:23
  58.1 16.9 %collective-permute-start.20 = (f32[64,128]{1,0:T(8,128)S(1)}, f32[64,128]{1,0:T(8,128)S(1)}, u32[]{:S(2)}, u32[]{:S(2)}) collective-permute-start(f32[64,128]{1,0:T(8,128)S(1)} %get-tuple-element.68), channel_id=1, source_target_pairs={{0,192},{16,208},{32,224},{48,240},{64,128},{80,144},{96,160},{112... | collective-permute-start | bytes 98312 | tf_op jit(solution)/shard_map/ppermute | solution.py:23
  60.1 15.0 %collective-permute-start.21 = (f32[64,128]{1,0:T(8,128)S(1)}, f32[64,128]{1,0:T(8,128)S(1)}, u32[]{:S(2)}, u32[]{:S(2)}) collective-permute-start(f32[64,128]{1,0:T(8,128)S(1)} %get-tuple-element.69), channel_id=1, source_target_pairs={{0,128},{16,144},{32,160},{48,176},{64,192},{80,208},{96,224},{112... | collective-permute-start | bytes 98312 | tf_op jit(solution)/shard_map/ppermute | solution.py:23
  61.0 14.2 %collective-permute-start.19 = (f32[64,128]{1,0:T(8,128)S(1)}, f32[64,128]{1,0:T(8,128)S(1)}, u32[]{:S(2)}, u32[]{:S(2)}) collective-permute-start(f32[64,128]{1,0:T(8,128)S(1)} %get-tuple-element.70), channel_id=1, source_target_pairs={{0,64},{16,80},{32,96},{48,112},{64,0},{80,16},{96,32},{112,48},{1... | collective-permute-start | bytes 98312 | tf_op jit(solution)/shard_map/ppermute | solution.py:23
  61.5 6.5 %collective-permute-start.10 = (f32[4,32,384]{2,1,0:T(8,128)S(1)}, f32[4,32,384]{2,1,0:T(8,128)S(1)}, u32[]{:S(2)}, u32[]{:S(2)}) collective-permute-start(f32[4,32,384]{2,1,0:T(8,128)S(1)} %slice_add_fusion.1), channel_id=1, source_target_pairs={{0,192},{16,208},{32,224},{48,240},{64,128},{80,144},{96,160},{112... | collective-permute-start | bytes 589832 | tf_op jit(solution)/shard_map/ppermute | solution.py:23
  63.5 4.9 %collective-permute-start.12 = (f32[4,32,384]{2,1,0:T(8,128)S(1)}, f32[4,32,384]{2,1,0:T(8,128)S(1)}, u32[]{:S(2)}, u32[]{:S(2)}) collective-permute-start(f32[4,32,384]{2,1,0:T(8,128)S(1)} %slice_add_fusion), channel_id=1, source_target_pairs={{0,64},{16,80},{32,96},{48,112},{64,0},{80,16},{96,32},{112,48},{1... | collective-permute-start | bytes 589832 | tf_op jit(solution)/shard_map/ppermute | solution.py:23
  68.5 6.7 %collective-permute-start.13 = (f32[64,384]{1,0:T(8,128)S(1)}, f32[64,384]{1,0:T(8,128)S(1)}, u32[]{:S(2)}, u32[]{:S(2)}) collective-permute-start(f32[64,384]{1,0:T(8,128)S(1)} %pad_maximum_fusion.2), channel_id=1, source_target_pairs={{0,16},{16,0},{32,48},{48,32},{64,80},{80,64},{96,112},{112,96},{1... | collective-permute-start | bytes 294920 | tf_op jit(solution)/shard_map/ppermute | solution.py:23
  71.3 7.6 %collective-permute-start.15 = (f32[64,384]{1,0:T(8,128)S(1)}, f32[64,384]{1,0:T(8,128)S(1)}, u32[]{:S(2)}, u32[]{:S(2)}) collective-permute-start(f32[64,384]{1,0:T(8,128)S(1)} %pad_maximum_fusion.4), channel_id=1, source_target_pairs={{0,32},{16,48},{32,0},{48,16},{64,96},{80,112},{96,64},{112,80},{1... | collective-permute-start | bytes 294920 | tf_op jit(solution)/shard_map/ppermute | solution.py:23
  75.1 8.7 %collective-permute-start.14 = (f32[64,384]{1,0:T(8,128)S(1)}, f32[64,384]{1,0:T(8,128)S(1)}, u32[]{:S(2)}, u32[]{:S(2)}) collective-permute-start(f32[64,384]{1,0:T(8,128)S(1)} %pad_maximum_fusion.3), channel_id=1, source_target_pairs={{0,48},{16,32},{32,16},{48,0},{64,112},{80,96},{96,80},{112,64},{1... | collective-permute-start | bytes 294920 | tf_op jit(solution)/shard_map/ppermute | solution.py:23
  97.4 6.8 %collective-permute-start.29 = (f32[64,128]{1,0:T(8,128)S(1)}, f32[64,128]{1,0:T(8,128)S(1)}, u32[]{:S(2)}, u32[]{:S(2)}) collective-permute-start(f32[64,128]{1,0:T(8,128)S(1)} %add_add_fusion.1), channel_id=1, source_target_pairs={{0,32},{16,48},{32,0},{48,16},{64,96},{80,112},{96,64},{112,80},{1... | collective-permute-start | bytes 98312 | tf_op jit(solution)/shard_map/ppermute | solution.py:23
  101.0 5.2 %collective-permute-start.28 = (f32[64,128]{1,0:T(8,128)S(1)}, f32[64,128]{1,0:T(8,128)S(1)}, u32[]{:S(2)}, u32[]{:S(2)}) collective-permute-start(f32[64,128]{1,0:T(8,128)S(1)} %add_add_fusion.1), channel_id=1, source_target_pairs={{0,48},{16,32},{32,16},{48,0},{64,112},{80,96},{96,80},{112,64},{1... | collective-permute-start | bytes 98312 | tf_op jit(solution)/shard_map/ppermute | solution.py:23
  107.1 4.9 %collective-permute-start.32 = (f32[2,64,128]{2,1,0:T(8,128)S(1)}, f32[2,64,128]{2,1,0:T(8,128)S(1)}, u32[]{:S(2)}, u32[]{:S(2)}) collective-permute-start(f32[2,64,128]{2,1,0:T(8,128)S(1)} %get-tuple-element.79), channel_id=1, source_target_pairs={{0,128},{16,144},{32,160},{48,176},{64,192},{80,208},{96,224},{112... | collective-permute-start | bytes 196616 | tf_op jit(solution)/shard_map/ppermute | solution.py:23
  113.5 5.9 %collective-permute-start.34 = (f32[3,64,128]{2,1,0:T(8,128)S(1)}, f32[3,64,128]{2,1,0:T(8,128)S(1)}, u32[]{:S(2)}, u32[]{:S(2)}) collective-permute-start(f32[3,64,128]{2,1,0:T(8,128)S(1)} %pad_maximum_fusion.5), channel_id=1, source_target_pairs={{0,2},{2,0},{4,6},{6,4},{8,10},{10,8},{12,14},{14,12},{1,3},{3,1},... | collective-permute-start | bytes 294920 | tf_op jit(solution)/shard_map/ppermute | solution.py:23
  (11 other events, 37.1 us)

commit v4 on v2

--- a/solution.py
+++ b/solution.py
@@ -58,7 +58,6 @@
     else:
         rbuf, lh, ll, out, rh, rl, acc = refs
     me = lax.axis_index("coeffici")
-    core = me & 1
     size = out.shape[1]
     depth = lh.shape[0] // 4
     copies, others = [[] for _ in range(4)], []
@@ -69,19 +68,19 @@
             for t in range(4):
                 copies[step].append(
                     pltpu.make_async_copy(
-                        res.at[at(2 * t + (core ^ 1), size), cols], rbuf.at[pl.ds(t * size, size), cols], rsems.at[step, t]
+                        res.at[at(me ^ 1 ^ (X * RING[t]), size), cols], rbuf.at[pl.ds(t * size, size), cols], rsems.at[step, t]
                     )
                 )
         for t in range(4):
             others.append(
-                pltpu.make_async_copy(res.at[at(2 * t + core, size)], later.at[pl.ds(t * size, size)], nsems.at[t])
+                pltpu.make_async_copy(res.at[at(me ^ (X * RING[t]), size)], later.at[pl.ds(t * size, size)], nsems.at[t])
             )
-        for copy in copies[0] + copies[1] + copies[2]:
+        for copy in copies[0] + copies[1]:
             copy.start()
     for step in range(4):
         for copy in copies[step]:
             copy.wait()
-        for copy in (copies[3] + others[:1], others[1:], (), ())[step] if side else ():
+        for copy in (copies[2], copies[3] + others[:1], others[1:], ())[step] if side else ():
             copy.start()
         cols = slice(step * depth, (step + 1) * depth)
         if side:
@@ -94,8 +93,7 @@
         else:
             acc[...] += term
     for t in range(4):
-        mask = (me ^ (2 * t + (core ^ side))) >> 1
-        out[mask ^ (mask >> 1)] = acc[t * size : (t + 1) * size]
+        out[t] = acc[t * size : (t + 1) * size]
     for copy in others:
         copy.wait()
 
@@ -141,11 +139,9 @@
 
 def stage_kernel(*refs):
     pieces, out = refs[:-1], refs[-1]
-    me = lax.axis_index("coeffici")
-    for n in range(4):
-        piece = pieces[n][...] if len(pieces) == 4 else pieces[0][n]
-        high, low = split(piece)
-        where = at((me ^ (X * RING[n])) >> 1, LANE)
+    for n in range(2):
+        high, low = split(pieces[n][...] if len(pieces) == 2 else pieces[0][n])
+        where = slice(n * LANE, (n + 1) * LANE)
         for block in range(4):
             rows = slice(64 * block, 64 * block + 64)
             out[128 * block : 128 * block + 64, where] = high[rows]
@@ -155,7 +151,7 @@
 def stage(*pieces):
     return pl.pallas_call(
         stage_kernel,
-        out_shape=shape(4 * LANE, 4 * LANE, dtype=BF16),
+        out_shape=shape(4 * LANE, 2 * LANE, dtype=BF16),
         in_specs=[VMEM] * len(pieces),
         out_specs=VMEM,
         compiler_params=params(4),
@@ -164,11 +160,12 @@
     )(*pieces)
 
 
-def columns(refs, ys, zs):
-    return [jnp.concatenate([r[:, at(4 * y + z, LANE)] for z in zs for y in ys], axis=1) for r in refs]
-
-
-def pair_kernel(places, sides, add, *refs):
+def columns(refs, half, ys, zs):
+    rows = slice(2 * LANE * half, 2 * LANE * (half + 1))
+    return [jnp.concatenate([r[rows, at(4 * y + z, LANE)] for z in zs for y in ys], axis=1) for r in refs]
+
+
+def pair_kernel(places, half, sides, add, *refs):
     ops, before, (out_p, out_q) = refs[: 3 * sides], refs[3 * sides : 3 * sides + 2 * add], refs[-2:]
     particle = lax.axis_index("particle")
     y, z = particle >> 2, particle & 3
@@ -182,7 +179,7 @@
         total = None
         for side in range(sides):
             st, rh, rl = ops[3 * side : 3 * side + 3]
-            high, rest = columns((rh, rl), range(3), [z ^ s ^ (s >> 1) for s in spots])
+            high, rest = columns((rh, rl), half, range(3), [z ^ s ^ (s >> 1) for s in spots])
             left = jnp.concatenate([st[pl.ds(pl.multiple_of(s, 32), 32)] for s in starts])
             both, low = dot(left, high), dot(left[:LANE], rest)
             term = both[:LANE] + both[LANE:] + low
@@ -197,22 +194,22 @@
                     out[4 * n + spot] = value
 
 
-def covariance_pair(places, operands, before):
+def covariance_pair(places, half, operands, before):
     rows, coefs = operands[1].shape
     sides = len(operands) // 3
     out = shape(8, 32, 3 * LANE)
     return pl.pallas_call(
-        functools.partial(pair_kernel, places, sides, len(before) // 2),
+        functools.partial(pair_kernel, places, half, sides, len(before) // 2),
         out_shape=(out, out),
         in_specs=[VMEM] * (len(operands) + len(before)),
         out_specs=(VMEM, VMEM),
         compiler_params=params(16),
-        cost_estimate=cost(3 * rows * coefs * LANE * sides, 4),
+        cost_estimate=cost(2 * rows * coefs * LANE * sides, 4),
     )(*operands, *before)
 
 
-def third_kernel(*refs):
-    ops, out = refs[:6], refs[6]
+def third_kernel(half, *refs):
+    ops, before, out = refs[:6], refs[6:-1], refs[-1]
     particle = lax.axis_index("particle")
     y, z = particle >> 2, particle & 3
 
@@ -221,7 +218,7 @@
         spots = [2 * step, 2 * step + 1]
         both = low = None
         for st, rh, rl in (ops[:3], ops[3:]):
-            high, rest = columns((rh, rl), [3], [z ^ s ^ (s >> 1) for s in spots])
+            high, rest = columns((rh, rl), half, [3], [z ^ s ^ (s >> 1) for s in spots])
             left_high = jnp.concatenate([st[LANE * b : LANE * b + 64] for b in range(4)])
             first, second = dot(st[...], high), dot(left_high, rest)
             both = first if both is None else both + first
@@ -232,20 +229,21 @@
             top = LANE * b
             value = both[top : top + 64] + both[top + 64 : top + LANE] + low[64 * b : 64 * b + 64]
             for i, spot in enumerate(spots):
-                out[4 * spot + place] = value[:, LANE * i : LANE * (i + 1)]
-
-
-def covariance_third(operands):
+                mine = value[:, LANE * i : LANE * (i + 1)]
+                out[4 * spot + place] = mine + before[0][4 * spot + place] if before else mine
+
+
+def covariance_third(half, operands, *before):
     rows, coefs = operands[1].shape
     return pl.pallas_call(
-        third_kernel,
+        functools.partial(third_kernel, half),
         out_shape=shape(16, 64, LANE),
-        in_specs=[VMEM] * 6,
+        in_specs=[VMEM] * (6 + len(before)),
         out_specs=VMEM,
         compiler_params=params(16),
         cost_estimate=cost(3 * rows * coefs * LANE, 4),
         name="covariance_third",
-    )(*operands)
+    )(*operands, *before)
 
 
 def shrink_kernel(factor, load_h, load_l, mine, other, w_out, corr_out, cbuf):
@@ -349,18 +347,21 @@
     got = swap(far, "coeffici", CORE)
     near, nh, nl = scores(0, rest, lh, ll)
     own = own_block(near, got, *ring_swap([near[n] + got[n] for n in (1, 2, 3)], "coeffici", X))
-    pieces = [own] + ring_swap([own] * 3, "coeffici", X)
-    others = swap(jnp.stack(pieces), "coeffici", CORE)
-    near_ops = (stage(*pieces), nh, nl)
-    far_ops = (stage(others), fh, fl)
-
-    leave = covariance_pair((2, 3), near_ops, ())
-    leave_p, leave_q = covariance_pair((2, 3), far_ops, leave)
+    p1, p2, p3 = ring_swap([own] * 3, "coeffici", X)
+    far_a = swap(jnp.stack([own, p1]), "coeffici", CORE)
+    early = (stage(own, p1), nh, nl, stage(far_a), fh, fl)
+    leave = covariance_pair((2, 3), 0, early, ())
+    third = covariance_third(0, early)
+    keep = covariance_pair((0, 1), 0, early, ())
+    far_b = swap(jnp.stack([p2, p3]), "coeffici", CORE)
+    near_b, other_b = (stage(p2, p3), nh, nl), (stage(far_b), fh, fl)
+    leave = covariance_pair((2, 3), 1, near_b, leave)
+    leave_p, leave_q = covariance_pair((2, 3), 1, other_b, leave)
     one_p = swap(leave_p, "particle", Y)
     one_q = swap(leave_q, "particle", 3 * Y)
-    third = covariance_third(near_ops + far_ops)
+    third = covariance_third(1, near_b + other_b, third)
     sums = ring_swap([third[4 * n : 4 * n + 4] for n in (1, 2, 3)], "particle", Z)
-    keep_p, keep_q = covariance_pair((0, 1), near_ops + far_ops, ())
+    keep_p, keep_q = covariance_pair((0, 1), 1, near_b + other_b, keep)
     two_p = swap(keep_p[4:] + one_p[4:], "particle", 3 * Y)
     two_q = swap(keep_q[4:] + one_q[4:], "particle", Y)
 

time: 119 us -> 120 us (level)
  starting transfers between devices: 52.9 us -> 57.9 us
  waiting for transfers between devices: 48.2 us -> 43.5 us
    ppermute x34 -> x35, starting transfers between devices: 52.9 us -> 57.9 us  [swap(): lax.ppermute(value, axis, [(s, s ^ mask) for s in range(lax.axis_size(axi...]
    ppermute x34 -> x35, waiting for transfers between devices: 48.2 us -> 43.5 us  [swap(): lax.ppermute(value, axis, [(s, s ^ mask) for s in range(lax.axis_size(axi...]
    pallas_call x6 -> x11, Pallas kernels: 6.3 us -> 7.29 us  [the longest x5 5.31 us: covariance_pair(): pl.pallas_call(functools.partial(pair_kernel, places, half, sides, len(be...]
  transfers between devices with their start and end apart: 34 -> 35, of which waited for: 22 -> 20; matrix products, arithmetic and copies ran while one was open for 0% -> 0% of each run, Pallas kernels for 5% -> 6%
where the time goes in v4:
time: 120 us
  starting transfers between devices  57.9 us (48%)
  waiting for transfers between devices  43.5 us (36%)
  Pallas kernels  17 us (14%)
    ppermute x35, starting transfers between devices, swap(): lax.ppermute(value, axis, [(s, s ^ mask) for s in range(lax.axis_size(axi...  57.9 us
    ppermute x35, waiting for transfers between devices, swap(): lax.ppermute(value, axis, [(s, s ^ mask) for s in range(lax.axis_size(axi...  43.5 us
    pallas_call x2, Pallas kernels, scores(): pl.pallas_call(functools.partial(scores_kernel, side), out_shape=(shape(4...  7.7 us
    pallas_call x5, Pallas kernels, covariance_pair(): pl.pallas_call(functools.partial(pair_kernel, places, half, sides, len(be...  5.31 us
  transfers between devices with their start and end apart: 35, of which 20 were waited for; matrix products, arithmetic and copies ran while one was open for 0% of the time, Pallas kernels for 6%

profile of v4, /device:TPU:1, one launch (start us, length us, event | category | flops | bytes accessed | tf_op | source)
XLA Modules:
  0.0 119.8 jit_solution(2788417692547396655)
XLA Ops:
  0.6 5.7 %scores_far.1 = (f32[4,128,256]{2,1,0:T(8,128)S(1)}, bf16[512,2048]{1,0:T(8,128)(2,1)S(1)}, bf16[512,2048]{1,0:T(8,128)(2,1)S(1)}, bf16[2048,256]{1,0:T(8,128)(2...) custom-call(f32[1024,2048]{1,0:T(8,128)} %bitcast.52, f32[2048,256]{1,0:T(8,128)} %bitcast.53), custom_call_target="tpu_custom_call" | custom-call | flops 1610612736 | bytes 6291456 | tf_op jit(solution)/shard_map/scores_far/pallas_call | solution.py:109
  6.3 3.3 %collective-permute-start = (f32[4,128,256]{2,1,0:T(8,128)S(1)}, f32[4,128,256]{2,1,0:T(8,128)S(1)}, u32[]{:S(2)}, u32[]{:S(2)}) collective-permute-start(f32[4,128,256]{2,1,0:T(8,128)S(1)} %get-tuple-element.27), channel_id=1, source_target_pairs={{0,2},{2,0},{4,6},{6,4},{8,10},{10,8},{12,14},{14,12},{1,3},{3,1},... | collective-permute-start | bytes 1572872 | tf_op jit(solution)/shard_map/ppermute | solution.py:23
  9.6 2.0 %scores_near.1 = (f32[4,128,256]{2,1,0:T(8,128)S(1)}, bf16[512,2048]{1,0:T(8,128)(2,1)S(1)}, bf16[512,2048]{1,0:T(8,128)(2,1)S(1)}) custom-call(f32[512,2048]{1,0:T(8,128)S(1)} %get-tuple-element.25.refs_0_, bf16[2048,256]{1,0:T(8,128)(2,1)S(1)} %get-tuple-element.23.refs_1_.load_h, bf16[2048,256]{1,0:T(8,128)(2,1)S(1)} %get-tuple-element.24.refs_2_.load_l), custom_call_target="tpu_custom_call" | custom-call | flops 1610612736 | bytes 6291456 | tf_op jit(solution)/shard_map/scores_near/pallas_call | solution.py:109
  14.4 3.9 %collective-permute-done.3.r3 = f32[128,256]{1,0:T(8,128)S(1)} collective-permute-done((f32[128,256]{1,0:T(8,128)S(1)}, f32[128,256]{1,0:T(8,128)S(1)}, u32[]{:S(2)}, u32[]{:S(2)}) %collective-permute-start.3) | collective-permute-done | bytes 131104 | tf_op jit(solution)/shard_map/ppermute | solution.py:23
  18.3 3.2 %collective-permute-done.2.r2 = f32[128,256]{1,0:T(8,128)S(1)} collective-permute-done((f32[128,256]{1,0:T(8,128)S(1)}, f32[128,256]{1,0:T(8,128)S(1)}, u32[]{:S(2)}, u32[]{:S(2)}) %collective-permute-start.2) | collective-permute-done | bytes 131104 | tf_op jit(solution)/shard_map/ppermute | solution.py:23
  21.8 1.9 %collective-permute-start.5 = (f32[256,128]{1,0:T(8,128)S(1)}, f32[256,128]{1,0:T(8,128)S(1)}, u32[]{:S(2)}, u32[]{:S(2)}) collective-permute-start(f32[256,128]{1,0:T(8,128)S(1)} %own_block.1.refs_0_), channel_id=1, source_target_pairs={{0,8},{2,10},{4,12},{6,14},{8,0},{10,2},{12,4},{14,6},{1,9},{3,11}... | collective-permute-start | bytes 393224 | tf_op jit(solution)/shard_map/ppermute | solution.py:23
  26.4 2.3 %collective-permute-start.8 = (f32[2,256,128]{2,1,0:T(8,128)S(1)}, f32[2,256,128]{2,1,0:T(8,128)S(1)}, u32[]{:S(2)}, u32[]{:S(2)}) collective-permute-start(f32[2,256,128]{2,1,0:T(8,128)S(1)} %pad_maximum_fusion.1), channel_id=1, source_target_pairs={{0,2},{2,0},{4,6},{6,4},{8,10},{10,8},{12,14},{14,12},{1,3},{3,1},... | collective-permute-start | bytes 786440 | tf_op jit(solution)/shard_map/ppermute | solution.py:23
  29.6 2.6 %collective-permute-done.4.refs_0_ = f32[256,128]{1,0:T(8,128)S(1)} collective-permute-done((f32[256,128]{1,0:T(8,128)S(1)}, f32[256,128]{1,0:T(8,128)S(1)}, u32[]{:S(2)}, u32[]{:S(2)}) %collective-permute-start.4) | collective-permute-done | bytes 131104 | tf_op jit(solution)/shard_map/ppermute | solution.py:23
  39.7 3.3 %collective-permute-start.16 = (f32[4,64,128]{2,1,0:T(8,128)S(1)}, f32[4,64,128]{2,1,0:T(8,128)S(1)}, u32[]{:S(2)}, u32[]{:S(2)}) collective-permute-start(f32[4,64,128]{2,1,0:T(8,128)S(1)} %get-tuple-element.58), channel_id=1, source_target_pairs={{0,16},{16,0},{32,48},{48,32},{64,80},{80,64},{96,112},{112,96},{1... | collective-permute-start | bytes 393224 | tf_op jit(solution)/shard_map/ppermute | solution.py:23
  43.0 5.1 %collective-permute-start.18 = (f32[4,64,128]{2,1,0:T(8,128)S(1)}, f32[4,64,128]{2,1,0:T(8,128)S(1)}, u32[]{:S(2)}, u32[]{:S(2)}) collective-permute-start(f32[4,64,128]{2,1,0:T(8,128)S(1)} %get-tuple-element.59), channel_id=1, source_target_pairs={{0,32},{16,48},{32,0},{48,16},{64,96},{80,112},{96,64},{112,80},{1... | collective-permute-start | bytes 393224 | tf_op jit(solution)/shard_map/ppermute | solution.py:23
  52.4 4.9 %collective-permute-done.18 = f32[4,64,128]{2,1,0:T(8,128)S(1)} collective-permute-done((f32[4,64,128]{2,1,0:T(8,128)S(1)}, f32[4,64,128]{2,1,0:T(8,128)S(1)}, u32[]{:S(2)}, u32[]{:S(2)}) %collective-permute-start.18) | collective-permute-done | bytes 131104 | tf_op jit(solution)/shard_map/ppermute | solution.py:23
  57.3 1.9 %collective-permute-done.17 = f32[4,64,128]{2,1,0:T(8,128)S(1)} collective-permute-done((f32[4,64,128]{2,1,0:T(8,128)S(1)}, f32[4,64,128]{2,1,0:T(8,128)S(1)}, u32[]{:S(2)}, u32[]{:S(2)}) %collective-permute-start.17) | collective-permute-done | bytes 131104 | tf_op jit(solution)/shard_map/ppermute | solution.py:23
  59.3 2.0 %collective-permute-start.20 = (f32[64,128]{1,0:T(8,128)S(1)}, f32[64,128]{1,0:T(8,128)S(1)}, u32[]{:S(2)}, u32[]{:S(2)}) collective-permute-start(f32[64,128]{1,0:T(8,128)S(1)} %get-tuple-element.55), channel_id=1, source_target_pairs={{0,192},{16,208},{32,224},{48,240},{64,128},{80,144},{96,160},{112... | collective-permute-start | bytes 98312 | tf_op jit(solution)/shard_map/ppermute | solution.py:23
  62.7 2.0 %collective-permute-start.10 = (f32[4,32,384]{2,1,0:T(8,128)S(1)}, f32[4,32,384]{2,1,0:T(8,128)S(1)}, u32[]{:S(2)}, u32[]{:S(2)}) collective-permute-start(f32[4,32,384]{2,1,0:T(8,128)S(1)} %slice_add_fusion.1), channel_id=1, source_target_pairs={{0,192},{16,208},{32,224},{48,240},{64,128},{80,144},{96,160},{112... | collective-permute-start | bytes 589832 | tf_op jit(solution)/shard_map/ppermute | solution.py:23
  65.2 3.6 %collective-permute-done.10 = f32[4,32,384]{2,1,0:T(8,128)S(1)} collective-permute-done((f32[4,32,384]{2,1,0:T(8,128)S(1)}, f32[4,32,384]{2,1,0:T(8,128)S(1)}, u32[]{:S(2)}, u32[]{:S(2)}) %collective-permute-start.10) | collective-permute-done | bytes 196640 | tf_op jit(solution)/shard_map/ppermute | solution.py:23
  69.7 2.8 %collective-permute-start.13 = (f32[64,384]{1,0:T(8,128)S(1)}, f32[64,384]{1,0:T(8,128)S(1)}, u32[]{:S(2)}, u32[]{:S(2)}) collective-permute-start(f32[64,384]{1,0:T(8,128)S(1)} %pad_maximum_fusion.3), channel_id=1, source_target_pairs={{0,16},{16,0},{32,48},{48,32},{64,80},{80,64},{96,112},{112,96},{1... | collective-permute-start | bytes 294920 | tf_op jit(solution)/shard_map/ppermute | solution.py:23
  72.5 3.7 %collective-permute-start.15 = (f32[64,384]{1,0:T(8,128)S(1)}, f32[64,384]{1,0:T(8,128)S(1)}, u32[]{:S(2)}, u32[]{:S(2)}) collective-permute-start(f32[64,384]{1,0:T(8,128)S(1)} %pad_maximum_fusion.5), channel_id=1, source_target_pairs={{0,32},{16,48},{32,0},{48,16},{64,96},{80,112},{96,64},{112,80},{1... | collective-permute-start | bytes 294920 | tf_op jit(solution)/shard_map/ppermute | solution.py:23
  76.4 3.7 %collective-permute-done.15 = f32[64,384]{1,0:T(8,128)S(1)} collective-permute-done((f32[64,384]{1,0:T(8,128)S(1)}, f32[64,384]{1,0:T(8,128)S(1)}, u32[]{:S(2)}, u32[]{:S(2)}) %collective-permute-start.15) | collective-permute-done | bytes 98336 | tf_op jit(solution)/shard_map/ppermute | solution.py:23
  80.1 4.5 %collective-permute-done.14 = f32[64,384]{1,0:T(8,128)S(1)} collective-permute-done((f32[64,384]{1,0:T(8,128)S(1)}, f32[64,384]{1,0:T(8,128)S(1)}, u32[]{:S(2)}, u32[]{:S(2)}) %collective-permute-start.14) | collective-permute-done | bytes 98336 | tf_op jit(solution)/shard_map/ppermute | solution.py:23
  85.9 2.7 %collective-permute-done.22.other = f32[64,512]{1,0:T(8,128)S(1)} collective-permute-done((f32[64,512]{1,0:T(8,128)S(1)}, f32[64,512]{1,0:T(8,128)S(1)}, u32[]{:S(2)}, u32[]{:S(2)}) %collective-permute-start.22) | collective-permute-done | bytes 131104 | tf_op jit(solution)/shard_map/ppermute | solution.py:23
  88.9 3.1 %collective-permute-start.23 = (f32[64,128]{1,0:T(8,128)S(1)}, f32[64,128]{1,0:T(8,128)S(1)}, u32[]{:S(2)}, u32[]{:S(2)}) collective-permute-start(f32[64,128]{1,0:T(8,128)S(1)} %slice_bitcast_fusion), channel_id=1, source_target_pairs={{0,2},{2,0},{4,6},{6,4},{8,10},{10,8},{12,14},{14,12},{1,3},{3,1},... | collective-permute-start | bytes 98312 | tf_op jit(solution)/shard_map/ppermute | solution.py:23
  97.3 3.4 %collective-permute-start.29 = (f32[64,128]{1,0:T(8,128)S(1)}, f32[64,128]{1,0:T(8,128)S(1)}, u32[]{:S(2)}, u32[]{:S(2)}) collective-permute-start(f32[64,128]{1,0:T(8,128)S(1)} %add_add_fusion.1), channel_id=1, source_target_pairs={{0,32},{16,48},{32,0},{48,16},{64,96},{80,112},{96,64},{112,80},{1... | collective-permute-start | bytes 98312 | tf_op jit(solution)/shard_map/ppermute | solution.py:23
  100.7 2.2 %collective-permute-start.28 = (f32[64,128]{1,0:T(8,128)S(1)}, f32[64,128]{1,0:T(8,128)S(1)}, u32[]{:S(2)}, u32[]{:S(2)}) collective-permute-start(f32[64,128]{1,0:T(8,128)S(1)} %add_add_fusion.1), channel_id=1, source_target_pairs={{0,48},{16,32},{32,16},{48,0},{64,112},{80,96},{96,80},{112,64},{1... | collective-permute-start | bytes 98312 | tf_op jit(solution)/shard_map/ppermute | solution.py:23
  113.0 4.7 %collective-permute-start.34 = (f32[3,64,128]{2,1,0:T(8,128)S(1)}, f32[3,64,128]{2,1,0:T(8,128)S(1)}, u32[]{:S(2)}, u32[]{:S(2)}) collective-permute-start(f32[3,64,128]{2,1,0:T(8,128)S(1)} %pad_maximum_fusion.6), channel_id=1, source_target_pairs={{0,2},{2,0},{4,6},{6,4},{8,10},{10,8},{12,14},{14,12},{1,3},{3,1},... | collective-permute-start | bytes 294920 | tf_op jit(solution)/shard_map/ppermute | solution.py:23
  (88 shorter events, 40.2 us)
Async XLA Ops:
  6.3 5.3 %collective-permute-start = (f32[4,128,256]{2,1,0:T(8,128)S(1)}, f32[4,128,256]{2,1,0:T(8,128)S(1)}, u32[]{:S(2)}, u32[]{:S(2)}) collective-permute-start(f32[4,128,256]{2,1,0:T(8,128)S(1)} %get-tuple-element.27), channel_id=1, source_target_pairs={{0,2},{2,0},{4,6},{6,4},{8,10},{10,8},{12,14},{14,12},{1,3},{3,1},... | collective-permute-start | bytes 1572872 | tf_op jit(solution)/shard_map/ppermute | solution.py:23
  11.7 6.6 %collective-permute-start.3 = (f32[128,256]{1,0:T(8,128)S(1)}, f32[128,256]{1,0:T(8,128)S(1)}, u32[]{:S(2)}, u32[]{:S(2)}) collective-permute-start(f32[128,256]{1,0:T(8,128)S(1)} %get-tuple-element.44), channel_id=1, source_target_pairs={{0,8},{2,10},{4,12},{6,14},{8,0},{10,2},{12,4},{14,6},{1,9},{3,11}... | collective-permute-start | bytes 393224 | tf_op jit(solution)/shard_map/ppermute | solution.py:23
  12.8 8.7 %collective-permute-start.2 = (f32[128,256]{1,0:T(8,128)S(1)}, f32[128,256]{1,0:T(8,128)S(1)}, u32[]{:S(2)}, u32[]{:S(2)}) collective-permute-start(f32[128,256]{1,0:T(8,128)S(1)} %get-tuple-element.45), channel_id=1, source_target_pairs={{0,12},{2,14},{4,8},{6,10},{8,4},{10,6},{12,0},{14,2},{1,13},{3,15... | collective-permute-start | bytes 393224 | tf_op jit(solution)/shard_map/ppermute | solution.py:23
  13.7 7.9 %collective-permute-start.1 = (f32[128,256]{1,0:T(8,128)S(1)}, f32[128,256]{1,0:T(8,128)S(1)}, u32[]{:S(2)}, u32[]{:S(2)}) collective-permute-start(f32[128,256]{1,0:T(8,128)S(1)} %get-tuple-element.46), channel_id=1, source_target_pairs={{0,4},{2,6},{4,0},{6,2},{8,12},{10,14},{12,8},{14,10},{1,5},{3,7},... | collective-permute-start | bytes 393224 | tf_op jit(solution)/shard_map/ppermute | solution.py:23
  21.8 7.9 %collective-permute-start.5 = (f32[256,128]{1,0:T(8,128)S(1)}, f32[256,128]{1,0:T(8,128)S(1)}, u32[]{:S(2)}, u32[]{:S(2)}) collective-permute-start(f32[256,128]{1,0:T(8,128)S(1)} %own_block.1.refs_0_), channel_id=1, source_target_pairs={{0,8},{2,10},{4,12},{6,14},{8,0},{10,2},{12,4},{14,6},{1,9},{3,11}... | collective-permute-start | bytes 393224 | tf_op jit(solution)/shard_map/ppermute | solution.py:23
  23.7 8.5 %collective-permute-start.4 = (f32[256,128]{1,0:T(8,128)S(1)}, f32[256,128]{1,0:T(8,128)S(1)}, u32[]{:S(2)}, u32[]{:S(2)}) collective-permute-start(f32[256,128]{1,0:T(8,128)S(1)} %own_block.1.refs_0_), channel_id=1, source_target_pairs={{0,12},{2,14},{4,8},{6,10},{8,4},{10,6},{12,0},{14,2},{1,13},{3,15... | collective-permute-start | bytes 393224 | tf_op jit(solution)/shard_map/ppermute | solution.py:23
  26.4 7.1 %collective-permute-start.8 = (f32[2,256,128]{2,1,0:T(8,128)S(1)}, f32[2,256,128]{2,1,0:T(8,128)S(1)}, u32[]{:S(2)}, u32[]{:S(2)}) collective-permute-start(f32[2,256,128]{2,1,0:T(8,128)S(1)} %pad_maximum_fusion.1), channel_id=1, source_target_pairs={{0,2},{2,0},{4,6},{6,4},{8,10},{10,8},{12,14},{14,12},{1,3},{3,1},... | collective-permute-start | bytes 786440 | tf_op jit(solution)/shard_map/ppermute | solution.py:23
  38.3 24.3 %collective-permute-start.9 = (f32[8,32,384]{2,1,0:T(8,128)S(1)}, f32[8,32,384]{2,1,0:T(8,128)S(1)}, u32[]{:S(2)}, u32[]{:S(2)}) collective-permute-start(f32[8,32,384]{2,1,0:T(8,128)S(1)} %get-tuple-element.39), channel_id=1, source_target_pairs={{0,64},{16,80},{32,96},{48,112},{64,0},{80,16},{96,32},{112,48},{1... | collective-permute-start | bytes 1179656 | tf_op jit(solution)/shard_map/ppermute | solution.py:23
  39.7 12.7 %collective-permute-start.16 = (f32[4,64,128]{2,1,0:T(8,128)S(1)}, f32[4,64,128]{2,1,0:T(8,128)S(1)}, u32[]{:S(2)}, u32[]{:S(2)}) collective-permute-start(f32[4,64,128]{2,1,0:T(8,128)S(1)} %get-tuple-element.58), channel_id=1, source_target_pairs={{0,16},{16,0},{32,48},{48,32},{64,80},{80,64},{96,112},{112,96},{1... | collective-permute-start | bytes 393224 | tf_op jit(solution)/shard_map/ppermute | solution.py:23
  43.0 14.4 %collective-permute-start.18 = (f32[4,64,128]{2,1,0:T(8,128)S(1)}, f32[4,64,128]{2,1,0:T(8,128)S(1)}, u32[]{:S(2)}, u32[]{:S(2)}) collective-permute-start(f32[4,64,128]{2,1,0:T(8,128)S(1)} %get-tuple-element.59), channel_id=1, source_target_pairs={{0,32},{16,48},{32,0},{48,16},{64,96},{80,112},{96,64},{112,80},{1... | collective-permute-start | bytes 393224 | tf_op jit(solution)/shard_map/ppermute | solution.py:23
  48.1 11.2 %collective-permute-start.17 = (f32[4,64,128]{2,1,0:T(8,128)S(1)}, f32[4,64,128]{2,1,0:T(8,128)S(1)}, u32[]{:S(2)}, u32[]{:S(2)}) collective-permute-start(f32[4,64,128]{2,1,0:T(8,128)S(1)} %get-tuple-element.60), channel_id=1, source_target_pairs={{0,48},{16,32},{32,16},{48,0},{64,112},{80,96},{96,80},{112,64},{1... | collective-permute-start | bytes 393224 | tf_op jit(solution)/shard_map/ppermute | solution.py:23
  48.1 16.6 %collective-permute-start.11 = (f32[8,32,384]{2,1,0:T(8,128)S(1)}, f32[8,32,384]{2,1,0:T(8,128)S(1)}, u32[]{:S(2)}, u32[]{:S(2)}) collective-permute-start(f32[8,32,384]{2,1,0:T(8,128)S(1)} %get-tuple-element.41), channel_id=1, source_target_pairs={{0,192},{16,208},{32,224},{48,240},{64,128},{80,144},{96,160},{112... | collective-permute-start | bytes 1179656 | tf_op jit(solution)/shard_map/ppermute | solution.py:23
  59.3 17.0 %collective-permute-start.20 = (f32[64,128]{1,0:T(8,128)S(1)}, f32[64,128]{1,0:T(8,128)S(1)}, u32[]{:S(2)}, u32[]{:S(2)}) collective-permute-start(f32[64,128]{1,0:T(8,128)S(1)} %get-tuple-element.55), channel_id=1, source_target_pairs={{0,192},{16,208},{32,224},{48,240},{64,128},{80,144},{96,160},{112... | collective-permute-start | bytes 98312 | tf_op jit(solution)/shard_map/ppermute | solution.py:23
  61.3 15.0 %collective-permute-start.21 = (f32[64,128]{1,0:T(8,128)S(1)}, f32[64,128]{1,0:T(8,128)S(1)}, u32[]{:S(2)}, u32[]{:S(2)}) collective-permute-start(f32[64,128]{1,0:T(8,128)S(1)} %get-tuple-element.56), channel_id=1, source_target_pairs={{0,128},{16,144},{32,160},{48,176},{64,192},{80,208},{96,224},{112... | collective-permute-start | bytes 98312 | tf_op jit(solution)/shard_map/ppermute | solution.py:23
  62.1 14.2 %collective-permute-start.19 = (f32[64,128]{1,0:T(8,128)S(1)}, f32[64,128]{1,0:T(8,128)S(1)}, u32[]{:S(2)}, u32[]{:S(2)}) collective-permute-start(f32[64,128]{1,0:T(8,128)S(1)} %get-tuple-element.57), channel_id=1, source_target_pairs={{0,64},{16,80},{32,96},{48,112},{64,0},{80,16},{96,32},{112,48},{1... | collective-permute-start | bytes 98312 | tf_op jit(solution)/shard_map/ppermute | solution.py:23
  62.7 6.2 %collective-permute-start.10 = (f32[4,32,384]{2,1,0:T(8,128)S(1)}, f32[4,32,384]{2,1,0:T(8,128)S(1)}, u32[]{:S(2)}, u32[]{:S(2)}) collective-permute-start(f32[4,32,384]{2,1,0:T(8,128)S(1)} %slice_add_fusion.1), channel_id=1, source_target_pairs={{0,192},{16,208},{32,224},{48,240},{64,128},{80,144},{96,160},{112... | collective-permute-start | bytes 589832 | tf_op jit(solution)/shard_map/ppermute | solution.py:23
  64.7 4.9 %collective-permute-start.12 = (f32[4,32,384]{2,1,0:T(8,128)S(1)}, f32[4,32,384]{2,1,0:T(8,128)S(1)}, u32[]{:S(2)}, u32[]{:S(2)}) collective-permute-start(f32[4,32,384]{2,1,0:T(8,128)S(1)} %slice_add_fusion), channel_id=1, source_target_pairs={{0,64},{16,80},{32,96},{48,112},{64,0},{80,16},{96,32},{112,48},{1... | collective-permute-start | bytes 589832 | tf_op jit(solution)/shard_map/ppermute | solution.py:23
  69.7 6.7 %collective-permute-start.13 = (f32[64,384]{1,0:T(8,128)S(1)}, f32[64,384]{1,0:T(8,128)S(1)}, u32[]{:S(2)}, u32[]{:S(2)}) collective-permute-start(f32[64,384]{1,0:T(8,128)S(1)} %pad_maximum_fusion.3), channel_id=1, source_target_pairs={{0,16},{16,0},{32,48},{48,32},{64,80},{80,64},{96,112},{112,96},{1... | collective-permute-start | bytes 294920 | tf_op jit(solution)/shard_map/ppermute | solution.py:23
  72.5 7.6 %collective-permute-start.15 = (f32[64,384]{1,0:T(8,128)S(1)}, f32[64,384]{1,0:T(8,128)S(1)}, u32[]{:S(2)}, u32[]{:S(2)}) collective-permute-start(f32[64,384]{1,0:T(8,128)S(1)} %pad_maximum_fusion.5), channel_id=1, source_target_pairs={{0,32},{16,48},{32,0},{48,16},{64,96},{80,112},{96,64},{112,80},{1... | collective-permute-start | bytes 294920 | tf_op jit(solution)/shard_map/ppermute | solution.py:23
  76.2 8.4 %collective-permute-start.14 = (f32[64,384]{1,0:T(8,128)S(1)}, f32[64,384]{1,0:T(8,128)S(1)}, u32[]{:S(2)}, u32[]{:S(2)}) collective-permute-start(f32[64,384]{1,0:T(8,128)S(1)} %pad_maximum_fusion.4), channel_id=1, source_target_pairs={{0,48},{16,32},{32,16},{48,0},{64,112},{80,96},{96,80},{112,64},{1... | collective-permute-start | bytes 294920 | tf_op jit(solution)/shard_map/ppermute | solution.py:23
  97.3 6.8 %collective-permute-start.29 = (f32[64,128]{1,0:T(8,128)S(1)}, f32[64,128]{1,0:T(8,128)S(1)}, u32[]{:S(2)}, u32[]{:S(2)}) collective-permute-start(f32[64,128]{1,0:T(8,128)S(1)} %add_add_fusion.1), channel_id=1, source_target_pairs={{0,32},{16,48},{32,0},{48,16},{64,96},{80,112},{96,64},{112,80},{1... | collective-permute-start | bytes 98312 | tf_op jit(solution)/shard_map/ppermute | solution.py:23
  100.7 5.2 %collective-permute-start.28 = (f32[64,128]{1,0:T(8,128)S(1)}, f32[64,128]{1,0:T(8,128)S(1)}, u32[]{:S(2)}, u32[]{:S(2)}) collective-permute-start(f32[64,128]{1,0:T(8,128)S(1)} %add_add_fusion.1), channel_id=1, source_target_pairs={{0,48},{16,32},{32,16},{48,0},{64,112},{80,96},{96,80},{112,64},{1... | collective-permute-start | bytes 98312 | tf_op jit(solution)/shard_map/ppermute | solution.py:23
  106.9 4.7 %collective-permute-start.32 = (f32[2,64,128]{2,1,0:T(8,128)S(1)}, f32[2,64,128]{2,1,0:T(8,128)S(1)}, u32[]{:S(2)}, u32[]{:S(2)}) collective-permute-start(f32[2,64,128]{2,1,0:T(8,128)S(1)} %get-tuple-element.64), channel_id=1, source_target_pairs={{0,128},{16,144},{32,160},{48,176},{64,192},{80,208},{96,224},{112... | collective-permute-start | bytes 196616 | tf_op jit(solution)/shard_map/ppermute | solution.py:23
  113.0 5.9 %collective-permute-start.34 = (f32[3,64,128]{2,1,0:T(8,128)S(1)}, f32[3,64,128]{2,1,0:T(8,128)S(1)}, u32[]{:S(2)}, u32[]{:S(2)}) collective-permute-start(f32[3,64,128]{2,1,0:T(8,128)S(1)} %pad_maximum_fusion.6), channel_id=1, source_target_pairs={{0,2},{2,0},{4,6},{6,4},{8,10},{10,8},{12,14},{14,12},{1,3},{3,1},... | collective-permute-start | bytes 294920 | tf_op jit(solution)/shard_map/ppermute | solution.py:23
  (11 other events, 40.9 us)

commit v5 on v4

--- a/solution.py
+++ b/solution.py
@@ -165,7 +165,7 @@
     return [jnp.concatenate([r[rows, at(4 * y + z, LANE)] for z in zs for y in ys], axis=1) for r in refs]
 
 
-def pair_kernel(places, half, sides, add, *refs):
+def pair_kernel(places, halves, sides, add, *refs):
     ops, before, (out_p, out_q) = refs[: 3 * sides], refs[3 * sides : 3 * sides + 2 * add], refs[-2:]
     particle = lax.axis_index("particle")
     y, z = particle >> 2, particle & 3
@@ -179,7 +179,7 @@
         total = None
         for side in range(sides):
             st, rh, rl = ops[3 * side : 3 * side + 3]
-            high, rest = columns((rh, rl), half, range(3), [z ^ s ^ (s >> 1) for s in spots])
+            high, rest = columns((rh, rl), halves[side], range(3), [z ^ s ^ (s >> 1) for s in spots])
             left = jnp.concatenate([st[pl.ds(pl.multiple_of(s, 32), 32)] for s in starts])
             both, low = dot(left, high), dot(left[:LANE], rest)
             term = both[:LANE] + both[LANE:] + low
@@ -194,12 +194,12 @@
                     out[4 * n + spot] = value
 
 
-def covariance_pair(places, half, operands, before):
+def covariance_pair(places, halves, operands, before):
     rows, coefs = operands[1].shape
     sides = len(operands) // 3
     out = shape(8, 32, 3 * LANE)
     return pl.pallas_call(
-        functools.partial(pair_kernel, places, half, sides, len(before) // 2),
+        functools.partial(pair_kernel, places, halves, sides, len(before) // 2),
         out_shape=(out, out),
         in_specs=[VMEM] * (len(operands) + len(before)),
         out_specs=(VMEM, VMEM),
@@ -350,18 +350,17 @@
     p1, p2, p3 = ring_swap([own] * 3, "coeffici", X)
     far_a = swap(jnp.stack([own, p1]), "coeffici", CORE)
     early = (stage(own, p1), nh, nl, stage(far_a), fh, fl)
-    leave = covariance_pair((2, 3), 0, early, ())
+    leave = covariance_pair((2, 3), (0, 0), early, ())
     third = covariance_third(0, early)
-    keep = covariance_pair((0, 1), 0, early, ())
     far_b = swap(jnp.stack([p2, p3]), "coeffici", CORE)
     near_b, other_b = (stage(p2, p3), nh, nl), (stage(far_b), fh, fl)
-    leave = covariance_pair((2, 3), 1, near_b, leave)
-    leave_p, leave_q = covariance_pair((2, 3), 1, other_b, leave)
+    leave = covariance_pair((2, 3), (1,), near_b, leave)
+    leave_p, leave_q = covariance_pair((2, 3), (1,), other_b, leave)
     one_p = swap(leave_p, "particle", Y)
     one_q = swap(leave_q, "particle", 3 * Y)
     third = covariance_third(1, near_b + other_b, third)
     sums = ring_swap([third[4 * n : 4 * n + 4] for n in (1, 2, 3)], "particle", Z)
-    keep_p, keep_q = covariance_pair((0, 1), 1, near_b + other_b, keep)
+    keep_p, keep_q = covariance_pair((0, 1), (0, 0, 1, 1), early + near_b + other_b, ())
     two_p = swap(keep_p[4:] + one_p[4:], "particle", 3 * Y)
     two_q = swap(keep_q[4:] + one_q[4:], "particle", Y)
 

time: 120 us -> 120 us (level)
    pallas_call x5 -> x4, Pallas kernels: 5.31 us -> 5.11 us  [covariance_pair(): pl.pallas_call(functools.partial(pair_kernel, places, halves, sides, len(...]
where the time goes in v5:
time: 120 us
  starting transfers between devices  58 us (48%)
  waiting for transfers between devices  43.6 us (36%)
  Pallas kernels  16.8 us (14%)
    ppermute x35, starting transfers between devices, swap(): lax.ppermute(value, axis, [(s, s ^ mask) for s in range(lax.axis_size(axi...  58 us
    ppermute x35, waiting for transfers between devices, swap(): lax.ppermute(value, axis, [(s, s ^ mask) for s in range(lax.axis_size(axi...  43.6 us
    pallas_call x2, Pallas kernels, scores(): pl.pallas_call(functools.partial(scores_kernel, side), out_shape=(shape(4...  7.7 us
    pallas_call x4, Pallas kernels, covariance_pair(): pl.pallas_call(functools.partial(pair_kernel, places, halves, sides, len(...  5.11 us
  transfers between devices with their start and end apart: 35, of which 20 were waited for; matrix products, arithmetic and copies ran while one was open for 0% of the time, Pallas kernels for 6%

profile of v5, /device:TPU:1, one launch (start us, length us, event | category | flops | bytes accessed | tf_op | source)
XLA Modules:
  0.0 119.7 jit_solution(14272118573049772601)
XLA Ops:
  0.6 5.7 %scores_far.1 = (f32[4,128,256]{2,1,0:T(8,128)S(1)}, bf16[512,2048]{1,0:T(8,128)(2,1)S(1)}, bf16[512,2048]{1,0:T(8,128)(2,1)S(1)}, bf16[2048,256]{1,0:T(8,128)(2...) custom-call(f32[1024,2048]{1,0:T(8,128)} %bitcast.52, f32[2048,256]{1,0:T(8,128)} %bitcast.53), custom_call_target="tpu_custom_call" | custom-call | flops 1610612736 | bytes 6291456 | tf_op jit(solution)/shard_map/scores_far/pallas_call | solution.py:109
  6.3 3.3 %collective-permute-start = (f32[4,128,256]{2,1,0:T(8,128)S(1)}, f32[4,128,256]{2,1,0:T(8,128)S(1)}, u32[]{:S(2)}, u32[]{:S(2)}) collective-permute-start(f32[4,128,256]{2,1,0:T(8,128)S(1)} %get-tuple-element.25), channel_id=1, source_target_pairs={{0,2},{2,0},{4,6},{6,4},{8,10},{10,8},{12,14},{14,12},{1,3},{3,1},... | collective-permute-start | bytes 1572872 | tf_op jit(solution)/shard_map/ppermute | solution.py:23
  9.6 2.0 %scores_near.1 = (f32[4,128,256]{2,1,0:T(8,128)S(1)}, bf16[512,2048]{1,0:T(8,128)(2,1)S(1)}, bf16[512,2048]{1,0:T(8,128)(2,1)S(1)}) custom-call(f32[512,2048]{1,0:T(8,128)S(1)} %get-tuple-element.23.refs_0_, bf16[2048,256]{1,0:T(8,128)(2,1)S(1)} %get-tuple-element.21.refs_1_.load_h, bf16[2048,256]{1,0:T(8,128)(2,1)S(1)} %get-tuple-element.22.refs_2_.load_l), custom_call_target="tpu_custom_call" | custom-call | flops 1610612736 | bytes 6291456 | tf_op jit(solution)/shard_map/scores_near/pallas_call | solution.py:109
  14.4 3.9 %collective-permute-done.3.r3 = f32[128,256]{1,0:T(8,128)S(1)} collective-permute-done((f32[128,256]{1,0:T(8,128)S(1)}, f32[128,256]{1,0:T(8,128)S(1)}, u32[]{:S(2)}, u32[]{:S(2)}) %collective-permute-start.3) | collective-permute-done | bytes 131104 | tf_op jit(solution)/shard_map/ppermute | solution.py:23
  18.3 3.2 %collective-permute-done.2.r2 = f32[128,256]{1,0:T(8,128)S(1)} collective-permute-done((f32[128,256]{1,0:T(8,128)S(1)}, f32[128,256]{1,0:T(8,128)S(1)}, u32[]{:S(2)}, u32[]{:S(2)}) %collective-permute-start.2) | collective-permute-done | bytes 131104 | tf_op jit(solution)/shard_map/ppermute | solution.py:23
  21.8 1.9 %collective-permute-start.7 = (f32[256,128]{1,0:T(8,128)S(1)}, f32[256,128]{1,0:T(8,128)S(1)}, u32[]{:S(2)}, u32[]{:S(2)}) collective-permute-start(f32[256,128]{1,0:T(8,128)S(1)} %own_block.1.refs_0_), channel_id=1, source_target_pairs={{0,8},{2,10},{4,12},{6,14},{8,0},{10,2},{12,4},{14,6},{1,9},{3,11}... | collective-permute-start | bytes 393224 | tf_op jit(solution)/shard_map/ppermute | solution.py:23
  26.4 2.3 %collective-permute-start.5 = (f32[2,256,128]{2,1,0:T(8,128)S(1)}, f32[2,256,128]{2,1,0:T(8,128)S(1)}, u32[]{:S(2)}, u32[]{:S(2)}) collective-permute-start(f32[2,256,128]{2,1,0:T(8,128)S(1)} %pad_maximum_fusion), channel_id=1, source_target_pairs={{0,2},{2,0},{4,6},{6,4},{8,10},{10,8},{12,14},{14,12},{1,3},{3,1},... | collective-permute-start | bytes 786440 | tf_op jit(solution)/shard_map/ppermute | solution.py:23
  29.6 2.6 %collective-permute-done.6.refs_0_ = f32[256,128]{1,0:T(8,128)S(1)} collective-permute-done((f32[256,128]{1,0:T(8,128)S(1)}, f32[256,128]{1,0:T(8,128)S(1)}, u32[]{:S(2)}, u32[]{:S(2)}) %collective-permute-start.6) | collective-permute-done | bytes 131104 | tf_op jit(solution)/shard_map/ppermute | solution.py:23
  39.7 3.3 %collective-permute-start.16 = (f32[4,64,128]{2,1,0:T(8,128)S(1)}, f32[4,64,128]{2,1,0:T(8,128)S(1)}, u32[]{:S(2)}, u32[]{:S(2)}) collective-permute-start(f32[4,64,128]{2,1,0:T(8,128)S(1)} %get-tuple-element.54), channel_id=1, source_target_pairs={{0,16},{16,0},{32,48},{48,32},{64,80},{80,64},{96,112},{112,96},{1... | collective-permute-start | bytes 393224 | tf_op jit(solution)/shard_map/ppermute | solution.py:23
  43.0 5.1 %collective-permute-start.18 = (f32[4,64,128]{2,1,0:T(8,128)S(1)}, f32[4,64,128]{2,1,0:T(8,128)S(1)}, u32[]{:S(2)}, u32[]{:S(2)}) collective-permute-start(f32[4,64,128]{2,1,0:T(8,128)S(1)} %get-tuple-element.55), channel_id=1, source_target_pairs={{0,32},{16,48},{32,0},{48,16},{64,96},{80,112},{96,64},{112,80},{1... | collective-permute-start | bytes 393224 | tf_op jit(solution)/shard_map/ppermute | solution.py:23
  50.0 2.2 %shard_map.41 = (f32[8,32,384]{2,1,0:T(8,128)S(1)}, f32[8,32,384]{2,1,0:T(8,128)S(1)}) custom-call(bf16[512,256]{1,0:T(8,128)(2,1)S(1)} %stage.4.refs_0_, bf16[512,2048]{1,0:T(8,128)(2,1)S(1)} %get-tuple-element.26.refs_1_.refs_7_, bf16[512,2048]{1,0:T(8,128)(2,1)S(1)} %get-tuple-element.27.refs_2_.refs_8_, bf16[512,256]{1,0:T(8,128)(2,1)S(1)} %stage.5.refs_3_, ...), custom_call_target="tpu_custom_call" | custom-call | flops 1073741824 | bytes 4194304 | tf_op jit(solution)/shard_map/pallas_call | solution.py:201
  52.2 5.1 %collective-permute-done.18 = f32[4,64,128]{2,1,0:T(8,128)S(1)} collective-permute-done((f32[4,64,128]{2,1,0:T(8,128)S(1)}, f32[4,64,128]{2,1,0:T(8,128)S(1)}, u32[]{:S(2)}, u32[]{:S(2)}) %collective-permute-start.18) | collective-permute-done | bytes 131104 | tf_op jit(solution)/shard_map/ppermute | solution.py:23
  59.3 2.0 %collective-permute-start.20 = (f32[64,128]{1,0:T(8,128)S(1)}, f32[64,128]{1,0:T(8,128)S(1)}, u32[]{:S(2)}, u32[]{:S(2)}) collective-permute-start(f32[64,128]{1,0:T(8,128)S(1)} %get-tuple-element.51), channel_id=1, source_target_pairs={{0,192},{16,208},{32,224},{48,240},{64,128},{80,144},{96,160},{112... | collective-permute-start | bytes 98312 | tf_op jit(solution)/shard_map/ppermute | solution.py:23
  62.7 2.0 %collective-permute-start.10 = (f32[4,32,384]{2,1,0:T(8,128)S(1)}, f32[4,32,384]{2,1,0:T(8,128)S(1)}, u32[]{:S(2)}, u32[]{:S(2)}) collective-permute-start(f32[4,32,384]{2,1,0:T(8,128)S(1)} %slice_add_fusion.1), channel_id=1, source_target_pairs={{0,192},{16,208},{32,224},{48,240},{64,128},{80,144},{96,160},{112... | collective-permute-start | bytes 589832 | tf_op jit(solution)/shard_map/ppermute | solution.py:23
  65.2 3.6 %collective-permute-done.10 = f32[4,32,384]{2,1,0:T(8,128)S(1)} collective-permute-done((f32[4,32,384]{2,1,0:T(8,128)S(1)}, f32[4,32,384]{2,1,0:T(8,128)S(1)}, u32[]{:S(2)}, u32[]{:S(2)}) %collective-permute-start.10) | collective-permute-done | bytes 196640 | tf_op jit(solution)/shard_map/ppermute | solution.py:23
  69.7 2.8 %collective-permute-start.13 = (f32[64,384]{1,0:T(8,128)S(1)}, f32[64,384]{1,0:T(8,128)S(1)}, u32[]{:S(2)}, u32[]{:S(2)}) collective-permute-start(f32[64,384]{1,0:T(8,128)S(1)} %pad_maximum_fusion.3), channel_id=1, source_target_pairs={{0,16},{16,0},{32,48},{48,32},{64,80},{80,64},{96,112},{112,96},{1... | collective-permute-start | bytes 294920 | tf_op jit(solution)/shard_map/ppermute | solution.py:23
  72.5 3.7 %collective-permute-start.15 = (f32[64,384]{1,0:T(8,128)S(1)}, f32[64,384]{1,0:T(8,128)S(1)}, u32[]{:S(2)}, u32[]{:S(2)}) collective-permute-start(f32[64,384]{1,0:T(8,128)S(1)} %pad_maximum_fusion.5), channel_id=1, source_target_pairs={{0,32},{16,48},{32,0},{48,16},{64,96},{80,112},{96,64},{112,80},{1... | collective-permute-start | bytes 294920 | tf_op jit(solution)/shard_map/ppermute | solution.py:23
  76.4 3.7 %collective-permute-done.15 = f32[64,384]{1,0:T(8,128)S(1)} collective-permute-done((f32[64,384]{1,0:T(8,128)S(1)}, f32[64,384]{1,0:T(8,128)S(1)}, u32[]{:S(2)}, u32[]{:S(2)}) %collective-permute-start.15) | collective-permute-done | bytes 98336 | tf_op jit(solution)/shard_map/ppermute | solution.py:23
  80.1 4.5 %collective-permute-done.14 = f32[64,384]{1,0:T(8,128)S(1)} collective-permute-done((f32[64,384]{1,0:T(8,128)S(1)}, f32[64,384]{1,0:T(8,128)S(1)}, u32[]{:S(2)}, u32[]{:S(2)}) %collective-permute-start.14) | collective-permute-done | bytes 98336 | tf_op jit(solution)/shard_map/ppermute | solution.py:23
  85.9 2.7 %collective-permute-done.22.other = f32[64,512]{1,0:T(8,128)S(1)} collective-permute-done((f32[64,512]{1,0:T(8,128)S(1)}, f32[64,512]{1,0:T(8,128)S(1)}, u32[]{:S(2)}, u32[]{:S(2)}) %collective-permute-start.22) | collective-permute-done | bytes 131104 | tf_op jit(solution)/shard_map/ppermute | solution.py:23
  88.9 3.1 %collective-permute-start.23 = (f32[64,128]{1,0:T(8,128)S(1)}, f32[64,128]{1,0:T(8,128)S(1)}, u32[]{:S(2)}, u32[]{:S(2)}) collective-permute-start(f32[64,128]{1,0:T(8,128)S(1)} %slice_bitcast_fusion), channel_id=1, source_target_pairs={{0,2},{2,0},{4,6},{6,4},{8,10},{10,8},{12,14},{14,12},{1,3},{3,1},... | collective-permute-start | bytes 98312 | tf_op jit(solution)/shard_map/ppermute | solution.py:23
  97.3 3.4 %collective-permute-start.29 = (f32[64,128]{1,0:T(8,128)S(1)}, f32[64,128]{1,0:T(8,128)S(1)}, u32[]{:S(2)}, u32[]{:S(2)}) collective-permute-start(f32[64,128]{1,0:T(8,128)S(1)} %add_add_fusion.1), channel_id=1, source_target_pairs={{0,32},{16,48},{32,0},{48,16},{64,96},{80,112},{96,64},{112,80},{1... | collective-permute-start | bytes 98312 | tf_op jit(solution)/shard_map/ppermute | solution.py:23
  100.7 2.2 %collective-permute-start.28 = (f32[64,128]{1,0:T(8,128)S(1)}, f32[64,128]{1,0:T(8,128)S(1)}, u32[]{:S(2)}, u32[]{:S(2)}) collective-permute-start(f32[64,128]{1,0:T(8,128)S(1)} %add_add_fusion.1), channel_id=1, source_target_pairs={{0,48},{16,32},{32,16},{48,0},{64,112},{80,96},{96,80},{112,64},{1... | collective-permute-start | bytes 98312 | tf_op jit(solution)/shard_map/ppermute | solution.py:23
  113.0 4.7 %collective-permute-start.34 = (f32[3,64,128]{2,1,0:T(8,128)S(1)}, f32[3,64,128]{2,1,0:T(8,128)S(1)}, u32[]{:S(2)}, u32[]{:S(2)}) collective-permute-start(f32[3,64,128]{2,1,0:T(8,128)S(1)} %pad_maximum_fusion.6), channel_id=1, source_target_pairs={{0,2},{2,0},{4,6},{6,4},{8,10},{10,8},{12,14},{14,12},{1,3},{3,1},... | collective-permute-start | bytes 294920 | tf_op jit(solution)/shard_map/ppermute | solution.py:23
  (87 shorter events, 39.7 us)
Async XLA Ops:
  6.3 5.3 %collective-permute-start = (f32[4,128,256]{2,1,0:T(8,128)S(1)}, f32[4,128,256]{2,1,0:T(8,128)S(1)}, u32[]{:S(2)}, u32[]{:S(2)}) collective-permute-start(f32[4,128,256]{2,1,0:T(8,128)S(1)} %get-tuple-element.25), channel_id=1, source_target_pairs={{0,2},{2,0},{4,6},{6,4},{8,10},{10,8},{12,14},{14,12},{1,3},{3,1},... | collective-permute-start | bytes 1572872 | tf_op jit(solution)/shard_map/ppermute | solution.py:23
  11.7 6.6 %collective-permute-start.3 = (f32[128,256]{1,0:T(8,128)S(1)}, f32[128,256]{1,0:T(8,128)S(1)}, u32[]{:S(2)}, u32[]{:S(2)}) collective-permute-start(f32[128,256]{1,0:T(8,128)S(1)} %get-tuple-element.40), channel_id=1, source_target_pairs={{0,8},{2,10},{4,12},{6,14},{8,0},{10,2},{12,4},{14,6},{1,9},{3,11}... | collective-permute-start | bytes 393224 | tf_op jit(solution)/shard_map/ppermute | solution.py:23
  12.8 8.7 %collective-permute-start.2 = (f32[128,256]{1,0:T(8,128)S(1)}, f32[128,256]{1,0:T(8,128)S(1)}, u32[]{:S(2)}, u32[]{:S(2)}) collective-permute-start(f32[128,256]{1,0:T(8,128)S(1)} %get-tuple-element.41), channel_id=1, source_target_pairs={{0,12},{2,14},{4,8},{6,10},{8,4},{10,6},{12,0},{14,2},{1,13},{3,15... | collective-permute-start | bytes 393224 | tf_op jit(solution)/shard_map/ppermute | solution.py:23
  13.7 7.9 %collective-permute-start.1 = (f32[128,256]{1,0:T(8,128)S(1)}, f32[128,256]{1,0:T(8,128)S(1)}, u32[]{:S(2)}, u32[]{:S(2)}) collective-permute-start(f32[128,256]{1,0:T(8,128)S(1)} %get-tuple-element.42), channel_id=1, source_target_pairs={{0,4},{2,6},{4,0},{6,2},{8,12},{10,14},{12,8},{14,10},{1,5},{3,7},... | collective-permute-start | bytes 393224 | tf_op jit(solution)/shard_map/ppermute | solution.py:23
  21.8 7.9 %collective-permute-start.7 = (f32[256,128]{1,0:T(8,128)S(1)}, f32[256,128]{1,0:T(8,128)S(1)}, u32[]{:S(2)}, u32[]{:S(2)}) collective-permute-start(f32[256,128]{1,0:T(8,128)S(1)} %own_block.1.refs_0_), channel_id=1, source_target_pairs={{0,8},{2,10},{4,12},{6,14},{8,0},{10,2},{12,4},{14,6},{1,9},{3,11}... | collective-permute-start | bytes 393224 | tf_op jit(solution)/shard_map/ppermute | solution.py:23
  23.7 8.5 %collective-permute-start.6 = (f32[256,128]{1,0:T(8,128)S(1)}, f32[256,128]{1,0:T(8,128)S(1)}, u32[]{:S(2)}, u32[]{:S(2)}) collective-permute-start(f32[256,128]{1,0:T(8,128)S(1)} %own_block.1.refs_0_), channel_id=1, source_target_pairs={{0,12},{2,14},{4,8},{6,10},{8,4},{10,6},{12,0},{14,2},{1,13},{3,15... | collective-permute-start | bytes 393224 | tf_op jit(solution)/shard_map/ppermute | solution.py:23
  26.4 7.1 %collective-permute-start.5 = (f32[2,256,128]{2,1,0:T(8,128)S(1)}, f32[2,256,128]{2,1,0:T(8,128)S(1)}, u32[]{:S(2)}, u32[]{:S(2)}) collective-permute-start(f32[2,256,128]{2,1,0:T(8,128)S(1)} %pad_maximum_fusion), channel_id=1, source_target_pairs={{0,2},{2,0},{4,6},{6,4},{8,10},{10,8},{12,14},{14,12},{1,3},{3,1},... | collective-permute-start | bytes 786440 | tf_op jit(solution)/shard_map/ppermute | solution.py:23
  38.3 24.3 %collective-permute-start.9 = (f32[8,32,384]{2,1,0:T(8,128)S(1)}, f32[8,32,384]{2,1,0:T(8,128)S(1)}, u32[]{:S(2)}, u32[]{:S(2)}) collective-permute-start(f32[8,32,384]{2,1,0:T(8,128)S(1)} %get-tuple-element.35), channel_id=1, source_target_pairs={{0,64},{16,80},{32,96},{48,112},{64,0},{80,16},{96,32},{112,48},{1... | collective-permute-start | bytes 1179656 | tf_op jit(solution)/shard_map/ppermute | solution.py:23
  39.7 12.5 %collective-permute-start.16 = (f32[4,64,128]{2,1,0:T(8,128)S(1)}, f32[4,64,128]{2,1,0:T(8,128)S(1)}, u32[]{:S(2)}, u32[]{:S(2)}) collective-permute-start(f32[4,64,128]{2,1,0:T(8,128)S(1)} %get-tuple-element.54), channel_id=1, source_target_pairs={{0,16},{16,0},{32,48},{48,32},{64,80},{80,64},{96,112},{112,96},{1... | collective-permute-start | bytes 393224 | tf_op jit(solution)/shard_map/ppermute | solution.py:23
  43.0 14.4 %collective-permute-start.18 = (f32[4,64,128]{2,1,0:T(8,128)S(1)}, f32[4,64,128]{2,1,0:T(8,128)S(1)}, u32[]{:S(2)}, u32[]{:S(2)}) collective-permute-start(f32[4,64,128]{2,1,0:T(8,128)S(1)} %get-tuple-element.55), channel_id=1, source_target_pairs={{0,32},{16,48},{32,0},{48,16},{64,96},{80,112},{96,64},{112,80},{1... | collective-permute-start | bytes 393224 | tf_op jit(solution)/shard_map/ppermute | solution.py:23
  48.1 11.2 %collective-permute-start.17 = (f32[4,64,128]{2,1,0:T(8,128)S(1)}, f32[4,64,128]{2,1,0:T(8,128)S(1)}, u32[]{:S(2)}, u32[]{:S(2)}) collective-permute-start(f32[4,64,128]{2,1,0:T(8,128)S(1)} %get-tuple-element.56), channel_id=1, source_target_pairs={{0,48},{16,32},{32,16},{48,0},{64,112},{80,96},{96,80},{112,64},{1... | collective-permute-start | bytes 393224 | tf_op jit(solution)/shard_map/ppermute | solution.py:23
  48.1 16.6 %collective-permute-start.11 = (f32[8,32,384]{2,1,0:T(8,128)S(1)}, f32[8,32,384]{2,1,0:T(8,128)S(1)}, u32[]{:S(2)}, u32[]{:S(2)}) collective-permute-start(f32[8,32,384]{2,1,0:T(8,128)S(1)} %get-tuple-element.37), channel_id=1, source_target_pairs={{0,192},{16,208},{32,224},{48,240},{64,128},{80,144},{96,160},{112... | collective-permute-start | bytes 1179656 | tf_op jit(solution)/shard_map/ppermute | solution.py:23
  59.3 17.0 %collective-permute-start.20 = (f32[64,128]{1,0:T(8,128)S(1)}, f32[64,128]{1,0:T(8,128)S(1)}, u32[]{:S(2)}, u32[]{:S(2)}) collective-permute-start(f32[64,128]{1,0:T(8,128)S(1)} %get-tuple-element.51), channel_id=1, source_target_pairs={{0,192},{16,208},{32,224},{48,240},{64,128},{80,144},{96,160},{112... | collective-permute-start | bytes 98312 | tf_op jit(solution)/shard_map/ppermute | solution.py:23
  61.3 15.0 %collective-permute-start.21 = (f32[64,128]{1,0:T(8,128)S(1)}, f32[64,128]{1,0:T(8,128)S(1)}, u32[]{:S(2)}, u32[]{:S(2)}) collective-permute-start(f32[64,128]{1,0:T(8,128)S(1)} %get-tuple-element.52), channel_id=1, source_target_pairs={{0,128},{16,144},{32,160},{48,176},{64,192},{80,208},{96,224},{112... | collective-permute-start | bytes 98312 | tf_op jit(solution)/shard_map/ppermute | solution.py:23
  62.1 14.2 %collective-permute-start.19 = (f32[64,128]{1,0:T(8,128)S(1)}, f32[64,128]{1,0:T(8,128)S(1)}, u32[]{:S(2)}, u32[]{:S(2)}) collective-permute-start(f32[64,128]{1,0:T(8,128)S(1)} %get-tuple-element.53), channel_id=1, source_target_pairs={{0,64},{16,80},{32,96},{48,112},{64,0},{80,16},{96,32},{112,48},{1... | collective-permute-start | bytes 98312 | tf_op jit(solution)/shard_map/ppermute | solution.py:23
  62.7 6.2 %collective-permute-start.10 = (f32[4,32,384]{2,1,0:T(8,128)S(1)}, f32[4,32,384]{2,1,0:T(8,128)S(1)}, u32[]{:S(2)}, u32[]{:S(2)}) collective-permute-start(f32[4,32,384]{2,1,0:T(8,128)S(1)} %slice_add_fusion.1), channel_id=1, source_target_pairs={{0,192},{16,208},{32,224},{48,240},{64,128},{80,144},{96,160},{112... | collective-permute-start | bytes 589832 | tf_op jit(solution)/shard_map/ppermute | solution.py:23
  64.7 4.9 %collective-permute-start.12 = (f32[4,32,384]{2,1,0:T(8,128)S(1)}, f32[4,32,384]{2,1,0:T(8,128)S(1)}, u32[]{:S(2)}, u32[]{:S(2)}) collective-permute-start(f32[4,32,384]{2,1,0:T(8,128)S(1)} %slice_add_fusion), channel_id=1, source_target_pairs={{0,64},{16,80},{32,96},{48,112},{64,0},{80,16},{96,32},{112,48},{1... | collective-permute-start | bytes 589832 | tf_op jit(solution)/shard_map/ppermute | solution.py:23
  69.7 6.7 %collective-permute-start.13 = (f32[64,384]{1,0:T(8,128)S(1)}, f32[64,384]{1,0:T(8,128)S(1)}, u32[]{:S(2)}, u32[]{:S(2)}) collective-permute-start(f32[64,384]{1,0:T(8,128)S(1)} %pad_maximum_fusion.3), channel_id=1, source_target_pairs={{0,16},{16,0},{32,48},{48,32},{64,80},{80,64},{96,112},{112,96},{1... | collective-permute-start | bytes 294920 | tf_op jit(solution)/shard_map/ppermute | solution.py:23
  72.5 7.6 %collective-permute-start.15 = (f32[64,384]{1,0:T(8,128)S(1)}, f32[64,384]{1,0:T(8,128)S(1)}, u32[]{:S(2)}, u32[]{:S(2)}) collective-permute-start(f32[64,384]{1,0:T(8,128)S(1)} %pad_maximum_fusion.5), channel_id=1, source_target_pairs={{0,32},{16,48},{32,0},{48,16},{64,96},{80,112},{96,64},{112,80},{1... | collective-permute-start | bytes 294920 | tf_op jit(solution)/shard_map/ppermute | solution.py:23
  76.2 8.4 %collective-permute-start.14 = (f32[64,384]{1,0:T(8,128)S(1)}, f32[64,384]{1,0:T(8,128)S(1)}, u32[]{:S(2)}, u32[]{:S(2)}) collective-permute-start(f32[64,384]{1,0:T(8,128)S(1)} %pad_maximum_fusion.4), channel_id=1, source_target_pairs={{0,48},{16,32},{32,16},{48,0},{64,112},{80,96},{96,80},{112,64},{1... | collective-permute-start | bytes 294920 | tf_op jit(solution)/shard_map/ppermute | solution.py:23
  97.3 6.8 %collective-permute-start.29 = (f32[64,128]{1,0:T(8,128)S(1)}, f32[64,128]{1,0:T(8,128)S(1)}, u32[]{:S(2)}, u32[]{:S(2)}) collective-permute-start(f32[64,128]{1,0:T(8,128)S(1)} %add_add_fusion.1), channel_id=1, source_target_pairs={{0,32},{16,48},{32,0},{48,16},{64,96},{80,112},{96,64},{112,80},{1... | collective-permute-start | bytes 98312 | tf_op jit(solution)/shard_map/ppermute | solution.py:23
  100.7 5.2 %collective-permute-start.28 = (f32[64,128]{1,0:T(8,128)S(1)}, f32[64,128]{1,0:T(8,128)S(1)}, u32[]{:S(2)}, u32[]{:S(2)}) collective-permute-start(f32[64,128]{1,0:T(8,128)S(1)} %add_add_fusion.1), channel_id=1, source_target_pairs={{0,48},{16,32},{32,16},{48,0},{64,112},{80,96},{96,80},{112,64},{1... | collective-permute-start | bytes 98312 | tf_op jit(solution)/shard_map/ppermute | solution.py:23
  106.8 4.7 %collective-permute-start.32 = (f32[2,64,128]{2,1,0:T(8,128)S(1)}, f32[2,64,128]{2,1,0:T(8,128)S(1)}, u32[]{:S(2)}, u32[]{:S(2)}) collective-permute-start(f32[2,64,128]{2,1,0:T(8,128)S(1)} %get-tuple-element.60), channel_id=1, source_target_pairs={{0,128},{16,144},{32,160},{48,176},{64,192},{80,208},{96,224},{112... | collective-permute-start | bytes 196616 | tf_op jit(solution)/shard_map/ppermute | solution.py:23
  113.0 5.9 %collective-permute-start.34 = (f32[3,64,128]{2,1,0:T(8,128)S(1)}, f32[3,64,128]{2,1,0:T(8,128)S(1)}, u32[]{:S(2)}, u32[]{:S(2)}) collective-permute-start(f32[3,64,128]{2,1,0:T(8,128)S(1)} %pad_maximum_fusion.6), channel_id=1, source_target_pairs={{0,2},{2,0},{4,6},{6,4},{8,10},{10,8},{12,14},{14,12},{1,3},{3,1},... | collective-permute-start | bytes 294920 | tf_op jit(solution)/shard_map/ppermute | solution.py:23
  (11 other events, 40.8 us)
